TPU v7x, 32 devices: a whole 2x2x4 slice. The times are simulated.
32 devices in a mesh: groups: 2 (over y), frames: 4 (over z), heads: 2 (over x), rep: 2 (over core).
Axes of the slice: x: 2, y: 2, z: 4, core: 2. Of those that a mesh axis runs over, the one named last changes fastest.
Arguments:
- query: bfloat16 [4096, 3072], P(('groups', 'frames', 'rep'), 'heads'), parts along dimension 0, may hold values from -120 to 120
- key_proj: bfloat16 [4096, 3072], P(('groups', 'frames', 'rep'), 'heads'), parts along dimension 0, may hold values from -4 to 4
- value: bfloat16 [4096, 3072], P(('groups', 'frames', 'rep'), 'heads'), parts along dimension 0, may hold values from -6 to 6
- block_mask: int32 [24, 8, 8], P('heads'), may hold values from 0 to 1, as said below
- tile_sizes: int32 [2, 4], P('rep'), may hold values from 1 to 128, 256 in all within a row
- temporal_ids: int32 [8], P('heads'), may hold values from 0 to 23, as said below
Outputs:
- attended: bfloat16 [4096, 3072], P(('groups', 'frames', 'rep'), 'heads'), parts along dimension 0
There are 2 independent parts, one for each index of `groups`. A program takes and returns all parts, laid end to end along the dimension named above; an argument that names none is the same for every part. Nothing has to cross between parts.
Inputs may be any that keep to these rules, and one draw needn't show every extreme that they name: `block_mask`: each row of each head's block mask has exactly 4 ones, its diagonal entry among them. Entries j of temporal_ids are distinct and lie in heads (j // 4) * 12 to (j // 4 + 1) * 12 - 1. `tile_sizes`: each row sums to 256, and its largest entry is 128.
All inputs are finite; a program needn't handle non-finite values.
Results may differ from a plain program's by a relative error of at most 0.008.
Values may be sent and summed in bfloat16 or wider, within the bound.
No kernel may reach another device: no remote copies, remote signals or barrier semaphores. Data moves between devices by JAX's collectives and lax.ppermute only.
A program may use at most 64 MiB of HBM per device.

v0:
```python
import jax
import jax.numpy as jnp
from jax import lax
from jax.sharding import PartitionSpec as P

HD = 128
BLK = 64


MASKED_SCORE = -1e30


def softmax_weights(scores):
    highest = jnp.max(scores, axis=-1, keepdims=True)
    raised = jnp.exp(scores - highest)
    return (raised / jnp.sum(raised, axis=-1, keepdims=True)).astype(jnp.bfloat16)


def select_heads(token_rows, picker):
    head_grid = token_rows.reshape(token_rows.shape[0], -1, HD)
    chosen = jnp.einsum(
        "rhd,th->rtd", head_grid, picker.astype(jnp.bfloat16), preferred_element_type=jnp.float32
    )
    return chosen.astype(jnp.bfloat16)


def spread_heads(head_grid, picker):
    return jnp.einsum(
        "rtd,th->rhd", head_grid, picker.astype(jnp.bfloat16), preferred_element_type=jnp.float32
    )


def local(query, key_proj, value, block_mask, tile_sizes, temporal_ids):
    half_rows = query.shape[0]
    heads_here = block_mask.shape[0]
    temp_here = temporal_ids.shape[0]
    spat_here = heads_here - temp_here
    frame_blocks = block_mask.shape[1]
    frame_count = lax.axis_size("frames")
    slot_count = 2 * half_rows // frame_count
    score_scale = HD ** (-0.5)
    local_ids = temporal_ids - lax.axis_index("heads") * heads_here
    head_range = jnp.arange(heads_here, dtype=jnp.int32)
    pick_temp = local_ids[:, None] == head_range[None, :]
    temp_flag = jnp.sum(pick_temp.astype(jnp.int32), axis=0)
    spat_rank = jnp.cumsum(1 - temp_flag) - 1
    pick_spat = (spat_rank[None, :] == jnp.arange(spat_here, dtype=jnp.int32)[:, None]) & (
        temp_flag[None, :] == 0
    )
    tile_len = tile_sizes[0]
    starts = jnp.cumsum(tile_len) - tile_len
    slot_index = jnp.arange(slot_count, dtype=jnp.int32)
    source_rows = jnp.minimum(starts[:, None] + slot_index[None, :], half_rows - 1)
    frame_range = jnp.arange(frame_count, dtype=jnp.int32)
    own_len = jnp.sum(jnp.where(frame_range == lax.axis_index("frames"), tile_len, 0))
    key_live = jnp.tile(slot_index < own_len, frame_count)
    send_query = select_heads(query, pick_temp)[source_rows]
    send_keys = select_heads(key_proj, pick_temp)[source_rows]
    send_values = select_heads(value, pick_temp)[source_rows]
    tile_query = lax.all_to_all(send_query, "frames", split_axis=0, concat_axis=0, tiled=True)
    tile_keys = lax.all_to_all(send_keys, "frames", split_axis=0, concat_axis=0, tiled=True)
    tile_values = lax.all_to_all(send_values, "frames", split_axis=0, concat_axis=0, tiled=True)
    item_count = tile_query.shape[2]
    flat_query = tile_query.reshape(frame_count * slot_count, item_count, HD)
    flat_keys = tile_keys.reshape(frame_count * slot_count, item_count, HD)
    flat_values = tile_values.reshape(frame_count * slot_count, item_count, HD)
    scores = (
        jnp.einsum("qhd,khd->hqk", flat_query, flat_keys, preferred_element_type=jnp.float32)
        * score_scale
    )
    scores = jnp.where(key_live[None, None, :], scores, MASKED_SCORE)
    weights = softmax_weights(scores)
    tile_out = jnp.einsum(
        "hqk,khd->qhd", weights, flat_values, preferred_element_type=jnp.float32
    ).astype(jnp.bfloat16)
    returned = lax.all_to_all(
        tile_out.reshape(frame_count, slot_count, item_count, HD),
        "frames",
        split_axis=0,
        concat_axis=0,
        tiled=True,
    )
    own_keys = select_heads(key_proj, pick_spat)
    own_values = select_heads(value, pick_spat)
    spat_keys, spat_values = (
        lax.all_gather(own_keys, "rep", axis=0, tiled=True),
        lax.all_gather(own_values, "rep", axis=0, tiled=True),
    )
    spat_query = select_heads(query, pick_spat)
    spat_mask = (
        jnp.einsum("hij,th->tij", block_mask.astype(jnp.float32), pick_spat.astype(jnp.float32))
        > 0.5
    )
    query_blocks = half_rows // BLK
    mask_rows = lax.dynamic_slice_in_dim(
        spat_mask, lax.axis_index("rep") * query_blocks, query_blocks, 1
    )
    scores = (
        jnp.einsum("qhd,khd->hqk", spat_query, spat_keys, preferred_element_type=jnp.float32)
        * score_scale
    )
    shaped = scores.reshape(spat_here, query_blocks, BLK, frame_blocks, BLK)
    shaped = jnp.where(mask_rows[:, :, None, :, None], shaped, MASKED_SCORE)
    weights = softmax_weights(shaped.reshape(spat_here, half_rows, frame_blocks * BLK))
    spat_out = jnp.einsum(
        "hqk,khd->qhd", weights, spat_values, preferred_element_type=jnp.float32
    ).astype(jnp.bfloat16)
    positions = jnp.arange(half_rows, dtype=jnp.int32)
    tile_ends = starts + tile_len
    tile_of = jnp.sum((positions[:, None] >= tile_ends[None, :]).astype(jnp.int32), axis=1)
    picked_start = jnp.sum(
        jnp.where(tile_of[:, None] == frame_range[None, :], starts[None, :], 0), axis=1
    )
    flat_index = tile_of * slot_count + positions - picked_start
    temp_out = returned.reshape(frame_count * slot_count, temp_here, HD)[flat_index]
    combined = spread_heads(spat_out, pick_spat) + spread_heads(temp_out, pick_temp)
    return combined.astype(jnp.bfloat16).reshape(half_rows, heads_here * HD)


def solution(mesh):
    in_specs = (
        P(("groups", "frames", "rep"), "heads"),
        P(("groups", "frames", "rep"), "heads"),
        P(("groups", "frames", "rep"), "heads"),
        P("heads", None, None),
        P("rep", None),
        P("heads"),
    )
    out_specs = P(("groups", "frames", "rep"), "heads")
    return jax.shard_map(local, mesh=mesh, in_specs=in_specs, out_specs=out_specs, check_vma=False)
```

profile of v0, /device:TPU:0, one launch (start us, length us, event | category | flops | bytes accessed | tf_op | source)
XLA Modules:
  0.0 106.3 jit_solution(6965234729748970537)
XLA Ops:
  7.5 1.4 %copy.75 = bf16[256,1536]{0,1:T(8,128)(2,1)S(1)} copy(bf16[256,1536]{1,0:T(8,128)(2,1)} %param.7) | data formatting | bytes 1572864 | tf_op args[1]
  8.9 1.0 copy.76
  9.9 1.1 %fusion.18 = bf16[256,8,128]{2,1,0:T(8,128)(2,1)} fusion(bf16[256,12,128]{2,1,0:T(8,128)(2,1)S(1)} %copy.76, s32[12]{0:T(128)S(1)} %add_bitcast_fusion, pred[12]{0:T(512)(128)(4,1)S(1)} %broadcast_compare_fusion), kind=kOutput, calls=%fused_computation.32 | convolution fusion | flops 6553792 | bytes 1310780 | tf_op jit(solution)/shard_map/rhd,th->rtd/dot_general | solution.py:21
  11.0 1.4 %copy.73 = bf16[256,1536]{0,1:T(8,128)(2,1)S(1)} copy(bf16[256,1536]{1,0:T(8,128)(2,1)} %param.6) | data formatting | bytes 1572864 | tf_op args[0]
  12.5 1.0 copy.74
  13.7 0.7 bitcast_subtract_fusion.1
  14.8 2.5 %gather_fusion.1 = bf16[512,4,128]{2,1,0:T(4,128)(2,1)} fusion(bf16[256,4,128]{2,1,0:T(4,128)(2,1)S(1)} %fusion.20, s32[1024]{0:T(1024)S(1)} %pad_clamp_fusion.1), kind=kCustom, calls=%fused_computation.1 | custom fusion | bytes 1050624 | tf_op jit(solution)/shard_map/gather | solution.py:57
  17.4 6.3 %all-to-all-start.1 = ((bf16[4,128,4,128]{3,2,1,0:T(4,128)(2,1)}), bf16[4,128,4,128]{3,2,1,0:T(4,128)(2,1)}, u32[]{:S(2)}, u32[]{:S(2)}) async-start(bf16[4,128,4,128]{3,2,1,0:T(4,128)(2,1)} %bitcast.20), calls=%async_computation.1 | async-start | bytes 1048576 | tf_op jit(solution)/shard_map/all_to_all | solution.py:60
  23.7 2.3 %copy.70 = bf16[256,1536]{0,1:T(8,128)(2,1)} copy(bf16[256,1536]{1,0:T(8,128)(2,1)} %param.8) | data formatting | bytes 1572864 | tf_op args[2]
  26.0 1.9 %copy.71 = bf16[256,12,128]{2,1,0:T(8,128)(2,1)S(1)} copy(bf16[256,12,128]{0,2,1:T(8,128)(2,1)} %bitcast.86) | data formatting | bytes 1572864 | tf_op jit(solution)/shard_map/reshape | solution.py:20
  27.9 1.1 %fusion.16 = bf16[256,8,128]{2,1,0:T(8,128)(2,1)} fusion(bf16[256,12,128]{2,1,0:T(8,128)(2,1)S(1)} %copy.71, s32[12]{0:T(128)S(1)} %add_bitcast_fusion, pred[12]{0:T(512)(128)(4,1)S(1)} %broadcast_compare_fusion), kind=kOutput, calls=%fused_computation.30 | convolution fusion | flops 6553792 | bytes 1310780 | tf_op jit(solution)/shard_map/rhd,th->rtd/dot_general | solution.py:21
  29.7 2.6 %gather_fusion.2 = bf16[512,4,128]{2,1,0:T(4,128)(2,1)} fusion(bf16[256,4,128]{2,1,0:T(4,128)(2,1)S(1)} %fusion.21, s32[1024]{0:T(1024)S(1)} %pad_clamp_fusion.1), kind=kCustom, calls=%fused_computation.2 | custom fusion | bytes 1050624 | tf_op jit(solution)/shard_map/gather | solution.py:58
  32.3 2.6 %gather_fusion = bf16[512,4,128]{2,1,0:T(4,128)(2,1)} fusion(bf16[256,4,128]{2,1,0:T(4,128)(2,1)S(1)} %fusion.19, s32[1024]{0:T(1024)S(1)} %pad_clamp_fusion.1), kind=kCustom, calls=%fused_computation | custom fusion | bytes 1050624 | tf_op jit(solution)/shard_map/gather | solution.py:59
  34.8 0.7 iota_compare_fusion.4
  35.6 2.7 %all-to-all-done.1 = bf16[4,128,4,128]{3,2,1,0:T(4,128)(2,1)} async-done(((bf16[4,128,4,128]{3,2,1,0:T(4,128)(2,1)}), bf16[4,128,4,128]{3,2,1,0:T(4,128)(2,1)}, u32[]{:S(2)}, u32[]{:S(2)}) %all-to-all-start.1) | async-done | bytes 524320 | tf_op jit(solution)/shard_map/all_to_all | solution.py:60
  38.3 3.5 %all-to-all-start.2 = ((bf16[4,128,4,128]{3,2,1,0:T(4,128)(2,1)}), bf16[4,128,4,128]{3,2,1,0:T(4,128)(2,1)S(1)}, u32[]{:S(2)}, u32[]{:S(2)}) async-start(bf16[4,128,4,128]{3,2,1,0:T(4,128)(2,1)} %bitcast.23), calls=%async_computation.2 | async-start | bytes 1048576 | tf_op jit(solution)/shard_map/all_to_all | solution.py:61
  42.1 13.7 %all-to-all-done.2 = bf16[4,128,4,128]{3,2,1,0:T(4,128)(2,1)S(1)} async-done(((bf16[4,128,4,128]{3,2,1,0:T(4,128)(2,1)}), bf16[4,128,4,128]{3,2,1,0:T(4,128)(2,1)S(1)}, u32[]{:S(2)}, u32[]{:S(2)}) %all-to-all-start.2) | async-done | bytes 524320 | tf_op jit(solution)/shard_map/all_to_all | solution.py:61
  55.8 4.1 %all-to-all-start = ((bf16[4,128,4,128]{3,2,1,0:T(4,128)(2,1)}), bf16[4,128,4,128]{3,2,1,0:T(4,128)(2,1)}, u32[]{:S(2)}, u32[]{:S(2)}) async-start(bf16[4,128,4,128]{3,2,1,0:T(4,128)(2,1)} %bitcast.16), calls=%async_computation | async-start | bytes 1048576 | tf_op jit(solution)/shard_map/all_to_all | solution.py:62
  60.6 4.7 %broadcast_in_dim.68 = pred[8,256,512]{2,1,0:T(32,128)(4,1)} reshape(pred[8,4,64,8,64]{4,3,2,1,0:T(8,128)(4,1)S(1)} %broadcast_in_dim.46) | data formatting | bytes 2097152 | tf_op jit(solution)/shard_map/jit(_where)/broadcast_in_dim | solution.py:103
  65.7 1.1 %copy.84 = bf16[4,128,4,128]{3,1,0,2:T(8,128)(2,1)S(1)} copy(bf16[4,128,4,128]{3,2,1,0:T(4,128)(2,1)} %all-to-all-done.1) | data formatting | bytes 1048576 | tf_op jit(solution)/shard_map/all_to_all | solution.py:60
  66.8 1.1 %copy.86 = bf16[4,128,4,128]{3,1,0,2:T(8,128)(2,1)S(1)} copy(bf16[4,128,4,128]{3,2,1,0:T(4,128)(2,1)} %copy-done) | data formatting | bytes 1048576 | tf_op jit(solution)/shard_map/all_to_all | solution.py:61
  67.9 3.5 %fusion.68 = (f32[4,512]{1,0:T(4,128)S(1)}, f32[4,512,512]{1,2,0:T(8,128)}) fusion(pred[512]{0:T(512)(128)(4,1)S(1)} %broadcast_bitcast_fusion, bf16[512,4,128]{2,0,1:T(8,128)(2,1)S(1)} %bitcast.88, bf16[512,4,128]{2,0,1:T(8,128)(2,1)S(1)} %bitcast.89), kind=kOutput, calls=%fused_computation.82 | convolution fusion | flops 272630272 | bytes 5251584 | tf_op jit(solution)/shard_map/sub | solution.py:15
  71.4 2.7 %all-to-all-done = bf16[4,128,4,128]{3,2,1,0:T(4,128)(2,1)} async-done(((bf16[4,128,4,128]{3,2,1,0:T(4,128)(2,1)}), bf16[4,128,4,128]{3,2,1,0:T(4,128)(2,1)}, u32[]{:S(2)}, u32[]{:S(2)}) %all-to-all-start) | async-done | bytes 524320 | tf_op jit(solution)/shard_map/all_to_all | solution.py:62
  74.1 3.0 %fusion.15 = bf16[4,16,4,8,128]{4,3,2,1,0:T(8,128)(2,1)S(1)} fusion(f32[4,512,512]{1,2,0:T(8,128)} %get-tuple-element.10, f32[4,512]{1,0:T(4,128)S(1)} %get-tuple-element.9, bf16[512,4,128]{2,1,0:T(4,128)(2,1)} %bitcast.17), kind=kOutput, calls=%fused_computation.29 | convolution fusion | flops 270794752 | bytes 5251072 | tf_op jit(solution)/shard_map/hqk,khd->qhd/dot_general | solution.py:73
  77.1 0.9 copy.120
  78.0 3.6 %all-to-all-start.3 = ((bf16[4,128,4,128]{1,3,2,0:T(8,128)(2,1)}), bf16[4,128,4,128]{1,3,2,0:T(8,128)(2,1)S(1)}, u32[]{:S(2)}, u32[]{:S(2)}) async-start(bf16[4,128,4,128]{1,3,2,0:T(8,128)(2,1)} %bitcast.82), calls=%async_computation.3 | async-start | bytes 1048576 | tf_op jit(solution)/shard_map/all_to_all | solution.py:76
  81.7 4.9 %fusion.63 = (f32[8,256]{1,0:T(8,128)S(1)}, f32[8,256,512]{2,1,0:T(8,128)}) fusion(pred[8,256,512]{2,1,0:T(32,128)(4,1)S(1)} %copy-done.1, bf16[512,8,128]{2,1,0:T(8,128)(2,1)} %all-gather.5.cloned.1.call-done, bf16[256,8,128]{2,1,0:T(8,128)(2,1)S(1)} %fusion.17), kind=kOutput, calls=%fused_computation.81 | convolution fusion | flops 272630272 | bytes 6823936 | tf_op jit(solution)/shard_map/sub | solution.py:15
  86.6 3.5 %fusion.14 = bf16[256,8,128]{0,2,1:T(8,128)(2,1)S(1)} fusion(f32[8,256,512]{2,1,0:T(8,128)} %get-tuple-element.8, f32[8,256]{1,0:T(8,128)S(1)} %get-tuple-element.7, bf16[512,8,128]{2,1,0:T(8,128)(2,1)} %all-gather.3.cloned.1.call-done), kind=kOutput, calls=%fused_computation.28 | convolution fusion | flops 270794752 | bytes 5775360 | tf_op jit(solution)/shard_map/hqk,khd->qhd/dot_general | solution.py:105
  90.9 4.7 %all-to-all-done.3 = bf16[4,128,4,128]{1,3,2,0:T(8,128)(2,1)S(1)} async-done(((bf16[4,128,4,128]{1,3,2,0:T(8,128)(2,1)}), bf16[4,128,4,128]{1,3,2,0:T(8,128)(2,1)S(1)}, u32[]{:S(2)}, u32[]{:S(2)}) %all-to-all-start.3) | async-done | bytes 524320 | tf_op jit(solution)/shard_map/all_to_all | solution.py:76
  95.8 1.0 gather_fusion.3
  97.4 0.9 copy.90
  98.3 1.2 %copy.91 = bf16[256,1536]{1,0:T(8,128)(2,1)} copy(bf16[256,1536]{0,1:T(8,128)(2,1)S(1)} %bitcast.83) | data formatting | bytes 1572864 | tf_op jit(solution)/shard_map/reshape | solution.py:117
  (42 shorter events, 5.3 us)
Async XLA Ops:
  6.5 75.2 %all-gather.5.cloned.1.call-start = ((), (), s32[]{:S(2)}) async-start(), calls=%async_computation.5 | async-start | bytes 1572864 | tf_op jit(solution)/shard_map/all_gather | solution.py:86
  7.5 6.0 %copy-start.3 = (s32[1,4]{1,0:T(1,128)S(1)}, s32[1,4]{1,0:T(1,128)}, u32[]{:S(2)}) copy-start(s32[1,4]{1,0:T(1,128)} %param.10) | copy-start | bytes 52
  17.4 20.9 %all-to-all-start.1 = ((bf16[4,128,4,128]{3,2,1,0:T(4,128)(2,1)}), bf16[4,128,4,128]{3,2,1,0:T(4,128)(2,1)}, u32[]{:S(2)}, u32[]{:S(2)}) async-start(bf16[4,128,4,128]{3,2,1,0:T(4,128)(2,1)} %bitcast.20), calls=%async_computation.1 | async-start | bytes 1048576 | tf_op jit(solution)/shard_map/all_to_all | solution.py:60
  23.7 62.9 %all-gather.3.cloned.1.call-start = ((), (), s32[]{:S(2)}) async-start(), calls=%async_computation.4 | async-start | bytes 1572864 | tf_op jit(solution)/shard_map/all_gather | solution.py:87
  27.9 14.0 %copy-start.2 = (s32[12,8,8]{0,2,1:T(8,128)S(1)}, s32[12,8,8]{0,2,1:T(8,128)}, u32[]{:S(2)}) copy-start(s32[12,8,8]{0,2,1:T(8,128)} %param.9) | copy-start | bytes 9220
  38.3 17.5 %all-to-all-start.2 = ((bf16[4,128,4,128]{3,2,1,0:T(4,128)(2,1)}), bf16[4,128,4,128]{3,2,1,0:T(4,128)(2,1)S(1)}, u32[]{:S(2)}, u32[]{:S(2)}) async-start(bf16[4,128,4,128]{3,2,1,0:T(4,128)(2,1)} %bitcast.23), calls=%async_computation.2 | async-start | bytes 1048576 | tf_op jit(solution)/shard_map/all_to_all | solution.py:61
  55.8 4.2 %copy-start = (bf16[4,128,4,128]{3,2,1,0:T(4,128)(2,1)}, bf16[4,128,4,128]{3,2,1,0:T(4,128)(2,1)S(1)}, u32[]{:S(2)}) copy-start(bf16[4,128,4,128]{3,2,1,0:T(4,128)(2,1)S(1)} %all-to-all-done.2) | copy-start | bytes 1572868
  55.8 18.3 %all-to-all-start = ((bf16[4,128,4,128]{3,2,1,0:T(4,128)(2,1)}), bf16[4,128,4,128]{3,2,1,0:T(4,128)(2,1)}, u32[]{:S(2)}, u32[]{:S(2)}) async-start(bf16[4,128,4,128]{3,2,1,0:T(4,128)(2,1)} %bitcast.16), calls=%async_computation | async-start | bytes 1048576 | tf_op jit(solution)/shard_map/all_to_all | solution.py:62
  74.1 7.6 %copy-start.1 = (pred[8,256,512]{2,1,0:T(32,128)(4,1)S(1)}, pred[8,256,512]{2,1,0:T(32,128)(4,1)}, u32[]{:S(2)}) copy-start(pred[8,256,512]{2,1,0:T(32,128)(4,1)} %broadcast_in_dim.68) | copy-start | bytes 3145732
  78.0 17.5 %all-to-all-start.3 = ((bf16[4,128,4,128]{1,3,2,0:T(8,128)(2,1)}), bf16[4,128,4,128]{1,3,2,0:T(8,128)(2,1)S(1)}, u32[]{:S(2)}, u32[]{:S(2)}) async-start(bf16[4,128,4,128]{1,3,2,0:T(8,128)(2,1)} %bitcast.82), calls=%async_computation.3 | async-start | bytes 1048576 | tf_op jit(solution)/shard_map/all_to_all | solution.py:76
Sparse Core Ops, SparseCore 0:
  11.2 11.7 all-gather.4
  29.1 10.4 all-gather.2
where the time goes:
time: 107 us; the launch traced here: 106 us
  local copies, waits for them, and re-layouts  28.9 us (27%)
  waiting for transfers between devices  23.8 us (22%)
  matrix products  19.5 us (18%)
  starting transfers between devices  17.6 us (16%)
  between operations  13.6 us (13%)
  other arithmetic  2.82 us (3%)
    all_to_all x1, waiting for transfers between devices, local(): lax.all_to_all(send_keys, 'frames', split_axis=0, concat_axis=0, tiled=True)  13.7 us
    sub x2, matrix products, softmax_weights(): raised = jnp.exp(scores - highest)  8.31 us
    all_to_all x1, starting transfers between devices, local(): lax.all_to_all(send_query, 'frames', split_axis=0, concat_axis=0, tiled=T...  6.35 us
    broadcast_in_dim x2, local copies, waits for them, and re-layouts, local(): shaped = jnp.where(mask_rows[:, :, None, :, None], shaped, MASKED_SCORE)  5.33 us
    unnamed x11, local copies, waits for them, and re-layouts  5.12 us
    all_to_all x1, waiting for transfers between devices, local(): lax.all_to_all(tile_out.reshape(frame_count, slot_count, item_count, HD),...  4.65 us
    all_to_all x1, starting transfers between devices, local(): lax.all_to_all(send_values, 'frames', split_axis=0, concat_axis=0, tiled=...  4.14 us
    reshape x3, local copies, waits for them, and re-layouts, select_heads(): head_grid = token_rows.reshape(token_rows.shape[0], -1, HD)  3.93 us
  transfers between devices with their start and end apart: 6, of which 4 were waited for; matrix products, arithmetic and copies ran while one was open for 40% of the time, Pallas kernels for 0%

commit v1 on v0

--- a/solution.py
+++ b/solution.py
@@ -1,6 +1,10 @@
+import math
+
 import jax
 import jax.numpy as jnp
 from jax import lax
+from jax.experimental import pallas as pl
+from jax.experimental.pallas import tpu as pltpu
 from jax.sharding import PartitionSpec as P
 
 HD = 128
@@ -30,7 +34,7 @@
     )
 
 
-def local(query, key_proj, value, block_mask, tile_sizes, temporal_ids):
+def local_by_tile(query, key_proj, value, block_mask, tile_sizes, temporal_ids):
     half_rows = query.shape[0]
     heads_here = block_mask.shape[0]
     temp_here = temporal_ids.shape[0]
@@ -117,6 +121,218 @@
     return combined.astype(jnp.bfloat16).reshape(half_rows, heads_here * HD)
 
 
+EXP2_SCALE = HD ** -0.5 * math.log2(math.e)
+ANY = pl.BlockSpec(memory_space=pl.ANY)
+SMEM = pl.BlockSpec(memory_space=pltpu.SMEM)
+VMEM = pl.BlockSpec(memory_space=pltpu.VMEM)
+
+
+def scores_of(rows, keys):
+    return lax.dot_general(rows, keys, (((1,), (1,)), ((), ())), preferred_element_type=jnp.float32)
+
+
+def attend(scores, values):
+    highest = scores[0].max(axis=-1, keepdims=True)
+    for more in scores[1:]:
+        highest = jnp.maximum(highest, more.max(axis=-1, keepdims=True))
+    total, out = 0.0, 0.0
+    for group, group_values in zip(scores, values):
+        raised = jnp.exp2((group - highest) * EXP2_SCALE)
+        total = total + raised.sum(axis=-1, keepdims=True)
+        out = out + jnp.dot(raised.astype(jnp.bfloat16), group_values, preferred_element_type=jnp.float32)
+    return (out / total).astype(jnp.bfloat16)
+
+
+def columns(index):
+    return pl.ds(pl.multiple_of(index * HD, HD), HD)
+
+
+def head_of(ids_ref, slot, heads_here):
+    return lax.rem(ids_ref[slot], heads_here)
+
+
+def pack_kernel(frames, heads_here, parts, where_ref, ids_ref, query, key_proj, value, *rest):
+    outs, sems = rest[:-1], rest[-1]
+    sources = {"q": query, "k": key_proj, "v": value}
+    copies = []
+    for out, (mask, names) in zip(outs, parts):
+        head = head_of(ids_ref, where_ref[0] ^ mask, heads_here)
+        for place, name in enumerate(names):
+            copies.append(
+                pltpu.make_async_copy(
+                    sources[name].at[:, columns(head)],
+                    out.at[:, place * HD : (place + 1) * HD],
+                    sems.at[len(copies)],
+                )
+            )
+            copies[-1].start()
+    for copy in copies:
+        copy.wait()
+
+
+def pack(where, ids, query, key_proj, value, parts, frames, heads_here):
+    rows = query.shape[0]
+    count = sum(len(names) for _, names in parts)
+    return pl.pallas_call(
+        lambda *refs: pack_kernel(frames, heads_here, parts, *refs),
+        out_shape=[jax.ShapeDtypeStruct((rows, len(names) * HD), query.dtype) for _, names in parts],
+        in_specs=[SMEM, SMEM, ANY, ANY, ANY],
+        out_specs=[ANY] * len(parts),
+        scratch_shapes=[pltpu.SemaphoreType.DMA((count,))],
+        name="pack",
+        compiler_params=pltpu.CompilerParams(vmem_limit_bytes=4 << 20),
+        cost_estimate=pl.CostEstimate(flops=0, bytes_accessed=2 * count * rows * HD * 2, transcendentals=0),
+    )(where, ids, query, key_proj, value)
+
+
+def spatial_kernel(step_heads, heads_here, where_ref, ids_ref, mask_ref, query, key_own, key_other, value_own, value_other, out):
+    rows = query.shape[0]
+    own_blocks, frame_blocks = rows // BLK, mask_ref.shape[-1]
+    rep = where_ref[1]
+    block = lax.broadcasted_iota(jnp.int32, (frame_blocks, 2 * rows), 1) // BLK
+    block = lax.rem(block + rep * own_blocks, frame_blocks)
+    spread = (block == lax.broadcasted_iota(jnp.int32, block.shape, 0)).astype(jnp.float32)
+    for item in range(step_heads):
+        here = pl.program_id(0) * step_heads + item
+        temporal = head_of(ids_ref, 0, heads_here) == here
+        for slot in range(1, ids_ref.shape[0]):
+            temporal |= head_of(ids_ref, slot, heads_here) == here
+
+        @pl.when(jnp.logical_not(temporal))
+        def _():
+            part = slice(item * HD, (item + 1) * HD)
+            seen = jnp.dot(mask_ref[item].astype(jnp.float32), spread, preferred_element_type=jnp.float32)
+            seen = jnp.where(rep == 0, seen[:own_blocks], seen[own_blocks:])
+            bias = jnp.where(seen > 0.5, 0.0, MASKED_SCORE)
+            bias = jnp.broadcast_to(bias[:, None, :], (own_blocks, BLK, 2 * rows)).reshape(rows, 2 * rows)
+            own = scores_of(query[:, part], key_own[:, part]) + bias[:, :rows]
+            other = scores_of(query[:, part], key_other[:, part]) + bias[:, rows:]
+            out[:, part] = attend([own, other], [value_own[:, part], value_other[:, part]])
+
+
+def spatial(where, ids, mask, query, key_own, key_other, value_own, value_other, step_heads=2):
+    rows, width = query.shape
+    heads_here, blocks = width // HD, mask.shape[-1]
+    piece = pl.BlockSpec((rows, step_heads * HD), lambda i: (0, i))
+    return pl.pallas_call(
+        lambda *refs: spatial_kernel(step_heads, heads_here, *refs),
+        out_shape=jax.ShapeDtypeStruct((rows, width), query.dtype),
+        grid=(heads_here // step_heads,),
+        in_specs=[SMEM, SMEM, pl.BlockSpec((step_heads, blocks, blocks), lambda i: (i, 0, 0))] + [piece] * 5,
+        out_specs=piece,
+        name="spatial",
+        compiler_params=pltpu.CompilerParams(vmem_limit_bytes=24 << 20),
+        cost_estimate=pl.CostEstimate(
+            flops=8 * rows * rows * width, bytes_accessed=12 * rows * width, transcendentals=2 * rows * rows * heads_here
+        ),
+    )(where, ids, mask, query, key_own, key_other, value_own, value_other)
+
+
+def tile_bias(sizes_ref, rows):
+    down = lax.broadcasted_iota(jnp.int32, (rows, 1), 0)
+    across = lax.broadcasted_iota(jnp.int32, (1, rows), 1)
+    tile_down, tile_across, end = jnp.zeros_like(down), jnp.zeros_like(across), 0
+    for tile in range(sizes_ref.shape[1]):
+        end = end + sizes_ref[0, tile]
+        tile_down = tile_down + (down >= end).astype(jnp.int32)
+        tile_across = tile_across + (across >= end).astype(jnp.int32)
+    return jnp.where(tile_down == tile_across, 0.0, MASKED_SCORE)
+
+
+def temporal_kernel(heads_here, where_ref, ids_ref, sizes_ref, query, key_proj, value, *rest):
+    partners = len(rest) // 2 - 1
+    received, outs, own, sems = rest[:partners], rest[partners : 2 * partners + 1], rest[-2], rest[-1]
+    rows = query.shape[0]
+    head = head_of(ids_ref, where_ref[0], heads_here)
+    copies = [
+        pltpu.make_async_copy(source.at[:, columns(head)], own.at[:, i * HD : (i + 1) * HD], sems.at[i])
+        for i, source in enumerate((query, key_proj, value))
+    ]
+    for copy in copies:
+        copy.start()
+    bias = tile_bias(sizes_ref, rows)
+    for copy in copies:
+        copy.wait()
+    pieces = (own,) + tuple(received)
+    keys = [piece[:, HD : 2 * HD] for piece in pieces]
+    values = [piece[:, 2 * HD :] for piece in pieces]
+    for piece, out in zip(pieces, outs):
+        out[...] = attend([scores_of(piece[:, :HD], group) + bias for group in keys], values)
+
+
+def temporal(where, ids, sizes, query, key_proj, value, received):
+    rows, width = query.shape
+    frames = len(received) + 1
+    return pl.pallas_call(
+        lambda *refs: temporal_kernel(width // HD, *refs),
+        out_shape=[jax.ShapeDtypeStruct((rows, HD), query.dtype)] * frames,
+        in_specs=[SMEM] * 3 + [ANY] * 3 + [VMEM] * len(received),
+        out_specs=[VMEM] * frames,
+        scratch_shapes=[pltpu.VMEM((rows, 3 * HD), query.dtype), pltpu.SemaphoreType.DMA((3,))],
+        name="temporal",
+        compiler_params=pltpu.CompilerParams(vmem_limit_bytes=24 << 20),
+        cost_estimate=pl.CostEstimate(
+            flops=4 * (frames * rows) ** 2 * HD, bytes_accessed=8 * frames * rows * HD, transcendentals=(frames * rows) ** 2
+        ),
+    )(where, ids, sizes, query, key_proj, value, *received)
+
+
+def merge_kernel(heads_here, where_ref, ids_ref, given, *rest):
+    pieces, out, sems = rest[:-2], rest[-2], rest[-1]
+    copies = []
+    for mask, piece in enumerate(pieces):
+        head = head_of(ids_ref, where_ref[0] ^ mask, heads_here)
+        copies.append(pltpu.make_async_copy(piece, out.at[:, columns(head)], sems.at[mask]))
+        copies[-1].start()
+    for copy in copies:
+        copy.wait()
+
+
+def merge(where, ids, out, pieces):
+    rows, width = out.shape
+    return pl.pallas_call(
+        lambda *refs: merge_kernel(width // HD, *refs),
+        out_shape=jax.ShapeDtypeStruct(out.shape, out.dtype),
+        in_specs=[SMEM, SMEM, ANY] + [VMEM] * len(pieces),
+        out_specs=ANY,
+        scratch_shapes=[pltpu.SemaphoreType.DMA((len(pieces),))],
+        input_output_aliases={2: 0},
+        name="merge",
+        compiler_params=pltpu.CompilerParams(vmem_limit_bytes=4 << 20),
+        cost_estimate=pl.CostEstimate(flops=0, bytes_accessed=4 * len(pieces) * rows * HD, transcendentals=0),
+    )(where, ids, out, *pieces)
+
+
+def local_by_head(query, key_proj, value, block_mask, tile_sizes, temporal_ids):
+    frames = lax.axis_size("frames")
+    heads_here = block_mask.shape[0]
+    where = jnp.stack([lax.axis_index("frames"), lax.axis_index("rep")]).astype(jnp.int32)
+
+    def exchange(array, mask):
+        return lax.ppermute(array, "frames", [(i, i ^ mask) for i in range(frames)])
+
+    def swap(array):
+        return lax.ppermute(array, "rep", [(0, 1), (1, 0)])
+
+    masks = list(range(1, frames))
+    packed = pack(where, temporal_ids, query, key_proj, value, [(m, "qkv") for m in masks], frames, heads_here)
+    received = [exchange(piece, m) for piece, m in zip(packed, masks)]
+    keys_sent, values_sent, *_ = lax.optimization_barrier((key_proj, value, *packed))
+    key_other, value_other = swap(keys_sent), swap(values_sent)
+    out = spatial(where, temporal_ids, block_mask, query, key_proj, key_other, value, value_other)
+    out, *received = lax.optimization_barrier((out, *received))
+    pieces = temporal(where, temporal_ids, tile_sizes, query, key_proj, value, received)
+    returned = [pieces[0]] + [exchange(piece, m) for piece, m in zip(pieces[1:], masks)]
+    return merge(where, temporal_ids, out, returned)
+
+
+def local(query, key_proj, value, block_mask, tile_sizes, temporal_ids):
+    frames, reps = lax.axis_size("frames"), lax.axis_size("rep")
+    by_head = temporal_ids.shape[0] == frames and frames & (frames - 1) == 0 and reps == 2
+    form = local_by_head if by_head else local_by_tile
+    return form(query, key_proj, value, block_mask, tile_sizes, temporal_ids)
+
+
 def solution(mesh):
     in_specs = (
         P(("groups", "frames", "rep"), "heads"),

time: 107 us -> 44.2 us (0.41)
  local copies, waits for them, and re-layouts: 28.9 us -> 1.84 us
  matrix products: 19.5 us -> 0 us
  Pallas kernels: 0 us -> 17.3 us
  between operations: 13.6 us -> 0.05 us
  waiting for transfers between devices: 23.8 us -> 12.3 us
  starting transfers between devices: 17.6 us -> 12.4 us
  other arithmetic: 2.82 us -> 0.07 us
    all_to_all x4 -> x0, waiting for transfers between devices: 23.8 us -> none  [the longest x1 13.7 us: local(): lax.all_to_all(send_keys, 'frames', split_axis=0, concat_axis=0, tiled=True)]
    all_to_all x4 -> x0, starting transfers between devices: 17.6 us -> none  [the longest x1 6.35 us: local(): lax.all_to_all(send_query, 'frames', split_axis=0, concat_axis=0, tiled=T...]
    pallas_call x0 -> x4, Pallas kernels: none -> 17.3 us  [the longest x1 6.77 us: spatial(): pl.pallas_call(lambda *refs: spatial_kernel(step_heads, heads_here, *refs...]
    ppermute x0 -> x8, starting transfers between devices: none -> 12.4 us  [the longest x6 11.8 us: exchange(): return lax.ppermute(array, 'frames', [(i, i ^ mask) for i in range(frames)])]
    ppermute x0 -> x8, waiting for transfers between devices: none -> 12.3 us  [the longest x6 12.3 us: exchange(): return lax.ppermute(array, 'frames', [(i, i ^ mask) for i in range(frames)])]
    dot_general x11 -> x0, matrix products: 11.2 us -> none  [the longest x6 3.5 us: select_heads(): jnp.einsum('rhd,th->rtd', head_grid, picker.astype(jnp.bfloat16), preferr...]
    gather x4 -> x0, local copies, waits for them, and re-layouts: 8.63 us -> none  [the longest x1 2.55 us: local(): send_keys = select_heads(key_proj, pick_temp)[source_rows]]
    sub x2 -> x0, matrix products: 8.31 us -> none  [softmax_weights(): raised = jnp.exp(scores - highest)]
  transfers between devices with their start and end apart: 6 -> 8, of which waited for: 4 -> 3; matrix products, arithmetic and copies ran while one was open for 40% -> 0% of each run, Pallas kernels for 0% -> 15%
where the time goes in v1:
time: 44.2 us; the launch traced here: 43.9 us
  Pallas kernels  17.3 us (39%)
  starting transfers between devices  12.4 us (28%)
  waiting for transfers between devices  12.3 us (28%)
  local copies, waits for them, and re-layouts  1.84 us (4%)
    ppermute x6, waiting for transfers between devices, exchange(): return lax.ppermute(array, 'frames', [(i, i ^ mask) for i in range(frames)])  12.3 us
    ppermute x6, starting transfers between devices, exchange(): return lax.ppermute(array, 'frames', [(i, i ^ mask) for i in range(frames)])  11.8 us
    pallas_call x1, Pallas kernels, spatial(): pl.pallas_call(lambda *refs: spatial_kernel(step_heads, heads_here, *refs...  6.77 us
    pallas_call x1, Pallas kernels, pack(): pl.pallas_call(lambda *refs: pack_kernel(frames, heads_here, parts, *refs...  5.72 us
    pallas_call x1, Pallas kernels, temporal(): pl.pallas_call(lambda *refs: temporal_kernel(width // HD, *refs), out_sha...  3.52 us
    unnamed x11, local copies, waits for them, and re-layouts  1.84 us
    pallas_call x1, Pallas kernels, merge(): pl.pallas_call(lambda *refs: merge_kernel(width // HD, *refs), out_shape=...  1.28 us
  transfers between devices with their start and end apart: 8, of which 3 were waited for; matrix products, arithmetic and copies ran while one was open for 0% of the time, Pallas kernels for 15%

profile of v1, /device:TPU:0, one launch (start us, length us, event | category | flops | bytes accessed | tf_op | source)
XLA Modules:
  0.0 43.9 jit_solution(7156589520731714645)
XLA Ops:
  0.0 0.0 copy-start.2
  0.0 0.1 pad_add_fusion.refs_0_
  0.1 0.6 %copy-done.2 = s32[4]{0:T(128)S(1)} copy-done((s32[4]{0:T(128)S(1)}, s32[4]{0:T(128)}, u32[]{:S(2)}) %copy-start.2) | copy-done | bytes 40
  0.7 0.0 copy-start
  0.7 1.1 %copy-done = bf16[256,1536]{1,0:T(8,128)(2,1)S(1)} copy-done((bf16[256,1536]{1,0:T(8,128)(2,1)S(1)}, bf16[256,1536]{1,0:T(8,128)(2,1)}, u32[]{:S(2)}) %copy-start) | copy-done | bytes 786456
  1.8 0.0 copy-start.4
  1.8 0.0 copy-start.1
  1.8 5.7 %pack.1 = (bf16[256,384]{1,0:T(8,128)(2,1)}, bf16[256,384]{1,0:T(8,128)(2,1)S(1)}, bf16[256,384]{1,0:T(8,128)(2,1)S(1)}) custom-call(s32[2]{0:T(128)S(1)} %pad_add_fusion.refs_0_, s32[4]{0:T(128)S(1)} %copy-done.2, bf16[256,1536]{1,0:T(8,128)(2,1)S(1)} %copy-done, bf16[256,1536]{1,0:T(8,128)(2,1)} %refs_4_.5, bf16[256,1536]{1,0:T(8,128)(2,1)} %refs_5_.1), custom_call_target="tpu_custom_call" | custom-call | bytes 1179648 | tf_op jit(solution)/shard_map/pack/pallas_call | solution.py:176
  7.5 0.6 %collective-permute-start = (bf16[256,1536]{1,0:T(8,128)(2,1)}, bf16[256,1536]{1,0:T(8,128)(2,1)S(1)}, u32[]{:S(2)}, u32[]{:S(2)}) collective-permute-start(bf16[256,1536]{1,0:T(8,128)(2,1)} %refs_4_.5), channel_id=1, source_target_pairs={{0,1},{1,0},{2,3},{3,2},{4,5},{5,4},{6,7},{7,6},{8,9},{9,8},{10,11... | collective-permute-start | bytes 2359304 | tf_op jit(solution)/shard_map/ppermute | solution.py:315
  8.1 0.1 collective-permute-start.1
  8.2 3.0 %collective-permute-start.2 = (bf16[256,384]{1,0:T(8,128)(2,1)}, bf16[256,384]{1,0:T(8,128)(2,1)S(1)}, u32[]{:S(2)}, u32[]{:S(2)}) collective-permute-start(bf16[256,384]{1,0:T(8,128)(2,1)} %get-tuple-element.18), channel_id=1, source_target_pairs={{0,4},{4,0},{8,12},{12,8},{1,5},{5,1},{9,13},{13,9},{2,6},{6,2},{1... | collective-permute-start | bytes 589832 | tf_op jit(solution)/shard_map/ppermute | solution.py:312
  11.1 2.6 %collective-permute-start.3 = (bf16[256,384]{1,0:T(8,128)(2,1)S(1)}, bf16[256,384]{1,0:T(8,128)(2,1)S(1)}, u32[]{:S(2)}, u32[]{:S(2)}) collective-permute-start(bf16[256,384]{1,0:T(8,128)(2,1)S(1)} %get-tuple-element.19), channel_id=1, source_target_pairs={{0,8},{4,12},{8,0},{12,4},{1,9},{5,13},{9,1},{13,5},{2,10},{6,14},... | collective-permute-start | bytes 589832 | tf_op jit(solution)/shard_map/ppermute | solution.py:312
  13.7 0.0 collective-permute-start.4
  13.7 0.0 copy-done.4
  13.7 0.1 copy.8.refs_2_
  13.9 0.0 copy-start.3
  13.9 0.0 collective-permute-done.refs_5_
  13.9 0.0 collective-permute-done.1.refs_7_
  13.9 0.0 copy-done.1
  13.9 6.8 %spatial.1.refs_2_ = bf16[256,1536]{1,0:T(8,128)(2,1)} custom-call(s32[2]{0:T(128)S(1)} %pad_add_fusion.refs_0_, s32[4]{0:T(128)S(1)} %copy-done.2, s32[12,8,8]{2,1,0:T(8,128)S(1)} %copy.8.refs_2_, bf16[256,1536]{1,0:T(8,128)(2,1)S(1)} %copy-done.1, bf16[256,1536]{1,0:T(8,128)(2,1)} %refs_4_.5, bf16[256,1536]{1,0:T(8,128)(2,1)S(1)} %collective-permute-done.refs_5_, ...), custom_call_target="tpu_custom_call" | custom-call | flops 805306368 | bytes 4718592 | tf_op jit(solution)/shard_map/spatial/pallas_call | solution.py:217
  20.7 0.0 collective-permute-done.2.refs_6_
  20.7 7.6 %collective-permute-done.3.refs_7_ = bf16[256,384]{1,0:T(8,128)(2,1)S(1)} collective-permute-done((bf16[256,384]{1,0:T(8,128)(2,1)S(1)}, bf16[256,384]{1,0:T(8,128)(2,1)S(1)}, u32[]{:S(2)}, u32[]{:S(2)}) %collective-permute-start.3) | collective-permute-done | bytes 196640 | tf_op jit(solution)/shard_map/ppermute | solution.py:312
  28.2 0.0 collective-permute-done.4.refs_8_
  28.3 0.0 copy-done.3
  28.3 3.5 %temporal.1 = (bf16[256,128]{1,0:T(8,128)(2,1)S(1)}, bf16[256,128]{1,0:T(8,128)(2,1)S(1)}, bf16[256,128]{1,0:T(8,128)(2,1)S(1)}, bf16[256,128]{1,0:T(8,128)(2,1)S(1)}) custom-call(s32[2]{0:T(128)S(1)} %pad_add_fusion.refs_0_, s32[4]{0:T(128)S(1)} %copy-done.2, s32[1,4]{1,0:T(1,128)S(1)} %copy-done.3, bf16[256,1536]{1,0:T(8,128)(2,1)S(1)} %copy-done.1, ...), custom_call_target="tpu_custom_call" | custom-call | flops 536870912 | bytes 1048576 | tf_op jit(solution)/shard_map/temporal/pallas_call | solution.py:266
  31.8 3.7 %collective-permute-start.5 = (bf16[256,128]{1,0:T(8,128)(2,1)S(1)}, bf16[256,128]{1,0:T(8,128)(2,1)S(1)}, u32[]{:S(2)}, u32[]{:S(2)}) collective-permute-start(bf16[256,128]{1,0:T(8,128)(2,1)S(1)} %get-tuple-element.28), channel_id=1, source_target_pairs={{0,4},{4,0},{8,12},{12,8},{1,5},{5,1},{9,13},{13,9},{2,6},{6,2},{1... | collective-permute-start | bytes 196616 | tf_op jit(solution)/shard_map/ppermute | solution.py:312
  35.5 1.1 %collective-permute-start.6 = (bf16[256,128]{1,0:T(8,128)(2,1)S(1)}, bf16[256,128]{1,0:T(8,128)(2,1)S(1)}, u32[]{:S(2)}, u32[]{:S(2)}) collective-permute-start(bf16[256,128]{1,0:T(8,128)(2,1)S(1)} %get-tuple-element.29), channel_id=1, source_target_pairs={{0,8},{4,12},{8,0},{12,4},{1,9},{5,13},{9,1},{13,5},{2,10},{6,14},... | collective-permute-start | bytes 196616 | tf_op jit(solution)/shard_map/ppermute | solution.py:312
  36.6 1.4 %collective-permute-start.7 = (bf16[256,128]{1,0:T(8,128)(2,1)S(1)}, bf16[256,128]{1,0:T(8,128)(2,1)S(1)}, u32[]{:S(2)}, u32[]{:S(2)}) collective-permute-start(bf16[256,128]{1,0:T(8,128)(2,1)S(1)} %get-tuple-element.30), channel_id=1, source_target_pairs={{0,12},{4,8},{8,4},{12,0},{1,13},{5,9},{9,5},{13,1},{2,14},{6,10},... | collective-permute-start | bytes 196616 | tf_op jit(solution)/shard_map/ppermute | solution.py:312
  38.0 0.0 collective-permute-done.5.refs_4_
  38.0 3.9 %collective-permute-done.6.refs_5_ = bf16[256,128]{1,0:T(8,128)(2,1)S(1)} collective-permute-done((bf16[256,128]{1,0:T(8,128)(2,1)S(1)}, bf16[256,128]{1,0:T(8,128)(2,1)S(1)}, u32[]{:S(2)}, u32[]{:S(2)}) %collective-permute-start.6) | collective-permute-done | bytes 65568 | tf_op jit(solution)/shard_map/ppermute | solution.py:312
  41.9 0.7 %collective-permute-done.7.refs_6_ = bf16[256,128]{1,0:T(8,128)(2,1)S(1)} collective-permute-done((bf16[256,128]{1,0:T(8,128)(2,1)S(1)}, bf16[256,128]{1,0:T(8,128)(2,1)S(1)}, u32[]{:S(2)}, u32[]{:S(2)}) %collective-permute-start.7) | collective-permute-done | bytes 65568 | tf_op jit(solution)/shard_map/ppermute | solution.py:312
  42.7 1.3 %merge.1 = bf16[256,1536]{1,0:T(8,128)(2,1)} custom-call(s32[2]{0:T(128)S(1)} %pad_add_fusion.refs_0_, s32[4]{0:T(128)S(1)} %copy-done.2, bf16[256,1536]{1,0:T(8,128)(2,1)} %spatial.1.refs_2_, bf16[256,128]{1,0:T(8,128)(2,1)S(1)} %get-tuple-element.27.refs_3_, bf16[256,128]{1,0:T(8,128)(2,1)S(1)} %collective-permute-done.5.refs_4_, ...), custom_call_target="tpu_custom_call", output_to_operand_aliasing={{}: (2, {})} | custom-call | bytes 524288 | tf_op jit(solution)/shard_map/merge/pallas_call | solution.py:293
Async XLA Ops:
  0.0 0.7 %copy-start.2 = (s32[4]{0:T(128)S(1)}, s32[4]{0:T(128)}, u32[]{:S(2)}) copy-start(s32[4]{0:T(128)} %refs_1_.7) | copy-start | bytes 52
  0.7 1.1 %copy-start = (bf16[256,1536]{1,0:T(8,128)(2,1)S(1)}, bf16[256,1536]{1,0:T(8,128)(2,1)}, u32[]{:S(2)}) copy-start(bf16[256,1536]{1,0:T(8,128)(2,1)} %refs_3_.5) | copy-start | bytes 2359300
  1.8 12.0 %copy-start.4 = (s32[12,8,8]{0,2,1:T(8,128)S(1)}, s32[12,8,8]{0,2,1:T(8,128)}, u32[]{:S(2)}) copy-start(s32[12,8,8]{0,2,1:T(8,128)} %param.9) | copy-start | bytes 9220
  1.8 12.1 %copy-start.1 = (bf16[256,1536]{1,0:T(8,128)(2,1)S(1)}, bf16[256,1536]{1,0:T(8,128)(2,1)}, u32[]{:S(2)}) copy-start(bf16[256,1536]{1,0:T(8,128)(2,1)} %refs_3_.5) | copy-start | bytes 2359300
  7.5 6.3 %collective-permute-start = (bf16[256,1536]{1,0:T(8,128)(2,1)}, bf16[256,1536]{1,0:T(8,128)(2,1)S(1)}, u32[]{:S(2)}, u32[]{:S(2)}) collective-permute-start(bf16[256,1536]{1,0:T(8,128)(2,1)} %refs_4_.5), channel_id=1, source_target_pairs={{0,1},{1,0},{2,3},{3,2},{4,5},{5,4},{6,7},{7,6},{8,9},{9,8},{10,11... | collective-permute-start | bytes 2359304 | tf_op jit(solution)/shard_map/ppermute | solution.py:315
  8.1 5.8 %collective-permute-start.1 = (bf16[256,1536]{1,0:T(8,128)(2,1)}, bf16[256,1536]{1,0:T(8,128)(2,1)S(1)}, u32[]{:S(2)}, u32[]{:S(2)}) collective-permute-start(bf16[256,1536]{1,0:T(8,128)(2,1)} %refs_5_.1), channel_id=1, source_target_pairs={{0,1},{1,0},{2,3},{3,2},{4,5},{5,4},{6,7},{7,6},{8,9},{9,8},{10,11... | collective-permute-start | bytes 2359304 | tf_op jit(solution)/shard_map/ppermute | solution.py:315
  8.2 12.5 %collective-permute-start.2 = (bf16[256,384]{1,0:T(8,128)(2,1)}, bf16[256,384]{1,0:T(8,128)(2,1)S(1)}, u32[]{:S(2)}, u32[]{:S(2)}) collective-permute-start(bf16[256,384]{1,0:T(8,128)(2,1)} %get-tuple-element.18), channel_id=1, source_target_pairs={{0,4},{4,0},{8,12},{12,8},{1,5},{5,1},{9,13},{13,9},{2,6},{6,2},{1... | collective-permute-start | bytes 589832 | tf_op jit(solution)/shard_map/ppermute | solution.py:312
  11.1 17.1 %collective-permute-start.3 = (bf16[256,384]{1,0:T(8,128)(2,1)S(1)}, bf16[256,384]{1,0:T(8,128)(2,1)S(1)}, u32[]{:S(2)}, u32[]{:S(2)}) collective-permute-start(bf16[256,384]{1,0:T(8,128)(2,1)S(1)} %get-tuple-element.19), channel_id=1, source_target_pairs={{0,8},{4,12},{8,0},{12,4},{1,9},{5,13},{9,1},{13,5},{2,10},{6,14},... | collective-permute-start | bytes 589832 | tf_op jit(solution)/shard_map/ppermute | solution.py:312
  13.7 14.5 %collective-permute-start.4 = (bf16[256,384]{1,0:T(8,128)(2,1)S(1)}, bf16[256,384]{1,0:T(8,128)(2,1)S(1)}, u32[]{:S(2)}, u32[]{:S(2)}) collective-permute-start(bf16[256,384]{1,0:T(8,128)(2,1)S(1)} %get-tuple-element.20), channel_id=1, source_target_pairs={{0,12},{4,8},{8,4},{12,0},{1,13},{5,9},{9,5},{13,1},{2,14},{6,10},... | collective-permute-start | bytes 589832 | tf_op jit(solution)/shard_map/ppermute | solution.py:312
  13.9 14.4 %copy-start.3 = (s32[1,4]{1,0:T(1,128)S(1)}, s32[1,4]{1,0:T(1,128)}, u32[]{:S(2)}) copy-start(s32[1,4]{1,0:T(1,128)} %refs_2_.4) | copy-start | bytes 52
  31.8 6.2 %collective-permute-start.5 = (bf16[256,128]{1,0:T(8,128)(2,1)S(1)}, bf16[256,128]{1,0:T(8,128)(2,1)S(1)}, u32[]{:S(2)}, u32[]{:S(2)}) collective-permute-start(bf16[256,128]{1,0:T(8,128)(2,1)S(1)} %get-tuple-element.28), channel_id=1, source_target_pairs={{0,4},{4,0},{8,12},{12,8},{1,5},{5,1},{9,13},{13,9},{2,6},{6,2},{1... | collective-permute-start | bytes 196616 | tf_op jit(solution)/shard_map/ppermute | solution.py:312
  35.5 6.4 %collective-permute-start.6 = (bf16[256,128]{1,0:T(8,128)(2,1)S(1)}, bf16[256,128]{1,0:T(8,128)(2,1)S(1)}, u32[]{:S(2)}, u32[]{:S(2)}) collective-permute-start(bf16[256,128]{1,0:T(8,128)(2,1)S(1)} %get-tuple-element.29), channel_id=1, source_target_pairs={{0,8},{4,12},{8,0},{12,4},{1,9},{5,13},{9,1},{13,5},{2,10},{6,14},... | collective-permute-start | bytes 196616 | tf_op jit(solution)/shard_map/ppermute | solution.py:312
  36.6 6.1 %collective-permute-start.7 = (bf16[256,128]{1,0:T(8,128)(2,1)S(1)}, bf16[256,128]{1,0:T(8,128)(2,1)S(1)}, u32[]{:S(2)}, u32[]{:S(2)}) collective-permute-start(bf16[256,128]{1,0:T(8,128)(2,1)S(1)} %get-tuple-element.30), channel_id=1, source_target_pairs={{0,12},{4,8},{8,4},{12,0},{1,13},{5,9},{9,5},{13,1},{2,14},{6,10},... | collective-permute-start | bytes 196616 | tf_op jit(solution)/shard_map/ppermute | solution.py:312

commit v2 on v1

--- a/solution.py
+++ b/solution.py
@@ -6,6 +6,7 @@
 from jax.experimental import pallas as pl
 from jax.experimental.pallas import tpu as pltpu
 from jax.sharding import PartitionSpec as P
+
 
 HD = 128
 BLK = 64
@@ -122,6 +123,7 @@
 
 
 EXP2_SCALE = HD ** -0.5 * math.log2(math.e)
+HBM = pl.BlockSpec(memory_space=pltpu.HBM)
 ANY = pl.BlockSpec(memory_space=pl.ANY)
 SMEM = pl.BlockSpec(memory_space=pltpu.SMEM)
 VMEM = pl.BlockSpec(memory_space=pltpu.VMEM)
@@ -151,18 +153,22 @@
     return lax.rem(ids_ref[slot], heads_here)
 
 
-def pack_kernel(frames, heads_here, parts, where_ref, ids_ref, query, key_proj, value, *rest):
-    outs, sems = rest[:-1], rest[-1]
+def pack_kernel(heads_here, parts, ids_hbm, query, key_proj, value, *rest):
+    outs, ids_ref, sems = rest[: len(parts)], rest[-2], rest[-1]
     sources = {"q": query, "k": key_proj, "v": value}
+    fetch = pltpu.make_async_copy(ids_hbm, ids_ref, sems.at[0])
+    fetch.start()
+    frame = lax.axis_index("frames")
+    fetch.wait()
     copies = []
     for out, (mask, names) in zip(outs, parts):
-        head = head_of(ids_ref, where_ref[0] ^ mask, heads_here)
+        head = head_of(ids_ref, frame ^ mask, heads_here)
         for place, name in enumerate(names):
             copies.append(
                 pltpu.make_async_copy(
                     sources[name].at[:, columns(head)],
                     out.at[:, place * HD : (place + 1) * HD],
-                    sems.at[len(copies)],
+                    sems.at[len(copies) + 1],
                 )
             )
             copies[-1].start()
@@ -170,19 +176,19 @@
         copy.wait()
 
 
-def pack(where, ids, query, key_proj, value, parts, frames, heads_here):
+def pack(ids, query, key_proj, value, parts, heads_here):
     rows = query.shape[0]
     count = sum(len(names) for _, names in parts)
     return pl.pallas_call(
-        lambda *refs: pack_kernel(frames, heads_here, parts, *refs),
-        out_shape=[jax.ShapeDtypeStruct((rows, len(names) * HD), query.dtype) for _, names in parts],
-        in_specs=[SMEM, SMEM, ANY, ANY, ANY],
-        out_specs=[ANY] * len(parts),
-        scratch_shapes=[pltpu.SemaphoreType.DMA((count,))],
+        lambda *refs: pack_kernel(heads_here, parts, *refs),
+        out_shape=[pltpu.VMEM((rows, len(names) * HD), query.dtype) for _, names in parts],
+        in_specs=[HBM] * 4,
+        out_specs=[VMEM] * len(parts),
+        scratch_shapes=[pltpu.SMEM(ids.shape, jnp.int32), pltpu.SemaphoreType.DMA((count + 1,))],
         name="pack",
         compiler_params=pltpu.CompilerParams(vmem_limit_bytes=4 << 20),
-        cost_estimate=pl.CostEstimate(flops=0, bytes_accessed=2 * count * rows * HD * 2, transcendentals=0),
-    )(where, ids, query, key_proj, value)
+        cost_estimate=pl.CostEstimate(flops=0, bytes_accessed=4 * count * rows * HD, transcendentals=0),
+    )(*(pltpu.with_memory_space_constraint(array, pltpu.HBM) for array in (ids, query, key_proj, value)))
 
 
 def spatial_kernel(step_heads, heads_here, where_ref, ids_ref, mask_ref, query, key_own, key_other, value_own, value_other, out):
@@ -228,7 +234,8 @@
     )(where, ids, mask, query, key_own, key_other, value_own, value_other)
 
 
-def tile_bias(sizes_ref, rows):
+def tile_bias_kernel(sizes_ref, out):
+    rows = out.shape[0]
     down = lax.broadcasted_iota(jnp.int32, (rows, 1), 0)
     across = lax.broadcasted_iota(jnp.int32, (1, rows), 1)
     tile_down, tile_across, end = jnp.zeros_like(down), jnp.zeros_like(across), 0
@@ -236,45 +243,46 @@
         end = end + sizes_ref[0, tile]
         tile_down = tile_down + (down >= end).astype(jnp.int32)
         tile_across = tile_across + (across >= end).astype(jnp.int32)
-    return jnp.where(tile_down == tile_across, 0.0, MASKED_SCORE)
-
-
-def temporal_kernel(heads_here, where_ref, ids_ref, sizes_ref, query, key_proj, value, *rest):
-    partners = len(rest) // 2 - 1
-    received, outs, own, sems = rest[:partners], rest[partners : 2 * partners + 1], rest[-2], rest[-1]
-    rows = query.shape[0]
-    head = head_of(ids_ref, where_ref[0], heads_here)
-    copies = [
-        pltpu.make_async_copy(source.at[:, columns(head)], own.at[:, i * HD : (i + 1) * HD], sems.at[i])
-        for i, source in enumerate((query, key_proj, value))
-    ]
-    for copy in copies:
-        copy.start()
-    bias = tile_bias(sizes_ref, rows)
-    for copy in copies:
-        copy.wait()
-    pieces = (own,) + tuple(received)
-    keys = [piece[:, HD : 2 * HD] for piece in pieces]
-    values = [piece[:, 2 * HD :] for piece in pieces]
-    for piece, out in zip(pieces, outs):
-        out[...] = attend([scores_of(piece[:, :HD], group) + bias for group in keys], values)
-
-
-def temporal(where, ids, sizes, query, key_proj, value, received):
-    rows, width = query.shape
-    frames = len(received) + 1
-    return pl.pallas_call(
-        lambda *refs: temporal_kernel(width // HD, *refs),
-        out_shape=[jax.ShapeDtypeStruct((rows, HD), query.dtype)] * frames,
-        in_specs=[SMEM] * 3 + [ANY] * 3 + [VMEM] * len(received),
-        out_specs=[VMEM] * frames,
-        scratch_shapes=[pltpu.VMEM((rows, 3 * HD), query.dtype), pltpu.SemaphoreType.DMA((3,))],
+    out[...] = jnp.where(tile_down == tile_across, 0.0, MASKED_SCORE)
+
+
+def tile_bias(sizes, rows):
+    return pl.pallas_call(
+        tile_bias_kernel,
+        out_shape=jax.ShapeDtypeStruct((rows, rows), jnp.float32),
+        in_specs=[SMEM],
+        out_specs=VMEM,
+        name="tile_bias",
+        compiler_params=pltpu.CompilerParams(vmem_limit_bytes=4 << 20),
+        cost_estimate=pl.CostEstimate(flops=rows * rows, bytes_accessed=4 * rows * rows, transcendentals=0),
+    )(sizes)
+
+
+def temporal_kernel(keys_at, queries, bias_ref, *refs):
+    outs, pieces = refs[len(refs) - queries :], refs[: len(refs) - queries]
+    query_refs, group_refs = pieces[:queries], pieces[queries:]
+    bias = bias_ref[...]
+    keys = [ref[:, at : at + HD] for ref, at in zip(group_refs, keys_at)]
+    values = [ref[:, at + HD : at + 2 * HD] for ref, at in zip(group_refs, keys_at)]
+    for query_ref, out in zip(query_refs, outs):
+        rows = query_ref[:, :HD]
+        out[...] = attend([scores_of(rows, group) + bias for group in keys], values)
+
+
+def temporal(bias, queries, groups, keys_at):
+    rows = bias.shape[0]
+    work = len(queries) * len(groups) * rows * rows
+    return pl.pallas_call(
+        lambda *refs: temporal_kernel(keys_at, len(queries), *refs),
+        out_shape=[jax.ShapeDtypeStruct((rows, HD), queries[0].dtype)] * len(queries),
+        in_specs=[VMEM] * (1 + len(queries) + len(groups)),
+        out_specs=[VMEM] * len(queries),
         name="temporal",
-        compiler_params=pltpu.CompilerParams(vmem_limit_bytes=24 << 20),
+        compiler_params=pltpu.CompilerParams(vmem_limit_bytes=16 << 20),
         cost_estimate=pl.CostEstimate(
-            flops=4 * (frames * rows) ** 2 * HD, bytes_accessed=8 * frames * rows * HD, transcendentals=(frames * rows) ** 2
+            flops=4 * work * HD, bytes_accessed=4 * (len(queries) + len(groups)) * rows * HD, transcendentals=work
         ),
-    )(where, ids, sizes, query, key_proj, value, *received)
+    )(bias, *queries, *groups)
 
 
 def merge_kernel(heads_here, where_ref, ids_ref, given, *rest):
@@ -314,16 +322,31 @@
     def swap(array):
         return lax.ppermute(array, "rep", [(0, 1), (1, 0)])
 
-    masks = list(range(1, frames))
-    packed = pack(where, temporal_ids, query, key_proj, value, [(m, "qkv") for m in masks], frames, heads_here)
-    received = [exchange(piece, m) for piece, m in zip(packed, masks)]
+    *near, last = sorted(range(1, frames), key=lambda mask: (mask % 2 == 0, -mask))
+    parts = [(m, "qkv") for m in near[:1]] + [(last, "kv")] + [(m, "qkv") for m in near[1:]] + [(last, "q"), (0, "qkv")]
+    packed = pack(temporal_ids, query, key_proj, value, parts, heads_here)
+    *travelling, own = packed
+    arrived = [exchange(piece, mask) for piece, (mask, _) in zip(travelling, parts)]
     keys_sent, values_sent, *_ = lax.optimization_barrier((key_proj, value, *packed))
     key_other, value_other = swap(keys_sent), swap(values_sent)
+    bias = tile_bias(tile_sizes, query.shape[0])
     out = spatial(where, temporal_ids, block_mask, query, key_proj, key_other, value, value_other)
-    out, *received = lax.optimization_barrier((out, *received))
-    pieces = temporal(where, temporal_ids, tile_sizes, query, key_proj, value, received)
-    returned = [pieces[0]] + [exchange(piece, m) for piece, m in zip(pieces[1:], masks)]
-    return merge(where, temporal_ids, out, returned)
+    *arrived, late_query = arrived
+    out, *arrived = lax.optimization_barrier((out, *arrived))
+    groups = [own] + arrived
+    keys_at = [HD] + [HD if names == "qkv" else 0 for _, names in parts[: len(arrived)]]
+    whole = {mask: piece for piece, (mask, names) in zip(arrived, parts) if names == "qkv"}
+    returned = {}
+    (first,) = temporal(bias, [whole.pop(near[0])], groups, keys_at)
+    returned[near[0]] = exchange(first, near[0])
+    late_query, _ = lax.optimization_barrier((late_query, first))
+    (second,) = temporal(bias, [late_query], groups, keys_at)
+    returned[last] = exchange(second, last)
+    own_query, *others, _ = lax.optimization_barrier((own, *whole.values(), second))
+    mine, *rest = temporal(bias, [own_query, *others], groups, keys_at)
+    for mask, piece in zip(whole, rest):
+        returned[mask] = exchange(piece, mask)
+    return merge(where, temporal_ids, out, [mine] + [returned[mask] for mask in range(1, frames)])
 
 
 def local(query, key_proj, value, block_mask, tile_sizes, temporal_ids):

time: 44.2 us -> 38.7 us (0.88)
  Pallas kernels: 17.3 us -> 13.5 us
  waiting for transfers between devices: 12.3 us -> 9.65 us
  starting transfers between devices: 12.4 us -> 13 us
    pallas_call x2 -> x5, Pallas kernels: 9.23 us -> 5.81 us  [the longest x1 2.85 us: pack(): pl.pallas_call(lambda *refs: pack_kernel(heads_here, parts, *refs), out_s...]
    ppermute x6 -> x7, waiting for transfers between devices: 12.3 us -> 9.65 us  [exchange(): return lax.ppermute(array, 'frames', [(i, i ^ mask) for i in range(frames)])]
    ppermute x6 -> x7, starting transfers between devices: 11.8 us -> 12.5 us  [exchange(): return lax.ppermute(array, 'frames', [(i, i ^ mask) for i in range(frames)])]
    unnamed x11 -> x13, local copies, waits for them, and re-layouts: 1.84 us -> 2.09 us
  transfers between devices with their start and end apart: 8 -> 9, of which waited for: 3 -> 4; matrix products, arithmetic and copies ran while one was open for 0% -> 2% of each run, Pallas kernels for 15% -> 20%
where the time goes in v2:
time: 38.7 us; the launch traced here: 38.4 us
  Pallas kernels  13.5 us (35%)
  starting transfers between devices  13 us (34%)
  waiting for transfers between devices  9.65 us (25%)
  local copies, waits for them, and re-layouts  2.09 us (5%)
    ppermute x7, starting transfers between devices, exchange(): return lax.ppermute(array, 'frames', [(i, i ^ mask) for i in range(frames)])  12.5 us
    ppermute x7, waiting for transfers between devices, exchange(): return lax.ppermute(array, 'frames', [(i, i ^ mask) for i in range(frames)])  9.65 us
    pallas_call x1, Pallas kernels, spatial(): pl.pallas_call(lambda *refs: spatial_kernel(step_heads, heads_here, *refs...  6.4 us
    pallas_call x1, Pallas kernels, pack(): pl.pallas_call(lambda *refs: pack_kernel(heads_here, parts, *refs), out_s...  2.85 us
    pallas_call x3, Pallas kernels, temporal(): pl.pallas_call(lambda *refs: temporal_kernel(keys_at, len(queries), *refs...  2.35 us
    unnamed x13, local copies, waits for them, and re-layouts  2.09 us
    pallas_call x1, Pallas kernels, merge(): pl.pallas_call(lambda *refs: merge_kernel(width // HD, *refs), out_shape=...  1.28 us
  transfers between devices with their start and end apart: 9, of which 4 were waited for; matrix products, arithmetic and copies ran while one was open for 2% of the time, Pallas kernels for 20%

profile of v2, /device:TPU:0, one launch (start us, length us, event | category | flops | bytes accessed | tf_op | source)
XLA Modules:
  0.0 38.4 jit_solution(10619389079876117328)
XLA Ops:
  0.0 2.8 %pack.1 = (bf16[256,384]{1,0:T(8,128)(2,1)}, bf16[256,256]{1,0:T(8,128)(2,1)S(1)}, bf16[256,384]{1,0:T(8,128)(2,1)}, bf16[256,128]{1,0:T(8,128)(2,1)S(1)}, bf16[256,384]{1,0:T(8,128)(2,1)S(1)}) custom-call(s32[4]{0:T(128)} %refs_1_.5, bf16[256,1536]{1,0:T(8,128)(2,1)} %refs_3_.3, bf16[256,1536]{1,0:T(8,128)(2,1)} %refs_4_.1, bf16[256,1536]{1,0:T(8,128)(2,1)} %refs_6_.1), custom_call_target="tpu_custom_call" | custom-call | bytes 1572864 | tf_op jit(solution)/shard_map/pack/pallas_call | solution.py:182
  2.9 0.0 copy-start.5
  2.9 0.6 %copy-done.5 = bf16[256,128]{1,0:T(8,128)(2,1)} copy-done((bf16[256,128]{1,0:T(8,128)(2,1)}, bf16[256,128]{1,0:T(8,128)(2,1)S(1)}, u32[]{:S(2)}) %copy-start.5) | copy-done | bytes 65560
  3.5 0.5 %collective-permute-start = (bf16[256,1536]{1,0:T(8,128)(2,1)S(1)}, bf16[256,1536]{1,0:T(8,128)(2,1)}, u32[]{:S(2)}, u32[]{:S(2)}) collective-permute-start(bf16[256,1536]{1,0:T(8,128)(2,1)S(1)} %copy-done.1), channel_id=1, source_target_pairs={{0,1},{1,0},{2,3},{3,2},{4,5},{5,4},{6,7},{7,6},{8,9},{9,8},{10,11... | collective-permute-start | bytes 2359304 | tf_op jit(solution)/shard_map/ppermute | solution.py:323
  4.0 0.1 collective-permute-start.1
  4.1 5.0 %collective-permute-start.2 = (bf16[256,384]{1,0:T(8,128)(2,1)}, bf16[256,384]{1,0:T(8,128)(2,1)S(1)}, u32[]{:S(2)}, u32[]{:S(2)}) collective-permute-start(bf16[256,384]{1,0:T(8,128)(2,1)} %get-tuple-element.21), channel_id=1, source_target_pairs={{0,12},{4,8},{8,4},{12,0},{1,13},{5,9},{9,5},{13,1},{2,14},{6,10},... | collective-permute-start | bytes 589832 | tf_op jit(solution)/shard_map/ppermute | solution.py:320
  9.1 0.0 collective-permute-start.4
  9.1 0.6 %collective-permute-start.3 = (bf16[256,256]{1,0:T(8,128)(2,1)S(1)}, bf16[256,256]{1,0:T(8,128)(2,1)S(1)}, u32[]{:S(2)}, u32[]{:S(2)}) collective-permute-start(bf16[256,256]{1,0:T(8,128)(2,1)S(1)} %get-tuple-element.22), channel_id=1, source_target_pairs={{0,8},{4,12},{8,0},{12,4},{1,9},{5,13},{9,1},{13,5},{2,10},{6,14},... | collective-permute-start | bytes 393224 | tf_op jit(solution)/shard_map/ppermute | solution.py:320
  9.7 0.1 pad_add_fusion.refs_0_
  9.7 0.6 %copy-done.4 = s32[1,4]{1,0:T(1,128)S(1)} copy-done((s32[1,4]{1,0:T(1,128)S(1)}, s32[1,4]{1,0:T(1,128)}, u32[]{:S(2)}) %copy-start.4) | copy-done | bytes 40
  10.3 0.6 %tile_bias.1.refs_0_ = f32[256,256]{1,0:T(8,128)S(1)} custom-call(s32[1,4]{1,0:T(1,128)S(1)} %copy-done.4), custom_call_target="tpu_custom_call" | custom-call | flops 65536 | bytes 262144 | tf_op jit(solution)/shard_map/tile_bias/pallas_call | solution.py:250
  10.9 0.0 copy-start.3
  10.9 0.9 %copy.8.refs_2_ = s32[12,8,8]{2,1,0:T(8,128)S(1)} copy(s32[12,8,8]{0,2,1:T(8,128)} %param.9) | data formatting | bytes 6144 | tf_op args[3]
  11.8 0.0 collective-permute-done.refs_5_
  11.8 2.4 %collective-permute-start.5 = (bf16[256,128]{1,0:T(8,128)(2,1)}, bf16[256,128]{1,0:T(8,128)(2,1)S(1)}, u32[]{:S(2)}, u32[]{:S(2)}) collective-permute-start(bf16[256,128]{1,0:T(8,128)(2,1)} %copy-done.5), channel_id=1, source_target_pairs={{0,8},{4,12},{8,0},{12,4},{1,9},{5,13},{9,1},{13,5},{2,10},{6,14},... | collective-permute-start | bytes 196616 | tf_op jit(solution)/shard_map/ppermute | solution.py:320
  14.3 0.0 collective-permute-done.1.refs_7_
  14.3 0.0 copy-done
  14.3 6.4 %spatial.1.refs_2_ = bf16[256,1536]{1,0:T(8,128)(2,1)} custom-call(s32[2]{0:T(128)S(1)} %pad_add_fusion.refs_0_, s32[4]{0:T(128)S(1)} %copy-done.3, s32[12,8,8]{2,1,0:T(8,128)S(1)} %copy.8.refs_2_, bf16[256,1536]{1,0:T(8,128)(2,1)S(1)} %copy-done, bf16[256,1536]{1,0:T(8,128)(2,1)S(1)} %copy-done.1, bf16[256,1536]{1,0:T(8,128)(2,1)} %collective-permute-done.refs_5_, ...), custom_call_target="tpu_custom_call" | custom-call | flops 805306368 | bytes 4718592 | tf_op jit(solution)/shard_map/spatial/pallas_call | solution.py:223
  20.7 4.9 %collective-permute-done.3.refs_4_.refs_5_ = bf16[256,256]{1,0:T(8,128)(2,1)S(1)} collective-permute-done((bf16[256,256]{1,0:T(8,128)(2,1)S(1)}, bf16[256,256]{1,0:T(8,128)(2,1)S(1)}, u32[]{:S(2)}, u32[]{:S(2)}) %collective-permute-start.3) | collective-permute-done | bytes 131104 | tf_op jit(solution)/shard_map/ppermute | solution.py:320
  25.5 0.0 collective-permute-done.2.refs_1_.refs_3_.refs_4_
  25.5 0.0 collective-permute-done.4.refs_5_.refs_2_.refs_6_
  25.5 0.6 %temporal.3 = bf16[256,128]{1,0:T(8,128)(2,1)S(1)} custom-call(f32[256,256]{1,0:T(8,128)S(1)} %tile_bias.1.refs_0_, bf16[256,384]{1,0:T(8,128)(2,1)S(1)} %collective-permute-done.2.refs_1_.refs_3_.refs_4_, bf16[256,384]{1,0:T(8,128)(2,1)S(1)} %get-tuple-element.33.refs_2_.refs_1_.refs_3_, ...), custom_call_target="tpu_custom_call" | custom-call | flops 134217728 | bytes 655360 | tf_op jit(solution)/shard_map/temporal/pallas_call | solution.py:275
  26.2 0.1 collective-permute-done.5.refs_1_
  26.2 0.6 %temporal.4 = bf16[256,128]{1,0:T(8,128)(2,1)S(1)} custom-call(f32[256,256]{1,0:T(8,128)S(1)} %tile_bias.1.refs_0_, bf16[256,128]{1,0:T(8,128)(2,1)S(1)} %collective-permute-done.5.refs_1_, bf16[256,384]{1,0:T(8,128)(2,1)S(1)} %get-tuple-element.33.refs_2_.refs_1_.refs_3_, bf16[256,384]{1,0:T(8,128)(2,1)S(1)} %collective-permute-done.2.refs_1_.refs_3_.refs_4_, ...), custom_call_target="tpu_custom_call" | custom-call | flops 134217728 | bytes 655360 | tf_op jit(solution)/shard_map/temporal/pallas_call | solution.py:275
  26.9 1.1 %temporal.5 = (bf16[256,128]{1,0:T(8,128)(2,1)S(1)}, bf16[256,128]{1,0:T(8,128)(2,1)S(1)}) custom-call(f32[256,256]{1,0:T(8,128)S(1)} %tile_bias.1.refs_0_, bf16[256,384]{1,0:T(8,128)(2,1)S(1)} %get-tuple-element.33.refs_2_.refs_1_.refs_3_, bf16[256,384]{1,0:T(8,128)(2,1)S(1)} %collective-permute-done.4.refs_5_.refs_2_.refs_6_, ...), custom_call_target="tpu_custom_call" | custom-call | flops 268435456 | bytes 786432 | tf_op jit(solution)/shard_map/temporal/pallas_call | solution.py:275
  28.0 0.1 collective-permute-start.6
  28.0 3.0 %collective-permute-start.7 = (bf16[256,128]{1,0:T(8,128)(2,1)S(1)}, bf16[256,128]{1,0:T(8,128)(2,1)S(1)}, u32[]{:S(2)}, u32[]{:S(2)}) collective-permute-start(bf16[256,128]{1,0:T(8,128)(2,1)S(1)} %temporal.4), channel_id=1, source_target_pairs={{0,8},{4,12},{8,0},{12,4},{1,9},{5,13},{9,1},{13,5},{2,10},{6,14},... | collective-permute-start | bytes 196616 | tf_op jit(solution)/shard_map/ppermute | solution.py:320
  31.1 1.4 %collective-permute-start.8 = (bf16[256,128]{1,0:T(8,128)(2,1)S(1)}, bf16[256,128]{1,0:T(8,128)(2,1)S(1)}, u32[]{:S(2)}, u32[]{:S(2)}) collective-permute-start(bf16[256,128]{1,0:T(8,128)(2,1)S(1)} %temporal.3), channel_id=1, source_target_pairs={{0,12},{4,8},{8,4},{12,0},{1,13},{5,9},{9,5},{13,1},{2,14},{6,10},... | collective-permute-start | bytes 196616 | tf_op jit(solution)/shard_map/ppermute | solution.py:320
  32.4 0.0 collective-permute-done.6.refs_4_
  32.4 3.0 %collective-permute-done.7.refs_5_ = bf16[256,128]{1,0:T(8,128)(2,1)S(1)} collective-permute-done((bf16[256,128]{1,0:T(8,128)(2,1)S(1)}, bf16[256,128]{1,0:T(8,128)(2,1)S(1)}, u32[]{:S(2)}, u32[]{:S(2)}) %collective-permute-start.7) | collective-permute-done | bytes 65568 | tf_op jit(solution)/shard_map/ppermute | solution.py:320
  35.5 1.7 %collective-permute-done.8.refs_6_ = bf16[256,128]{1,0:T(8,128)(2,1)S(1)} collective-permute-done((bf16[256,128]{1,0:T(8,128)(2,1)S(1)}, bf16[256,128]{1,0:T(8,128)(2,1)S(1)}, u32[]{:S(2)}, u32[]{:S(2)}) %collective-permute-start.8) | collective-permute-done | bytes 65568 | tf_op jit(solution)/shard_map/ppermute | solution.py:320
  37.1 1.3 %merge.1 = bf16[256,1536]{1,0:T(8,128)(2,1)} custom-call(s32[2]{0:T(128)S(1)} %pad_add_fusion.refs_0_, s32[4]{0:T(128)S(1)} %copy-done.3, bf16[256,1536]{1,0:T(8,128)(2,1)} %spatial.1.refs_2_, bf16[256,128]{1,0:T(8,128)(2,1)S(1)} %get-tuple-element.35.refs_3_, bf16[256,128]{1,0:T(8,128)(2,1)S(1)} %collective-permute-done.6.refs_4_, ...), custom_call_target="tpu_custom_call", output_to_operand_aliasing={{}: (2, {})} | custom-call | bytes 524288 | tf_op jit(solution)/shard_map/merge/pallas_call | solution.py:301
  (7 shorter events, 0.0 us)
Async XLA Ops:
  0.0 14.3 %copy-start = (bf16[256,1536]{1,0:T(8,128)(2,1)S(1)}, bf16[256,1536]{1,0:T(8,128)(2,1)}, u32[]{:S(2)}) copy-start(bf16[256,1536]{1,0:T(8,128)(2,1)} %refs_3_.3) | copy-start | bytes 2359300
  0.0 3.5 %copy-start.1 = (bf16[256,1536]{1,0:T(8,128)(2,1)S(1)}, bf16[256,1536]{1,0:T(8,128)(2,1)}, u32[]{:S(2)}) copy-start(bf16[256,1536]{1,0:T(8,128)(2,1)} %refs_4_.1) | copy-start | bytes 2359300
  0.0 4.0 %copy-start.2 = (bf16[256,1536]{1,0:T(8,128)(2,1)S(1)}, bf16[256,1536]{1,0:T(8,128)(2,1)}, u32[]{:S(2)}) copy-start(bf16[256,1536]{1,0:T(8,128)(2,1)} %refs_6_.1) | copy-start | bytes 2359300
  2.9 0.6 %copy-start.5 = (bf16[256,128]{1,0:T(8,128)(2,1)}, bf16[256,128]{1,0:T(8,128)(2,1)S(1)}, u32[]{:S(2)}) copy-start(bf16[256,128]{1,0:T(8,128)(2,1)S(1)} %get-tuple-element.24) | copy-start | bytes 196612
  3.5 8.3 %collective-permute-start = (bf16[256,1536]{1,0:T(8,128)(2,1)S(1)}, bf16[256,1536]{1,0:T(8,128)(2,1)}, u32[]{:S(2)}, u32[]{:S(2)}) collective-permute-start(bf16[256,1536]{1,0:T(8,128)(2,1)S(1)} %copy-done.1), channel_id=1, source_target_pairs={{0,1},{1,0},{2,3},{3,2},{4,5},{5,4},{6,7},{7,6},{8,9},{9,8},{10,11... | collective-permute-start | bytes 2359304 | tf_op jit(solution)/shard_map/ppermute | solution.py:323
  4.0 10.3 %collective-permute-start.1 = (bf16[256,1536]{1,0:T(8,128)(2,1)S(1)}, bf16[256,1536]{1,0:T(8,128)(2,1)}, u32[]{:S(2)}, u32[]{:S(2)}) collective-permute-start(bf16[256,1536]{1,0:T(8,128)(2,1)S(1)} %copy-done.2), channel_id=1, source_target_pairs={{0,1},{1,0},{2,3},{3,2},{4,5},{5,4},{6,7},{7,6},{8,9},{9,8},{10,11... | collective-permute-start | bytes 2359304 | tf_op jit(solution)/shard_map/ppermute | solution.py:323
  4.1 21.5 %collective-permute-start.2 = (bf16[256,384]{1,0:T(8,128)(2,1)}, bf16[256,384]{1,0:T(8,128)(2,1)S(1)}, u32[]{:S(2)}, u32[]{:S(2)}) collective-permute-start(bf16[256,384]{1,0:T(8,128)(2,1)} %get-tuple-element.21), channel_id=1, source_target_pairs={{0,12},{4,8},{8,4},{12,0},{1,13},{5,9},{9,5},{13,1},{2,14},{6,10},... | collective-permute-start | bytes 589832 | tf_op jit(solution)/shard_map/ppermute | solution.py:320
  9.1 16.4 %collective-permute-start.4 = (bf16[256,384]{1,0:T(8,128)(2,1)}, bf16[256,384]{1,0:T(8,128)(2,1)S(1)}, u32[]{:S(2)}, u32[]{:S(2)}) collective-permute-start(bf16[256,384]{1,0:T(8,128)(2,1)} %get-tuple-element.23), channel_id=1, source_target_pairs={{0,4},{4,0},{8,12},{12,8},{1,5},{5,1},{9,13},{13,9},{2,6},{6,2},{1... | collective-permute-start | bytes 589832 | tf_op jit(solution)/shard_map/ppermute | solution.py:320
  9.1 16.4 %collective-permute-start.3 = (bf16[256,256]{1,0:T(8,128)(2,1)S(1)}, bf16[256,256]{1,0:T(8,128)(2,1)S(1)}, u32[]{:S(2)}, u32[]{:S(2)}) collective-permute-start(bf16[256,256]{1,0:T(8,128)(2,1)S(1)} %get-tuple-element.22), channel_id=1, source_target_pairs={{0,8},{4,12},{8,0},{12,4},{1,9},{5,13},{9,1},{13,5},{2,10},{6,14},... | collective-permute-start | bytes 393224 | tf_op jit(solution)/shard_map/ppermute | solution.py:320
  9.7 0.7 %copy-start.4 = (s32[1,4]{1,0:T(1,128)S(1)}, s32[1,4]{1,0:T(1,128)}, u32[]{:S(2)}) copy-start(s32[1,4]{1,0:T(1,128)} %sizes_ref.1) | copy-start | bytes 52
  10.9 3.3 %copy-start.3 = (s32[4]{0:T(128)S(1)}, s32[4]{0:T(128)}, u32[]{:S(2)}) copy-start(s32[4]{0:T(128)} %refs_1_.5) | copy-start | bytes 52
  11.8 14.4 %collective-permute-start.5 = (bf16[256,128]{1,0:T(8,128)(2,1)}, bf16[256,128]{1,0:T(8,128)(2,1)S(1)}, u32[]{:S(2)}, u32[]{:S(2)}) collective-permute-start(bf16[256,128]{1,0:T(8,128)(2,1)} %copy-done.5), channel_id=1, source_target_pairs={{0,8},{4,12},{8,0},{12,4},{1,9},{5,13},{9,1},{13,5},{2,10},{6,14},... | collective-permute-start | bytes 196616 | tf_op jit(solution)/shard_map/ppermute | solution.py:320
  28.0 4.5 %collective-permute-start.6 = (bf16[256,128]{1,0:T(8,128)(2,1)S(1)}, bf16[256,128]{1,0:T(8,128)(2,1)S(1)}, u32[]{:S(2)}, u32[]{:S(2)}) collective-permute-start(bf16[256,128]{1,0:T(8,128)(2,1)S(1)} %get-tuple-element.36), channel_id=1, source_target_pairs={{0,4},{4,0},{8,12},{12,8},{1,5},{5,1},{9,13},{13,9},{2,6},{6,2},{1... | collective-permute-start | bytes 196616 | tf_op jit(solution)/shard_map/ppermute | solution.py:320
  28.0 7.4 %collective-permute-start.7 = (bf16[256,128]{1,0:T(8,128)(2,1)S(1)}, bf16[256,128]{1,0:T(8,128)(2,1)S(1)}, u32[]{:S(2)}, u32[]{:S(2)}) collective-permute-start(bf16[256,128]{1,0:T(8,128)(2,1)S(1)} %temporal.4), channel_id=1, source_target_pairs={{0,8},{4,12},{8,0},{12,4},{1,9},{5,13},{9,1},{13,5},{2,10},{6,14},... | collective-permute-start | bytes 196616 | tf_op jit(solution)/shard_map/ppermute | solution.py:320
  31.1 6.1 %collective-permute-start.8 = (bf16[256,128]{1,0:T(8,128)(2,1)S(1)}, bf16[256,128]{1,0:T(8,128)(2,1)S(1)}, u32[]{:S(2)}, u32[]{:S(2)}) collective-permute-start(bf16[256,128]{1,0:T(8,128)(2,1)S(1)} %temporal.3), channel_id=1, source_target_pairs={{0,12},{4,8},{8,4},{12,0},{1,13},{5,9},{9,5},{13,1},{2,14},{6,10},... | collective-permute-start | bytes 196616 | tf_op jit(solution)/shard_map/ppermute | solution.py:320

commit v3 on v2

--- a/solution.py
+++ b/solution.py
@@ -191,47 +191,54 @@
     )(*(pltpu.with_memory_space_constraint(array, pltpu.HBM) for array in (ids, query, key_proj, value)))
 
 
-def spatial_kernel(step_heads, heads_here, where_ref, ids_ref, mask_ref, query, key_own, key_other, value_own, value_other, out):
+def spatial_kernel(first, heads_ref, mask_ref, query, key_own, key_other, value_own, value_other, *rest):
+    out = rest[-1]
     rows = query.shape[0]
     own_blocks, frame_blocks = rows // BLK, mask_ref.shape[-1]
-    rep = where_ref[1]
+    rep = lax.axis_index("rep")
     block = lax.broadcasted_iota(jnp.int32, (frame_blocks, 2 * rows), 1) // BLK
     block = lax.rem(block + rep * own_blocks, frame_blocks)
     spread = (block == lax.broadcasted_iota(jnp.int32, block.shape, 0)).astype(jnp.float32)
-    for item in range(step_heads):
-        here = pl.program_id(0) * step_heads + item
-        temporal = head_of(ids_ref, 0, heads_here) == here
-        for slot in range(1, ids_ref.shape[0]):
-            temporal |= head_of(ids_ref, slot, heads_here) == here
-
-        @pl.when(jnp.logical_not(temporal))
-        def _():
-            part = slice(item * HD, (item + 1) * HD)
-            seen = jnp.dot(mask_ref[item].astype(jnp.float32), spread, preferred_element_type=jnp.float32)
-            seen = jnp.where(rep == 0, seen[:own_blocks], seen[own_blocks:])
-            bias = jnp.where(seen > 0.5, 0.0, MASKED_SCORE)
-            bias = jnp.broadcast_to(bias[:, None, :], (own_blocks, BLK, 2 * rows)).reshape(rows, 2 * rows)
-            own = scores_of(query[:, part], key_own[:, part]) + bias[:, :rows]
-            other = scores_of(query[:, part], key_other[:, part]) + bias[:, rows:]
-            out[:, part] = attend([own, other], [value_own[:, part], value_other[:, part]])
-
-
-def spatial(where, ids, mask, query, key_own, key_other, value_own, value_other, step_heads=2):
+    mask = mask_ref[heads_ref[first + pl.program_id(0)]].astype(jnp.float32)
+    seen = jnp.dot(mask, spread, preferred_element_type=jnp.float32)
+    seen = jnp.where(rep == 0, seen[:own_blocks], seen[own_blocks:])
+    bias = jnp.where(seen > 0.5, 0.0, MASKED_SCORE)
+    bias = jnp.broadcast_to(bias[:, None, :], (own_blocks, BLK, 2 * rows)).reshape(rows, 2 * rows)
+    own = scores_of(query[...], key_own[...]) + bias[:, :rows]
+    other = scores_of(query[...], key_other[...]) + bias[:, rows:]
+    out[...] = attend([own, other], [value_own[...], value_other[...]])
+
+
+def spatial(heads, first, count, mask, query, key_own, key_other, value_own, value_other, out=None):
     rows, width = query.shape
-    heads_here, blocks = width // HD, mask.shape[-1]
-    piece = pl.BlockSpec((rows, step_heads * HD), lambda i: (0, i))
-    return pl.pallas_call(
-        lambda *refs: spatial_kernel(step_heads, heads_here, *refs),
+    piece = pl.BlockSpec((rows, HD), lambda i, heads_ref: (0, heads_ref[first + i]))
+    whole_mask = pl.BlockSpec(mask.shape, lambda i, heads_ref: (0, 0, 0))
+    given = () if out is None else (out,)
+    query, key_own, value_own = (pltpu.with_memory_space_constraint(x, pltpu.HBM) for x in (query, key_own, value_own))
+    return pl.pallas_call(
+        lambda *refs: spatial_kernel(first, *refs),
         out_shape=jax.ShapeDtypeStruct((rows, width), query.dtype),
-        grid=(heads_here // step_heads,),
-        in_specs=[SMEM, SMEM, pl.BlockSpec((step_heads, blocks, blocks), lambda i: (i, 0, 0))] + [piece] * 5,
-        out_specs=piece,
+        grid_spec=pltpu.PrefetchScalarGridSpec(
+            num_scalar_prefetch=1,
+            grid=(count,),
+            in_specs=[whole_mask] + [piece] * 5 + [ANY] * len(given),
+            out_specs=piece,
+        ),
+        input_output_aliases={7: 0} if given else {},
         name="spatial",
-        compiler_params=pltpu.CompilerParams(vmem_limit_bytes=24 << 20),
+        compiler_params=pltpu.CompilerParams(vmem_limit_bytes=16 << 20),
         cost_estimate=pl.CostEstimate(
-            flops=8 * rows * rows * width, bytes_accessed=12 * rows * width, transcendentals=2 * rows * rows * heads_here
+            flops=8 * rows * rows * HD * count, bytes_accessed=12 * rows * HD * count, transcendentals=2 * rows * rows * count
         ),
-    )(where, ids, mask, query, key_own, key_other, value_own, value_other)
+    )(heads, mask, query, key_own, key_other, value_own, value_other, *given)
+
+
+def spatial_heads(ids, heads_here):
+    head = jnp.arange(heads_here, dtype=jnp.int32)
+    kept = jnp.all(lax.rem(ids, heads_here)[None, :] != head[:, None], axis=1)
+    rank = jnp.sum((head[None, :] < head[:, None]) & kept[None, :], axis=1)
+    place = jnp.arange(heads_here - ids.shape[0], dtype=jnp.int32)
+    return jnp.sum(jnp.where(kept[None, :] & (rank[None, :] == place[:, None]), head[None, :], 0), axis=1)
 
 
 def tile_bias_kernel(sizes_ref, out):
@@ -285,36 +292,36 @@
     )(bias, *queries, *groups)
 
 
-def merge_kernel(heads_here, where_ref, ids_ref, given, *rest):
+def merge_kernel(heads_here, ids_ref, given, *rest):
     pieces, out, sems = rest[:-2], rest[-2], rest[-1]
+    frame = lax.axis_index("frames")
     copies = []
     for mask, piece in enumerate(pieces):
-        head = head_of(ids_ref, where_ref[0] ^ mask, heads_here)
+        head = head_of(ids_ref, frame ^ mask, heads_here)
         copies.append(pltpu.make_async_copy(piece, out.at[:, columns(head)], sems.at[mask]))
         copies[-1].start()
     for copy in copies:
         copy.wait()
 
 
-def merge(where, ids, out, pieces):
+def merge(ids, out, pieces):
     rows, width = out.shape
     return pl.pallas_call(
         lambda *refs: merge_kernel(width // HD, *refs),
         out_shape=jax.ShapeDtypeStruct(out.shape, out.dtype),
-        in_specs=[SMEM, SMEM, ANY] + [VMEM] * len(pieces),
+        in_specs=[SMEM, ANY] + [VMEM] * len(pieces),
         out_specs=ANY,
         scratch_shapes=[pltpu.SemaphoreType.DMA((len(pieces),))],
-        input_output_aliases={2: 0},
+        input_output_aliases={1: 0},
         name="merge",
         compiler_params=pltpu.CompilerParams(vmem_limit_bytes=4 << 20),
         cost_estimate=pl.CostEstimate(flops=0, bytes_accessed=4 * len(pieces) * rows * HD, transcendentals=0),
-    )(where, ids, out, *pieces)
+    )(ids, out, *pieces)
 
 
 def local_by_head(query, key_proj, value, block_mask, tile_sizes, temporal_ids):
     frames = lax.axis_size("frames")
     heads_here = block_mask.shape[0]
-    where = jnp.stack([lax.axis_index("frames"), lax.axis_index("rep")]).astype(jnp.int32)
 
     def exchange(array, mask):
         return lax.ppermute(array, "frames", [(i, i ^ mask) for i in range(frames)])
@@ -330,23 +337,22 @@
     keys_sent, values_sent, *_ = lax.optimization_barrier((key_proj, value, *packed))
     key_other, value_other = swap(keys_sent), swap(values_sent)
     bias = tile_bias(tile_sizes, query.shape[0])
-    out = spatial(where, temporal_ids, block_mask, query, key_proj, key_other, value, value_other)
+    heads = spatial_heads(temporal_ids, heads_here)
+    inputs = (block_mask, query, key_proj, key_other, value, value_other)
+    early = heads.shape[0] * 5 // 8
+    out = spatial(heads, 0, early, *inputs)
     *arrived, late_query = arrived
     out, *arrived = lax.optimization_barrier((out, *arrived))
     groups = [own] + arrived
     keys_at = [HD] + [HD if names == "qkv" else 0 for _, names in parts[: len(arrived)]]
-    whole = {mask: piece for piece, (mask, names) in zip(arrived, parts) if names == "qkv"}
+    turns = [(mask, piece) for piece, (mask, names) in zip(arrived, parts) if names == "qkv"]
+    turns = turns + [(last, late_query), (0, own)]
     returned = {}
-    (first,) = temporal(bias, [whole.pop(near[0])], groups, keys_at)
-    returned[near[0]] = exchange(first, near[0])
-    late_query, _ = lax.optimization_barrier((late_query, first))
-    (second,) = temporal(bias, [late_query], groups, keys_at)
-    returned[last] = exchange(second, last)
-    own_query, *others, _ = lax.optimization_barrier((own, *whole.values(), second))
-    mine, *rest = temporal(bias, [own_query, *others], groups, keys_at)
-    for mask, piece in zip(whole, rest):
-        returned[mask] = exchange(piece, mask)
-    return merge(where, temporal_ids, out, [mine] + [returned[mask] for mask in range(1, frames)])
+    for mask, rows in turns:
+        (done,) = temporal(bias, [rows], groups, keys_at)
+        returned[mask] = exchange(done, mask) if mask else done
+    out = spatial(heads, early, heads.shape[0] - early, *inputs, out)
+    return merge(temporal_ids, out, [returned[mask] for mask in range(frames)])
 
 
 def local(query, key_proj, value, block_mask, tile_sizes, temporal_ids):

time: 38.7 us -> 37.2 us (0.961)
  waiting for transfers between devices: 9.65 us -> 6.71 us
  Pallas kernels: 13.5 us -> 16 us
  local copies, waits for them, and re-layouts: 2.09 us -> 0.26 us
    pallas_call x1 -> x2, Pallas kernels: 6.4 us -> 9.53 us  [spatial(): pl.pallas_call(lambda *refs: spatial_kernel(first, *refs), out_shape=jax....]
    ppermute x7, waiting for transfers between devices: 9.65 us -> 6.71 us  [exchange(): return lax.ppermute(array, 'frames', [(i, i ^ mask) for i in range(frames)])]
    unnamed x13 -> x9, local copies, waits for them, and re-layouts: 2.09 us -> 0.26 us
    pallas_call x1, Pallas kernels: 2.85 us -> 2.1 us  [pack(): pl.pallas_call(lambda *refs: pack_kernel(heads_here, parts, *refs), out_s...]
    pallas_call x3 -> x4, Pallas kernels: 2.35 us -> 2.49 us  [temporal(): pl.pallas_call(lambda *refs: temporal_kernel(keys_at, len(queries), *refs...]
  transfers between devices with their start and end apart: 9 -> 9, of which waited for: 4 -> 1; matrix products, arithmetic and copies ran while one was open for 2% -> 1% of each run, Pallas kernels for 20% -> 35%
where the time goes in v3:
time: 37.2 us; the launch traced here: 36.6 us
  Pallas kernels  16 us (43%)
  starting transfers between devices  13.2 us (35%)
  waiting for transfers between devices  6.71 us (18%)
    ppermute x7, starting transfers between devices, exchange(): return lax.ppermute(array, 'frames', [(i, i ^ mask) for i in range(frames)])  12.5 us
    pallas_call x2, Pallas kernels, spatial(): pl.pallas_call(lambda *refs: spatial_kernel(first, *refs), out_shape=jax....  9.53 us
    ppermute x7, waiting for transfers between devices, exchange(): return lax.ppermute(array, 'frames', [(i, i ^ mask) for i in range(frames)])  6.71 us
    pallas_call x4, Pallas kernels, temporal(): pl.pallas_call(lambda *refs: temporal_kernel(keys_at, len(queries), *refs...  2.49 us
    pallas_call x1, Pallas kernels, pack(): pl.pallas_call(lambda *refs: pack_kernel(heads_here, parts, *refs), out_s...  2.1 us
    pallas_call x1, Pallas kernels, merge(): pl.pallas_call(lambda *refs: merge_kernel(width // HD, *refs), out_shape=...  1.29 us
  transfers between devices with their start and end apart: 9, of which 1 were waited for; matrix products, arithmetic and copies ran while one was open for 1% of the time, Pallas kernels for 35%

profile of v3, /device:TPU:0, one launch (start us, length us, event | category | flops | bytes accessed | tf_op | source)
XLA Modules:
  0.0 36.6 jit_solution(11363108630693097272)
XLA Ops:
  0.0 2.1 %pack.1 = (bf16[256,384]{1,0:T(8,128)(2,1)S(1)}, bf16[256,256]{1,0:T(8,128)(2,1)S(1)}, bf16[256,384]{1,0:T(8,128)(2,1)S(1)}, bf16[256,128]{1,0:T(8,128)(2,1)S(1)}, bf16[256,384]{1,0:T(8,128)(2,1)S(1)}) custom-call(s32[4]{0:T(128)} %refs_0_.3, bf16[256,1536]{1,0:T(8,128)(2,1)} %refs_2_.5, bf16[256,1536]{1,0:T(8,128)(2,1)} %refs_3_.5, bf16[256,1536]{1,0:T(8,128)(2,1)} %refs_5_.3), custom_call_target="tpu_custom_call" | custom-call | bytes 1572864 | tf_op jit(solution)/shard_map/pack/pallas_call | solution.py:182
  2.1 0.0 copy-start
  2.1 0.6 %collective-permute-start = (bf16[256,1536]{1,0:T(8,128)(2,1)S(1)}, bf16[256,1536]{1,0:T(8,128)(2,1)S(1)}, u32[]{:S(2)}, u32[]{:S(2)}) collective-permute-start(bf16[256,1536]{1,0:T(8,128)(2,1)S(1)} %copy-done.2), channel_id=1, source_target_pairs={{0,1},{1,0},{2,3},{3,2},{4,5},{5,4},{6,7},{7,6},{8,9},{9,8},{10,11... | collective-permute-start | bytes 2359304 | tf_op jit(solution)/shard_map/ppermute | solution.py:330
  2.7 0.1 collective-permute-start.1
  2.8 5.0 %collective-permute-start.2 = (bf16[256,384]{1,0:T(8,128)(2,1)S(1)}, bf16[256,384]{1,0:T(8,128)(2,1)S(1)}, u32[]{:S(2)}, u32[]{:S(2)}) collective-permute-start(bf16[256,384]{1,0:T(8,128)(2,1)S(1)} %get-tuple-element.16), channel_id=1, source_target_pairs={{0,12},{4,8},{8,4},{12,0},{1,13},{5,9},{9,5},{13,1},{2,14},{6,10},... | collective-permute-start | bytes 589832 | tf_op jit(solution)/shard_map/ppermute | solution.py:327
  7.8 0.0 collective-permute-start.4
  7.8 0.6 %collective-permute-start.3 = (bf16[256,256]{1,0:T(8,128)(2,1)S(1)}, bf16[256,256]{1,0:T(8,128)(2,1)S(1)}, u32[]{:S(2)}, u32[]{:S(2)}) collective-permute-start(bf16[256,256]{1,0:T(8,128)(2,1)S(1)} %get-tuple-element.17), channel_id=1, source_target_pairs={{0,8},{4,12},{8,0},{12,4},{1,9},{5,13},{9,1},{13,5},{2,10},{6,14},... | collective-permute-start | bytes 393224 | tf_op jit(solution)/shard_map/ppermute | solution.py:327
  8.4 0.1 fusion.2
  8.5 0.1 convert_reduce_fusion
  8.6 0.0 collective-permute-done.refs_4_
  8.6 2.4 %collective-permute-start.6 = (bf16[256,128]{1,0:T(8,128)(2,1)S(1)}, bf16[256,128]{1,0:T(8,128)(2,1)S(1)}, u32[]{:S(2)}, u32[]{:S(2)}) collective-permute-start(bf16[256,128]{1,0:T(8,128)(2,1)S(1)} %get-tuple-element.19), channel_id=1, source_target_pairs={{0,8},{4,12},{8,0},{12,4},{1,9},{5,13},{9,1},{13,5},{2,10},{6,14},... | collective-permute-start | bytes 196616 | tf_op jit(solution)/shard_map/ppermute | solution.py:327
  11.0 0.1 select_reduce_fusion.refs_0_
  11.1 0.0 copy-start.3
  11.1 0.6 %tile_bias.1.refs_0_ = f32[256,256]{1,0:T(8,128)S(1)} custom-call(s32[1,4]{1,0:T(1,128)S(1)} %copy-done.1), custom_call_target="tpu_custom_call" | custom-call | flops 65536 | bytes 262144 | tf_op jit(solution)/shard_map/tile_bias/pallas_call | solution.py:257
  11.8 0.1 copy-done.3
  11.9 0.1 copy.12.refs_1_
  12.0 5.5 %spatial.2.refs_7_ = bf16[256,1536]{1,0:T(8,128)(2,1)} custom-call(s32[8]{0:T(128)S(1)} %select_reduce_fusion.refs_0_, s32[12,8,8]{2,1,0:T(8,128)S(1)} %copy.12.refs_1_, bf16[256,1536]{1,0:T(8,128)(2,1)} %refs_2_.5, bf16[256,1536]{1,0:T(8,128)(2,1)} %refs_3_.5, bf16[256,1536]{1,0:T(8,128)(2,1)S(1)} %collective-permute-done.refs_4_, ...), custom_call_target="tpu_custom_call" | custom-call | flops 335544320 | bytes 1966080 | tf_op jit(solution)/shard_map/spatial/pallas_call | solution.py:218
  17.5 6.7 %collective-permute-done.3.refs_4_ = bf16[256,256]{1,0:T(8,128)(2,1)S(1)} collective-permute-done((bf16[256,256]{1,0:T(8,128)(2,1)S(1)}, bf16[256,256]{1,0:T(8,128)(2,1)S(1)}, u32[]{:S(2)}, u32[]{:S(2)}) %collective-permute-start.3) | collective-permute-done | bytes 131104 | tf_op jit(solution)/shard_map/ppermute | solution.py:327
  24.2 0.0 collective-permute-done.2.refs_3_.refs_1_
  24.2 0.0 collective-permute-done.4.refs_5_.refs_1_
  24.2 0.6 %temporal.7 = bf16[256,128]{1,0:T(8,128)(2,1)S(1)} custom-call(f32[256,256]{1,0:T(8,128)S(1)} %tile_bias.1.refs_0_, bf16[256,384]{1,0:T(8,128)(2,1)S(1)} %collective-permute-done.2.refs_3_.refs_1_, bf16[256,384]{1,0:T(8,128)(2,1)S(1)} %get-tuple-element.20.refs_1_.refs_2_, bf16[256,384]{1,0:T(8,128)(2,1)S(1)} %collective-permute-done.2.refs_3_.refs_1_, ...), custom_call_target="tpu_custom_call" | custom-call | flops 134217728 | bytes 655360 | tf_op jit(solution)/shard_map/temporal/pallas_call | solution.py:282
  24.8 2.6 %collective-permute-start.8 = (bf16[256,128]{1,0:T(8,128)(2,1)S(1)}, bf16[256,128]{1,0:T(8,128)(2,1)S(1)}, u32[]{:S(2)}, u32[]{:S(2)}) collective-permute-start(bf16[256,128]{1,0:T(8,128)(2,1)S(1)} %temporal.7), channel_id=1, source_target_pairs={{0,12},{4,8},{8,4},{12,0},{1,13},{5,9},{9,5},{13,1},{2,14},{6,10},... | collective-permute-start | bytes 196616 | tf_op jit(solution)/shard_map/ppermute | solution.py:327
  27.4 0.6 %temporal.5 = bf16[256,128]{1,0:T(8,128)(2,1)S(1)} custom-call(f32[256,256]{1,0:T(8,128)S(1)} %tile_bias.1.refs_0_, bf16[256,384]{1,0:T(8,128)(2,1)S(1)} %collective-permute-done.4.refs_5_.refs_1_, bf16[256,384]{1,0:T(8,128)(2,1)S(1)} %get-tuple-element.20.refs_1_.refs_2_, bf16[256,384]{1,0:T(8,128)(2,1)S(1)} %collective-permute-done.2.refs_3_.refs_1_, ...), custom_call_target="tpu_custom_call" | custom-call | flops 134217728 | bytes 655360 | tf_op jit(solution)/shard_map/temporal/pallas_call | solution.py:282
  28.0 0.0 collective-permute-done.6.refs_1_
  28.0 0.6 %temporal.6 = bf16[256,128]{1,0:T(8,128)(2,1)S(1)} custom-call(f32[256,256]{1,0:T(8,128)S(1)} %tile_bias.1.refs_0_, bf16[256,128]{1,0:T(8,128)(2,1)S(1)} %collective-permute-done.6.refs_1_, bf16[256,384]{1,0:T(8,128)(2,1)S(1)} %get-tuple-element.20.refs_1_.refs_2_, bf16[256,384]{1,0:T(8,128)(2,1)S(1)} %collective-permute-done.2.refs_3_.refs_1_, ...), custom_call_target="tpu_custom_call" | custom-call | flops 134217728 | bytes 655360 | tf_op jit(solution)/shard_map/temporal/pallas_call | solution.py:282
  28.6 0.1 collective-permute-start.7
  28.7 1.9 %collective-permute-start.5 = (bf16[256,128]{1,0:T(8,128)(2,1)S(1)}, bf16[256,128]{1,0:T(8,128)(2,1)S(1)}, u32[]{:S(2)}, u32[]{:S(2)}) collective-permute-start(bf16[256,128]{1,0:T(8,128)(2,1)S(1)} %temporal.5), channel_id=1, source_target_pairs={{0,4},{4,0},{8,12},{12,8},{1,5},{5,1},{9,13},{13,9},{2,6},{6,2},{1... | collective-permute-start | bytes 196616 | tf_op jit(solution)/shard_map/ppermute | solution.py:327
  30.6 0.6 %temporal.4.refs_2_ = bf16[256,128]{1,0:T(8,128)(2,1)S(1)} custom-call(f32[256,256]{1,0:T(8,128)S(1)} %tile_bias.1.refs_0_, bf16[256,384]{1,0:T(8,128)(2,1)S(1)} %get-tuple-element.20.refs_1_.refs_2_, bf16[256,384]{1,0:T(8,128)(2,1)S(1)} %get-tuple-element.20.refs_1_.refs_2_, bf16[256,384]{1,0:T(8,128)(2,1)S(1)} %collective-permute-done.2.refs_3_.refs_1_, ...), custom_call_target="tpu_custom_call" | custom-call | flops 134217728 | bytes 655360 | tf_op jit(solution)/shard_map/temporal/pallas_call | solution.py:282
  31.2 4.0 %spatial.3.refs_1_ = bf16[256,1536]{1,0:T(8,128)(2,1)} custom-call(s32[8]{0:T(128)S(1)} %select_reduce_fusion.refs_0_, s32[12,8,8]{2,1,0:T(8,128)S(1)} %copy.12.refs_1_, bf16[256,1536]{1,0:T(8,128)(2,1)} %refs_2_.5, bf16[256,1536]{1,0:T(8,128)(2,1)} %refs_3_.5, bf16[256,1536]{1,0:T(8,128)(2,1)S(1)} %collective-permute-done.refs_4_, ...), custom_call_target="tpu_custom_call", output_to_operand_aliasing={{}: (7, {})} | custom-call | flops 201326592 | bytes 1179648 | tf_op jit(solution)/shard_map/spatial/pallas_call | solution.py:218
  35.3 0.0 collective-permute-done.7.refs_4_
  35.3 0.0 collective-permute-done.5.refs_3_
  35.3 1.3 %merge.1 = bf16[256,1536]{1,0:T(8,128)(2,1)} custom-call(s32[4]{0:T(128)S(1)} %copy-done, bf16[256,1536]{1,0:T(8,128)(2,1)} %spatial.3.refs_1_, bf16[256,128]{1,0:T(8,128)(2,1)S(1)} %temporal.4.refs_2_, bf16[256,128]{1,0:T(8,128)(2,1)S(1)} %collective-permute-done.5.refs_3_, ...), custom_call_target="tpu_custom_call", output_to_operand_aliasing={{}: (1, {})} | custom-call | bytes 524288 | tf_op jit(solution)/shard_map/merge/pallas_call | solution.py:309
  (8 shorter events, 0.0 us)
Async XLA Ops:
  0.0 2.1 %copy-start.2 = (bf16[256,1536]{1,0:T(8,128)(2,1)S(1)}, bf16[256,1536]{1,0:T(8,128)(2,1)}, u32[]{:S(2)}) copy-start(bf16[256,1536]{1,0:T(8,128)(2,1)} %refs_3_.5) | copy-start | bytes 2359300
  2.1 6.2 %copy-start = (s32[4]{0:T(128)S(1)}, s32[4]{0:T(128)}, u32[]{:S(2)}) copy-start(s32[4]{0:T(128)} %refs_0_.3) | copy-start | bytes 52
  2.1 6.5 %collective-permute-start = (bf16[256,1536]{1,0:T(8,128)(2,1)S(1)}, bf16[256,1536]{1,0:T(8,128)(2,1)S(1)}, u32[]{:S(2)}, u32[]{:S(2)}) collective-permute-start(bf16[256,1536]{1,0:T(8,128)(2,1)S(1)} %copy-done.2), channel_id=1, source_target_pairs={{0,1},{1,0},{2,3},{3,2},{4,5},{5,4},{6,7},{7,6},{8,9},{9,8},{10,11... | collective-permute-start | bytes 2359304 | tf_op jit(solution)/shard_map/ppermute | solution.py:330
  2.7 9.3 %collective-permute-start.1 = (bf16[256,1536]{1,0:T(8,128)(2,1)}, bf16[256,1536]{1,0:T(8,128)(2,1)S(1)}, u32[]{:S(2)}, u32[]{:S(2)}) collective-permute-start(bf16[256,1536]{1,0:T(8,128)(2,1)} %refs_5_.3), channel_id=1, source_target_pairs={{0,1},{1,0},{2,3},{3,2},{4,5},{5,4},{6,7},{7,6},{8,9},{9,8},{10,11... | collective-permute-start | bytes 2359304 | tf_op jit(solution)/shard_map/ppermute | solution.py:330
  2.8 21.4 %collective-permute-start.2 = (bf16[256,384]{1,0:T(8,128)(2,1)S(1)}, bf16[256,384]{1,0:T(8,128)(2,1)S(1)}, u32[]{:S(2)}, u32[]{:S(2)}) collective-permute-start(bf16[256,384]{1,0:T(8,128)(2,1)S(1)} %get-tuple-element.16), channel_id=1, source_target_pairs={{0,12},{4,8},{8,4},{12,0},{1,13},{5,9},{9,5},{13,1},{2,14},{6,10},... | collective-permute-start | bytes 589832 | tf_op jit(solution)/shard_map/ppermute | solution.py:327
  7.8 16.4 %collective-permute-start.4 = (bf16[256,384]{1,0:T(8,128)(2,1)S(1)}, bf16[256,384]{1,0:T(8,128)(2,1)S(1)}, u32[]{:S(2)}, u32[]{:S(2)}) collective-permute-start(bf16[256,384]{1,0:T(8,128)(2,1)S(1)} %get-tuple-element.18), channel_id=1, source_target_pairs={{0,4},{4,0},{8,12},{12,8},{1,5},{5,1},{9,13},{13,9},{2,6},{6,2},{1... | collective-permute-start | bytes 589832 | tf_op jit(solution)/shard_map/ppermute | solution.py:327
  7.8 16.4 %collective-permute-start.3 = (bf16[256,256]{1,0:T(8,128)(2,1)S(1)}, bf16[256,256]{1,0:T(8,128)(2,1)S(1)}, u32[]{:S(2)}, u32[]{:S(2)}) collective-permute-start(bf16[256,256]{1,0:T(8,128)(2,1)S(1)} %get-tuple-element.17), channel_id=1, source_target_pairs={{0,8},{4,12},{8,0},{12,4},{1,9},{5,13},{9,1},{13,5},{2,10},{6,14},... | collective-permute-start | bytes 393224 | tf_op jit(solution)/shard_map/ppermute | solution.py:327
  8.6 2.6 %copy-start.1 = (s32[1,4]{1,0:T(1,128)S(1)}, s32[1,4]{1,0:T(1,128)}, u32[]{:S(2)}) copy-start(s32[1,4]{1,0:T(1,128)} %sizes_ref.1) | copy-start | bytes 52
  8.6 19.4 %collective-permute-start.6 = (bf16[256,128]{1,0:T(8,128)(2,1)S(1)}, bf16[256,128]{1,0:T(8,128)(2,1)S(1)}, u32[]{:S(2)}, u32[]{:S(2)}) collective-permute-start(bf16[256,128]{1,0:T(8,128)(2,1)S(1)} %get-tuple-element.19), channel_id=1, source_target_pairs={{0,8},{4,12},{8,0},{12,4},{1,9},{5,13},{9,1},{13,5},{2,10},{6,14},... | collective-permute-start | bytes 196616 | tf_op jit(solution)/shard_map/ppermute | solution.py:327
  11.1 0.8 %copy-start.3 = (s32[12,8,8]{0,2,1:T(8,128)S(1)}, s32[12,8,8]{0,2,1:T(8,128)}, u32[]{:S(2)}) copy-start(s32[12,8,8]{0,2,1:T(8,128)} %param.9) | copy-start | bytes 9220
  24.8 10.5 %collective-permute-start.8 = (bf16[256,128]{1,0:T(8,128)(2,1)S(1)}, bf16[256,128]{1,0:T(8,128)(2,1)S(1)}, u32[]{:S(2)}, u32[]{:S(2)}) collective-permute-start(bf16[256,128]{1,0:T(8,128)(2,1)S(1)} %temporal.7), channel_id=1, source_target_pairs={{0,12},{4,8},{8,4},{12,0},{1,13},{5,9},{9,5},{13,1},{2,14},{6,10},... | collective-permute-start | bytes 196616 | tf_op jit(solution)/shard_map/ppermute | solution.py:327
  28.6 6.6 %collective-permute-start.7 = (bf16[256,128]{1,0:T(8,128)(2,1)S(1)}, bf16[256,128]{1,0:T(8,128)(2,1)S(1)}, u32[]{:S(2)}, u32[]{:S(2)}) collective-permute-start(bf16[256,128]{1,0:T(8,128)(2,1)S(1)} %temporal.6), channel_id=1, source_target_pairs={{0,8},{4,12},{8,0},{12,4},{1,9},{5,13},{9,1},{13,5},{2,10},{6,14},... | collective-permute-start | bytes 196616 | tf_op jit(solution)/shard_map/ppermute | solution.py:327
  28.7 6.6 %collective-permute-start.5 = (bf16[256,128]{1,0:T(8,128)(2,1)S(1)}, bf16[256,128]{1,0:T(8,128)(2,1)S(1)}, u32[]{:S(2)}, u32[]{:S(2)}) collective-permute-start(bf16[256,128]{1,0:T(8,128)(2,1)S(1)} %temporal.5), channel_id=1, source_target_pairs={{0,4},{4,0},{8,12},{12,8},{1,5},{5,1},{9,13},{13,9},{2,6},{6,2},{1... | collective-permute-start | bytes 196616 | tf_op jit(solution)/shard_map/ppermute | solution.py:327

commit v4 on v3

--- a/solution.py
+++ b/solution.py
@@ -134,15 +134,18 @@
 
 
 def attend(scores, values):
-    highest = scores[0].max(axis=-1, keepdims=True)
+    highest = scores[0]
     for more in scores[1:]:
-        highest = jnp.maximum(highest, more.max(axis=-1, keepdims=True))
-    total, out = 0.0, 0.0
-    for group, group_values in zip(scores, values):
-        raised = jnp.exp2((group - highest) * EXP2_SCALE)
-        total = total + raised.sum(axis=-1, keepdims=True)
-        out = out + jnp.dot(raised.astype(jnp.bfloat16), group_values, preferred_element_type=jnp.float32)
-    return (out / total).astype(jnp.bfloat16)
+        highest = jnp.maximum(highest, more)
+    highest = highest.max(axis=-1, keepdims=True)
+    raised = [jnp.exp2((group - highest) * EXP2_SCALE) for group in scores]
+    total = raised[0]
+    for more in raised[1:]:
+        total = total + more
+    out = jnp.dot(raised[0].astype(jnp.bfloat16), values[0], preferred_element_type=jnp.float32)
+    for weights, group_values in zip(raised[1:], values[1:]):
+        out = out + jnp.dot(weights.astype(jnp.bfloat16), group_values, preferred_element_type=jnp.float32)
+    return (out / total.sum(axis=-1, keepdims=True)).astype(jnp.bfloat16)
 
 
 def columns(index):
@@ -191,46 +194,69 @@
     )(*(pltpu.with_memory_space_constraint(array, pltpu.HBM) for array in (ids, query, key_proj, value)))
 
 
-def spatial_kernel(first, heads_ref, mask_ref, query, key_own, key_other, value_own, value_other, *rest):
-    out = rest[-1]
-    rows = query.shape[0]
+def spatial_kernel(heads_ref, mask_ref, query, key_own, key_other, value_own, value_other, out, seen_ref, fetched, stage, arrive, leave):
+    rows, count = query.shape[0], heads_ref.shape[0]
     own_blocks, frame_blocks = rows // BLK, mask_ref.shape[-1]
+    coming, going = [], []
+    for item in range(count):
+        coming.append(
+            [
+                pltpu.make_async_copy(
+                    source.at[:, columns(heads_ref[item])], fetched.at[item, :, i * HD : (i + 1) * HD], arrive.at[item, i]
+                )
+                for i, source in enumerate((query, key_own, value_own))
+            ]
+        )
+        for copy in coming[-1]:
+            copy.start()
     rep = lax.axis_index("rep")
     block = lax.broadcasted_iota(jnp.int32, (frame_blocks, 2 * rows), 1) // BLK
     block = lax.rem(block + rep * own_blocks, frame_blocks)
     spread = (block == lax.broadcasted_iota(jnp.int32, block.shape, 0)).astype(jnp.float32)
-    mask = mask_ref[heads_ref[first + pl.program_id(0)]].astype(jnp.float32)
-    seen = jnp.dot(mask, spread, preferred_element_type=jnp.float32)
-    seen = jnp.where(rep == 0, seen[:own_blocks], seen[own_blocks:])
-    bias = jnp.where(seen > 0.5, 0.0, MASKED_SCORE)
-    bias = jnp.broadcast_to(bias[:, None, :], (own_blocks, BLK, 2 * rows)).reshape(rows, 2 * rows)
-    own = scores_of(query[...], key_own[...]) + bias[:, :rows]
-    other = scores_of(query[...], key_other[...]) + bias[:, rows:]
-    out[...] = attend([own, other], [value_own[...], value_other[...]])
-
-
-def spatial(heads, first, count, mask, query, key_own, key_other, value_own, value_other, out=None):
+    seen_ref[...] = jnp.dot(mask_ref[...].astype(jnp.float32), spread, preferred_element_type=jnp.float32)
+    for copies in coming:
+        for copy in copies:
+            copy.wait()
+    for item in range(count):
+        head = heads_ref[item]
+        seen = seen_ref[pl.ds(pl.multiple_of(head * frame_blocks, frame_blocks), frame_blocks), :]
+        seen = jnp.where(rep == 0, seen[:own_blocks], seen[own_blocks:])
+        bias = jnp.where(seen > 0.5, 0.0, MASKED_SCORE)
+        bias = jnp.broadcast_to(bias[:, None, :], (own_blocks, BLK, 2 * rows)).reshape(rows, 2 * rows)
+        asked = fetched[item, :, :HD]
+        own = scores_of(asked, fetched[item, :, HD : 2 * HD]) + bias[:, :rows]
+        other = scores_of(asked, key_other[:, columns(head)]) + bias[:, rows:]
+        stage[item] = attend([own, other], [fetched[item, :, 2 * HD :], value_other[:, columns(head)]])
+        if (item + 1) % 4 == 0 or item + 1 == count:
+            for sent in range(len(going), item + 1):
+                going.append(pltpu.make_async_copy(stage.at[sent], out.at[:, columns(heads_ref[sent])], leave.at[sent]))
+                going[-1].start()
+    for copy in going:
+        copy.wait()
+
+
+def spatial(heads, mask, query, key_own, key_other, value_own, value_other):
     rows, width = query.shape
-    piece = pl.BlockSpec((rows, HD), lambda i, heads_ref: (0, heads_ref[first + i]))
-    whole_mask = pl.BlockSpec(mask.shape, lambda i, heads_ref: (0, 0, 0))
-    given = () if out is None else (out,)
+    count, blocks = heads.shape[0], mask.shape[-1]
     query, key_own, value_own = (pltpu.with_memory_space_constraint(x, pltpu.HBM) for x in (query, key_own, value_own))
     return pl.pallas_call(
-        lambda *refs: spatial_kernel(first, *refs),
+        spatial_kernel,
         out_shape=jax.ShapeDtypeStruct((rows, width), query.dtype),
-        grid_spec=pltpu.PrefetchScalarGridSpec(
-            num_scalar_prefetch=1,
-            grid=(count,),
-            in_specs=[whole_mask] + [piece] * 5 + [ANY] * len(given),
-            out_specs=piece,
-        ),
-        input_output_aliases={7: 0} if given else {},
+        in_specs=[SMEM, VMEM, HBM, HBM, VMEM, HBM, VMEM],
+        out_specs=HBM,
+        scratch_shapes=[
+            pltpu.VMEM((mask.shape[0] * blocks, 2 * rows), jnp.float32),
+            pltpu.VMEM((count, rows, 3 * HD), query.dtype),
+            pltpu.VMEM((count, rows, HD), query.dtype),
+            pltpu.SemaphoreType.DMA((count, 3)),
+            pltpu.SemaphoreType.DMA((count,)),
+        ],
         name="spatial",
         compiler_params=pltpu.CompilerParams(vmem_limit_bytes=16 << 20),
         cost_estimate=pl.CostEstimate(
             flops=8 * rows * rows * HD * count, bytes_accessed=12 * rows * HD * count, transcendentals=2 * rows * rows * count
         ),
-    )(heads, mask, query, key_own, key_other, value_own, value_other, *given)
+    )(heads, mask.reshape(-1, blocks), query, key_own, key_other, value_own, value_other)
 
 
 def spatial_heads(ids, heads_here):
@@ -329,8 +355,9 @@
     def swap(array):
         return lax.ppermute(array, "rep", [(0, 1), (1, 0)])
 
-    *near, last = sorted(range(1, frames), key=lambda mask: (mask % 2 == 0, -mask))
-    parts = [(m, "qkv") for m in near[:1]] + [(last, "kv")] + [(m, "qkv") for m in near[1:]] + [(last, "q"), (0, "qkv")]
+    first, last = frames - 1, frames // 2
+    near = [m for m in range(1, first) if m != last]
+    parts = [(first, "qkv"), (last, "kv")] + [(m, "qkv") for m in near] + [(last, "q"), (0, "qkv")]
     packed = pack(temporal_ids, query, key_proj, value, parts, heads_here)
     *travelling, own = packed
     arrived = [exchange(piece, mask) for piece, (mask, _) in zip(travelling, parts)]
@@ -338,20 +365,21 @@
     key_other, value_other = swap(keys_sent), swap(values_sent)
     bias = tile_bias(tile_sizes, query.shape[0])
     heads = spatial_heads(temporal_ids, heads_here)
-    inputs = (block_mask, query, key_proj, key_other, value, value_other)
-    early = heads.shape[0] * 5 // 8
-    out = spatial(heads, 0, early, *inputs)
+    bias, *inputs = lax.optimization_barrier((bias, key_other, value_other))
+    out = spatial(heads, block_mask, query, key_proj, inputs[0], value, inputs[1])
     *arrived, late_query = arrived
     out, *arrived = lax.optimization_barrier((out, *arrived))
     groups = [own] + arrived
     keys_at = [HD] + [HD if names == "qkv" else 0 for _, names in parts[: len(arrived)]]
     turns = [(mask, piece) for piece, (mask, names) in zip(arrived, parts) if names == "qkv"]
-    turns = turns + [(last, late_query), (0, own)]
-    returned = {}
-    for mask, rows in turns:
-        (done,) = temporal(bias, [rows], groups, keys_at)
-        returned[mask] = exchange(done, mask) if mask else done
-    out = spatial(heads, early, heads.shape[0] - early, *inputs, out)
+    turns = turns[:1] + [(last, late_query)] + turns[1:] + [(0, own)]
+    order = turns[:1] + turns[2:-1] + turns[1:2] + turns[-1:]
+    attended = {}
+    for mask, rows in order:
+        (attended[mask],) = temporal(bias, [rows], groups, keys_at)
+    returned = {0: attended[0]}
+    for mask, _ in turns[:-1]:
+        returned[mask] = exchange(attended[mask], mask)
     return merge(temporal_ids, out, [returned[mask] for mask in range(frames)])
 
 

time: 37.2 us -> 36.2 us (0.973)
  Pallas kernels: 16 us -> 12 us
  starting transfers between devices: 13.2 us -> 16.4 us
  local copies, waits for them, and re-layouts: 0.26 us -> 0.79 us
  waiting for transfers between devices: 6.71 us -> 6.22 us
    pallas_call x2 -> x1, Pallas kernels: 9.53 us -> 5.56 us  [spatial(): pl.pallas_call(spatial_kernel, out_shape=jax.ShapeDtypeStruct((rows, widt...]
    ppermute x7, starting transfers between devices: 12.5 us -> 15.7 us  [exchange(): return lax.ppermute(array, 'frames', [(i, i ^ mask) for i in range(frames)])]
    unnamed x9 -> x7, local copies, waits for them, and re-layouts: 0.26 us -> 0.79 us
    ppermute x7, waiting for transfers between devices: 6.71 us -> 6.22 us  [exchange(): return lax.ppermute(array, 'frames', [(i, i ^ mask) for i in range(frames)])]
  transfers between devices with their start and end apart: 9 -> 9, of which waited for: 1 -> 3; matrix products, arithmetic and copies ran while one was open for 1% -> 1% of each run, Pallas kernels for 35% -> 24%
where the time goes in v4:
time: 36.2 us; the launch traced here: 35.9 us
  starting transfers between devices  16.4 us (45%)
  Pallas kernels  12 us (33%)
  waiting for transfers between devices  6.22 us (17%)
  local copies, waits for them, and re-layouts  0.79 us (2%)
    ppermute x7, starting transfers between devices, exchange(): return lax.ppermute(array, 'frames', [(i, i ^ mask) for i in range(frames)])  15.7 us
    ppermute x7, waiting for transfers between devices, exchange(): return lax.ppermute(array, 'frames', [(i, i ^ mask) for i in range(frames)])  6.22 us
    pallas_call x1, Pallas kernels, spatial(): pl.pallas_call(spatial_kernel, out_shape=jax.ShapeDtypeStruct((rows, widt...  5.56 us
    pallas_call x4, Pallas kernels, temporal(): pl.pallas_call(lambda *refs: temporal_kernel(keys_at, len(queries), *refs...  2.6 us
    pallas_call x1, Pallas kernels, pack(): pl.pallas_call(lambda *refs: pack_kernel(heads_here, parts, *refs), out_s...  1.97 us
    pallas_call x1, Pallas kernels, merge(): pl.pallas_call(lambda *refs: merge_kernel(width // HD, *refs), out_shape=...  1.29 us
    unnamed x7, local copies, waits for them, and re-layouts  0.79 us
  transfers between devices with their start and end apart: 9, of which 3 were waited for; matrix products, arithmetic and copies ran while one was open for 1% of the time, Pallas kernels for 24%

profile of v4, /device:TPU:0, one launch (start us, length us, event | category | flops | bytes accessed | tf_op | source)
XLA Modules:
  0.0 35.9 jit_solution(5010702614620699573)
XLA Ops:
  0.0 2.0 %pack.1 = (bf16[256,384]{1,0:T(8,128)(2,1)S(1)}, bf16[256,256]{1,0:T(8,128)(2,1)S(1)}, bf16[256,384]{1,0:T(8,128)(2,1)S(1)}, bf16[256,128]{1,0:T(8,128)(2,1)S(1)}, bf16[256,384]{1,0:T(8,128)(2,1)S(1)}) custom-call(s32[4]{0:T(128)} %refs_0_.3, bf16[256,1536]{1,0:T(8,128)(2,1)} %query.1, bf16[256,1536]{1,0:T(8,128)(2,1)} %key_own.1, bf16[256,1536]{1,0:T(8,128)(2,1)} %value_own.1), custom_call_target="tpu_custom_call" | custom-call | bytes 1572864 | tf_op jit(solution)/shard_map/pack/pallas_call | solution.py:185
  2.0 0.0 copy-start
  2.0 0.6 %collective-permute-start = (bf16[256,1536]{1,0:T(8,128)(2,1)}, bf16[256,1536]{1,0:T(8,128)(2,1)S(1)}, u32[]{:S(2)}, u32[]{:S(2)}) collective-permute-start(bf16[256,1536]{1,0:T(8,128)(2,1)} %key_own.1), channel_id=1, source_target_pairs={{0,1},{1,0},{2,3},{3,2},{4,5},{5,4},{6,7},{7,6},{8,9},{9,8},{10,11... | collective-permute-start | bytes 2359304 | tf_op jit(solution)/shard_map/ppermute | solution.py:356
  2.5 0.1 collective-permute-start.1
  2.6 4.0 %collective-permute-start.3 = (bf16[256,256]{1,0:T(8,128)(2,1)S(1)}, bf16[256,256]{1,0:T(8,128)(2,1)S(1)}, u32[]{:S(2)}, u32[]{:S(2)}) collective-permute-start(bf16[256,256]{1,0:T(8,128)(2,1)S(1)} %get-tuple-element.20), channel_id=1, source_target_pairs={{0,8},{4,12},{8,0},{12,4},{1,9},{5,13},{9,1},{13,5},{2,10},{6,14},... | collective-permute-start | bytes 393224 | tf_op jit(solution)/shard_map/ppermute | solution.py:353
  6.6 1.3 %collective-permute-start.2 = (bf16[256,384]{1,0:T(8,128)(2,1)S(1)}, bf16[256,384]{1,0:T(8,128)(2,1)S(1)}, u32[]{:S(2)}, u32[]{:S(2)}) collective-permute-start(bf16[256,384]{1,0:T(8,128)(2,1)S(1)} %get-tuple-element.19), channel_id=1, source_target_pairs={{0,12},{4,8},{8,4},{12,0},{1,13},{5,9},{9,5},{13,1},{2,14},{6,10},... | collective-permute-start | bytes 589832 | tf_op jit(solution)/shard_map/ppermute | solution.py:353
  8.0 0.2 collective-permute-start.4
  8.2 0.1 fusion.2
  8.3 0.1 convert_reduce_fusion
  8.4 0.5 %copy-done.1 = s32[1,4]{1,0:T(1,128)S(1)} copy-done((s32[1,4]{1,0:T(1,128)S(1)}, s32[1,4]{1,0:T(1,128)}, u32[]{:S(2)}) %copy-start.1) | copy-done | bytes 40
  9.0 0.6 %tile_bias.1.refs_0_ = f32[256,256]{1,0:T(8,128)S(1)} custom-call(s32[1,4]{1,0:T(1,128)S(1)} %copy-done.1), custom_call_target="tpu_custom_call" | custom-call | flops 65536 | bytes 262144 | tf_op jit(solution)/shard_map/tile_bias/pallas_call | solution.py:283
  9.6 0.1 copy-done.2
  9.7 0.1 copy.9
  9.8 0.1 select_reduce_fusion.heads_ref
  10.0 0.0 collective-permute-done.key_other
  10.0 2.9 %collective-permute-start.6 = (bf16[256,128]{1,0:T(8,128)(2,1)S(1)}, bf16[256,128]{1,0:T(8,128)(2,1)S(1)}, u32[]{:S(2)}, u32[]{:S(2)}) collective-permute-start(bf16[256,128]{1,0:T(8,128)(2,1)S(1)} %get-tuple-element.22), channel_id=1, source_target_pairs={{0,8},{4,12},{8,0},{12,4},{1,9},{5,13},{9,1},{13,5},{2,10},{6,14},... | collective-permute-start | bytes 196616 | tf_op jit(solution)/shard_map/ppermute | solution.py:353
  12.8 0.0 collective-permute-done.1.value_other
  12.8 5.6 %spatial.1.refs_1_ = bf16[256,1536]{1,0:T(8,128)(2,1)} custom-call(s32[8]{0:T(128)S(1)} %select_reduce_fusion.heads_ref, s32[96,8]{1,0:T(8,128)S(1)} %bitcast.1, bf16[256,1536]{1,0:T(8,128)(2,1)} %query.1, bf16[256,1536]{1,0:T(8,128)(2,1)} %key_own.1, bf16[256,1536]{1,0:T(8,128)(2,1)S(1)} %collective-permute-done.key_other, bf16[256,1536]{1,0:T(8,128)(2,1)} %value_own.1, ...), custom_call_target="tpu_custom_call" | custom-call | flops 536870912 | bytes 3145728 | tf_op jit(solution)/shard_map/spatial/pallas_call | solution.py:242
  18.4 0.0 collective-permute-done.3.refs_4_
  18.4 0.0 collective-permute-done.2.refs_3_.refs_1_
  18.4 1.7 %collective-permute-done.4.refs_5_.refs_1_ = bf16[256,384]{1,0:T(8,128)(2,1)S(1)} collective-permute-done((bf16[256,384]{1,0:T(8,128)(2,1)S(1)}, bf16[256,384]{1,0:T(8,128)(2,1)S(1)}, u32[]{:S(2)}, u32[]{:S(2)}) %collective-permute-start.4) | collective-permute-done | bytes 196640 | tf_op jit(solution)/shard_map/ppermute | solution.py:353
  20.2 0.6 %temporal.5 = bf16[256,128]{1,0:T(8,128)(2,1)S(1)} custom-call(f32[256,256]{1,0:T(8,128)S(1)} %tile_bias.1.refs_0_, bf16[256,384]{1,0:T(8,128)(2,1)S(1)} %collective-permute-done.4.refs_5_.refs_1_, bf16[256,384]{1,0:T(8,128)(2,1)S(1)} %get-tuple-element.23.refs_1_.refs_2_, bf16[256,384]{1,0:T(8,128)(2,1)S(1)} %collective-permute-done.2.refs_3_.refs_1_, ...), custom_call_target="tpu_custom_call" | custom-call | flops 134217728 | bytes 655360 | tf_op jit(solution)/shard_map/temporal/pallas_call | solution.py:308
  20.8 4.1 %collective-permute-start.5 = (bf16[256,128]{1,0:T(8,128)(2,1)S(1)}, bf16[256,128]{1,0:T(8,128)(2,1)S(1)}, u32[]{:S(2)}, u32[]{:S(2)}) collective-permute-start(bf16[256,128]{1,0:T(8,128)(2,1)S(1)} %temporal.5), channel_id=1, source_target_pairs={{0,4},{4,0},{8,12},{12,8},{1,5},{5,1},{9,13},{13,9},{2,6},{6,2},{1... | collective-permute-start | bytes 196616 | tf_op jit(solution)/shard_map/ppermute | solution.py:353
  24.9 0.6 %temporal.7 = bf16[256,128]{1,0:T(8,128)(2,1)S(1)} custom-call(f32[256,256]{1,0:T(8,128)S(1)} %tile_bias.1.refs_0_, bf16[256,384]{1,0:T(8,128)(2,1)S(1)} %collective-permute-done.2.refs_3_.refs_1_, bf16[256,384]{1,0:T(8,128)(2,1)S(1)} %get-tuple-element.23.refs_1_.refs_2_, bf16[256,384]{1,0:T(8,128)(2,1)S(1)} %collective-permute-done.2.refs_3_.refs_1_, ...), custom_call_target="tpu_custom_call" | custom-call | flops 134217728 | bytes 655360 | tf_op jit(solution)/shard_map/temporal/pallas_call | solution.py:308
  25.6 3.1 %collective-permute-start.8 = (bf16[256,128]{1,0:T(8,128)(2,1)S(1)}, bf16[256,128]{1,0:T(8,128)(2,1)S(1)}, u32[]{:S(2)}, u32[]{:S(2)}) collective-permute-start(bf16[256,128]{1,0:T(8,128)(2,1)S(1)} %temporal.7), channel_id=1, source_target_pairs={{0,12},{4,8},{8,4},{12,0},{1,13},{5,9},{9,5},{13,1},{2,14},{6,10},... | collective-permute-start | bytes 196616 | tf_op jit(solution)/shard_map/ppermute | solution.py:353
  28.7 0.7 %temporal.6 = bf16[256,128]{1,0:T(8,128)(2,1)S(1)} custom-call(f32[256,256]{1,0:T(8,128)S(1)} %tile_bias.1.refs_0_, bf16[256,128]{1,0:T(8,128)(2,1)S(1)} %collective-permute-done.6.refs_1_, bf16[256,384]{1,0:T(8,128)(2,1)S(1)} %get-tuple-element.23.refs_1_.refs_2_, bf16[256,384]{1,0:T(8,128)(2,1)S(1)} %collective-permute-done.2.refs_3_.refs_1_, ...), custom_call_target="tpu_custom_call" | custom-call | flops 134217728 | bytes 655360 | tf_op jit(solution)/shard_map/temporal/pallas_call | solution.py:308
  29.3 0.1 collective-permute-start.7
  29.4 0.6 %temporal.4.refs_2_ = bf16[256,128]{1,0:T(8,128)(2,1)S(1)} custom-call(f32[256,256]{1,0:T(8,128)S(1)} %tile_bias.1.refs_0_, bf16[256,384]{1,0:T(8,128)(2,1)S(1)} %get-tuple-element.23.refs_1_.refs_2_, bf16[256,384]{1,0:T(8,128)(2,1)S(1)} %get-tuple-element.23.refs_1_.refs_2_, bf16[256,384]{1,0:T(8,128)(2,1)S(1)} %collective-permute-done.2.refs_3_.refs_1_, ...), custom_call_target="tpu_custom_call" | custom-call | flops 134217728 | bytes 655360 | tf_op jit(solution)/shard_map/temporal/pallas_call | solution.py:308
  30.1 0.0 collective-permute-done.5.refs_3_
  30.1 2.3 %collective-permute-done.8.refs_5_ = bf16[256,128]{1,0:T(8,128)(2,1)S(1)} collective-permute-done((bf16[256,128]{1,0:T(8,128)(2,1)S(1)}, bf16[256,128]{1,0:T(8,128)(2,1)S(1)}, u32[]{:S(2)}, u32[]{:S(2)}) %collective-permute-start.8) | collective-permute-done | bytes 65568 | tf_op jit(solution)/shard_map/ppermute | solution.py:353
  32.3 2.2 %collective-permute-done.7.refs_4_ = bf16[256,128]{1,0:T(8,128)(2,1)S(1)} collective-permute-done((bf16[256,128]{1,0:T(8,128)(2,1)S(1)}, bf16[256,128]{1,0:T(8,128)(2,1)S(1)}, u32[]{:S(2)}, u32[]{:S(2)}) %collective-permute-start.7) | collective-permute-done | bytes 65568 | tf_op jit(solution)/shard_map/ppermute | solution.py:353
  34.6 1.3 %merge.1 = bf16[256,1536]{1,0:T(8,128)(2,1)} custom-call(s32[4]{0:T(128)S(1)} %copy-done, bf16[256,1536]{1,0:T(8,128)(2,1)} %spatial.1.refs_1_, bf16[256,128]{1,0:T(8,128)(2,1)S(1)} %temporal.4.refs_2_, bf16[256,128]{1,0:T(8,128)(2,1)S(1)} %collective-permute-done.5.refs_3_, ...), custom_call_target="tpu_custom_call", output_to_operand_aliasing={{}: (1, {})} | custom-call | bytes 524288 | tf_op jit(solution)/shard_map/merge/pallas_call | solution.py:335
  (5 shorter events, 0.0 us)
Async XLA Ops:
  2.0 6.2 %copy-start = (s32[4]{0:T(128)S(1)}, s32[4]{0:T(128)}, u32[]{:S(2)}) copy-start(s32[4]{0:T(128)} %refs_0_.3) | copy-start | bytes 52
  2.0 8.0 %collective-permute-start = (bf16[256,1536]{1,0:T(8,128)(2,1)}, bf16[256,1536]{1,0:T(8,128)(2,1)S(1)}, u32[]{:S(2)}, u32[]{:S(2)}) collective-permute-start(bf16[256,1536]{1,0:T(8,128)(2,1)} %key_own.1), channel_id=1, source_target_pairs={{0,1},{1,0},{2,3},{3,2},{4,5},{5,4},{6,7},{7,6},{8,9},{9,8},{10,11... | collective-permute-start | bytes 2359304 | tf_op jit(solution)/shard_map/ppermute | solution.py:356
  2.5 10.3 %collective-permute-start.1 = (bf16[256,1536]{1,0:T(8,128)(2,1)}, bf16[256,1536]{1,0:T(8,128)(2,1)S(1)}, u32[]{:S(2)}, u32[]{:S(2)}) collective-permute-start(bf16[256,1536]{1,0:T(8,128)(2,1)} %value_own.1), channel_id=1, source_target_pairs={{0,1},{1,0},{2,3},{3,2},{4,5},{5,4},{6,7},{7,6},{8,9},{9,8},{10,11... | collective-permute-start | bytes 2359304 | tf_op jit(solution)/shard_map/ppermute | solution.py:356
  2.6 15.8 %collective-permute-start.3 = (bf16[256,256]{1,0:T(8,128)(2,1)S(1)}, bf16[256,256]{1,0:T(8,128)(2,1)S(1)}, u32[]{:S(2)}, u32[]{:S(2)}) collective-permute-start(bf16[256,256]{1,0:T(8,128)(2,1)S(1)} %get-tuple-element.20), channel_id=1, source_target_pairs={{0,8},{4,12},{8,0},{12,4},{1,9},{5,13},{9,1},{13,5},{2,10},{6,14},... | collective-permute-start | bytes 393224 | tf_op jit(solution)/shard_map/ppermute | solution.py:353
  6.6 11.8 %collective-permute-start.2 = (bf16[256,384]{1,0:T(8,128)(2,1)S(1)}, bf16[256,384]{1,0:T(8,128)(2,1)S(1)}, u32[]{:S(2)}, u32[]{:S(2)}) collective-permute-start(bf16[256,384]{1,0:T(8,128)(2,1)S(1)} %get-tuple-element.19), channel_id=1, source_target_pairs={{0,12},{4,8},{8,4},{12,0},{1,13},{5,9},{9,5},{13,1},{2,14},{6,10},... | collective-permute-start | bytes 589832 | tf_op jit(solution)/shard_map/ppermute | solution.py:353
  8.0 12.2 %collective-permute-start.4 = (bf16[256,384]{1,0:T(8,128)(2,1)S(1)}, bf16[256,384]{1,0:T(8,128)(2,1)S(1)}, u32[]{:S(2)}, u32[]{:S(2)}) collective-permute-start(bf16[256,384]{1,0:T(8,128)(2,1)S(1)} %get-tuple-element.21), channel_id=1, source_target_pairs={{0,4},{4,0},{8,12},{12,8},{1,5},{5,1},{9,13},{13,9},{2,6},{6,2},{1... | collective-permute-start | bytes 589832 | tf_op jit(solution)/shard_map/ppermute | solution.py:353
  8.3 0.7 %copy-start.1 = (s32[1,4]{1,0:T(1,128)S(1)}, s32[1,4]{1,0:T(1,128)}, u32[]{:S(2)}) copy-start(s32[1,4]{1,0:T(1,128)} %sizes_ref.1) | copy-start | bytes 52
  9.0 0.8 %copy-start.2 = (s32[12,8,8]{0,2,1:T(8,128)S(1)}, s32[12,8,8]{0,2,1:T(8,128)}, u32[]{:S(2)}) copy-start(s32[12,8,8]{0,2,1:T(8,128)} %param.9) | copy-start | bytes 9220
  10.0 18.7 %collective-permute-start.6 = (bf16[256,128]{1,0:T(8,128)(2,1)S(1)}, bf16[256,128]{1,0:T(8,128)(2,1)S(1)}, u32[]{:S(2)}, u32[]{:S(2)}) collective-permute-start(bf16[256,128]{1,0:T(8,128)(2,1)S(1)} %get-tuple-element.22), channel_id=1, source_target_pairs={{0,8},{4,12},{8,0},{12,4},{1,9},{5,13},{9,1},{13,5},{2,10},{6,14},... | collective-permute-start | bytes 196616 | tf_op jit(solution)/shard_map/ppermute | solution.py:353
  20.8 9.3 %collective-permute-start.5 = (bf16[256,128]{1,0:T(8,128)(2,1)S(1)}, bf16[256,128]{1,0:T(8,128)(2,1)S(1)}, u32[]{:S(2)}, u32[]{:S(2)}) collective-permute-start(bf16[256,128]{1,0:T(8,128)(2,1)S(1)} %temporal.5), channel_id=1, source_target_pairs={{0,4},{4,0},{8,12},{12,8},{1,5},{5,1},{9,13},{13,9},{2,6},{6,2},{1... | collective-permute-start | bytes 196616 | tf_op jit(solution)/shard_map/ppermute | solution.py:353
  25.6 6.7 %collective-permute-start.8 = (bf16[256,128]{1,0:T(8,128)(2,1)S(1)}, bf16[256,128]{1,0:T(8,128)(2,1)S(1)}, u32[]{:S(2)}, u32[]{:S(2)}) collective-permute-start(bf16[256,128]{1,0:T(8,128)(2,1)S(1)} %temporal.7), channel_id=1, source_target_pairs={{0,12},{4,8},{8,4},{12,0},{1,13},{5,9},{9,5},{13,1},{2,14},{6,10},... | collective-permute-start | bytes 196616 | tf_op jit(solution)/shard_map/ppermute | solution.py:353
  29.3 5.2 %collective-permute-start.7 = (bf16[256,128]{1,0:T(8,128)(2,1)S(1)}, bf16[256,128]{1,0:T(8,128)(2,1)S(1)}, u32[]{:S(2)}, u32[]{:S(2)}) collective-permute-start(bf16[256,128]{1,0:T(8,128)(2,1)S(1)} %temporal.6), channel_id=1, source_target_pairs={{0,8},{4,12},{8,0},{12,4},{1,9},{5,13},{9,1},{13,5},{2,10},{6,14},... | collective-permute-start | bytes 196616 | tf_op jit(solution)/shard_map/ppermute | solution.py:353

commit v5 on v4

--- a/solution.py
+++ b/solution.py
@@ -194,39 +194,37 @@
     )(*(pltpu.with_memory_space_constraint(array, pltpu.HBM) for array in (ids, query, key_proj, value)))
 
 
-def spatial_kernel(heads_ref, mask_ref, query, key_own, key_other, value_own, value_other, out, seen_ref, fetched, stage, arrive, leave):
+def spatial_kernel(heads_ref, mask_ref, query, key_own, key_other, value_own, value_other, out, bias_ref, asked, held, stage, arrive, leave):
     rows, count = query.shape[0], heads_ref.shape[0]
     own_blocks, frame_blocks = rows // BLK, mask_ref.shape[-1]
-    coming, going = [], []
+    coming = []
     for item in range(count):
-        coming.append(
-            [
-                pltpu.make_async_copy(
-                    source.at[:, columns(heads_ref[item])], fetched.at[item, :, i * HD : (i + 1) * HD], arrive.at[item, i]
-                )
-                for i, source in enumerate((query, key_own, value_own))
-            ]
-        )
-        for copy in coming[-1]:
-            copy.start()
+        here = columns(heads_ref[item])
+        for source, target in (
+            (query, asked.at[item]),
+            (key_own, held.at[item, 0, 0]),
+            (value_own, held.at[item, 1, 0]),
+            (key_other, held.at[item, 0, 1]),
+            (value_other, held.at[item, 1, 1]),
+        ):
+            coming.append(pltpu.make_async_copy(source.at[:, here], target, arrive.at[len(coming)]))
+            coming[-1].start()
     rep = lax.axis_index("rep")
     block = lax.broadcasted_iota(jnp.int32, (frame_blocks, 2 * rows), 1) // BLK
     block = lax.rem(block + rep * own_blocks, frame_blocks)
     spread = (block == lax.broadcasted_iota(jnp.int32, block.shape, 0)).astype(jnp.float32)
-    seen_ref[...] = jnp.dot(mask_ref[...].astype(jnp.float32), spread, preferred_element_type=jnp.float32)
-    for copies in coming:
-        for copy in copies:
-            copy.wait()
     for item in range(count):
-        head = heads_ref[item]
-        seen = seen_ref[pl.ds(pl.multiple_of(head * frame_blocks, frame_blocks), frame_blocks), :]
-        seen = jnp.where(rep == 0, seen[:own_blocks], seen[own_blocks:])
-        bias = jnp.where(seen > 0.5, 0.0, MASKED_SCORE)
-        bias = jnp.broadcast_to(bias[:, None, :], (own_blocks, BLK, 2 * rows)).reshape(rows, 2 * rows)
-        asked = fetched[item, :, :HD]
-        own = scores_of(asked, fetched[item, :, HD : 2 * HD]) + bias[:, :rows]
-        other = scores_of(asked, key_other[:, columns(head)]) + bias[:, rows:]
-        stage[item] = attend([own, other], [fetched[item, :, 2 * HD :], value_other[:, columns(head)]])
+        mask = mask_ref[heads_ref[item]].astype(jnp.float32)
+        mask = jnp.where(rep == 0, mask[:own_blocks], mask[own_blocks:])
+        seen = jnp.dot(mask, spread, preferred_element_type=jnp.float32)
+        bias_ref[item] = jnp.where(seen > 0.5, 0.0, MASKED_SCORE)
+    for copy in coming:
+        copy.wait()
+    going = []
+    for item in range(count):
+        bias = jnp.broadcast_to(bias_ref[item][:, None, :], (own_blocks, BLK, 2 * rows)).reshape(rows, 2 * rows)
+        scores = [scores_of(asked[item], held[item, 0, half]) + bias[:, half * rows : (half + 1) * rows] for half in range(2)]
+        stage[item] = attend(scores, [held[item, 1, half] for half in range(2)])
         if (item + 1) % 4 == 0 or item + 1 == count:
             for sent in range(len(going), item + 1):
                 going.append(pltpu.make_async_copy(stage.at[sent], out.at[:, columns(heads_ref[sent])], leave.at[sent]))
@@ -237,7 +235,7 @@
 
 def spatial(heads, mask, query, key_own, key_other, value_own, value_other):
     rows, width = query.shape
-    count, blocks = heads.shape[0], mask.shape[-1]
+    count = heads.shape[0]
     query, key_own, value_own = (pltpu.with_memory_space_constraint(x, pltpu.HBM) for x in (query, key_own, value_own))
     return pl.pallas_call(
         spatial_kernel,
@@ -245,10 +243,11 @@
         in_specs=[SMEM, VMEM, HBM, HBM, VMEM, HBM, VMEM],
         out_specs=HBM,
         scratch_shapes=[
-            pltpu.VMEM((mask.shape[0] * blocks, 2 * rows), jnp.float32),
-            pltpu.VMEM((count, rows, 3 * HD), query.dtype),
+            pltpu.VMEM((count, rows // BLK, 2 * rows), jnp.float32),
             pltpu.VMEM((count, rows, HD), query.dtype),
-            pltpu.SemaphoreType.DMA((count, 3)),
+            pltpu.VMEM((count, 2, 2, rows, HD), query.dtype),
+            pltpu.VMEM((count, rows, HD), query.dtype),
+            pltpu.SemaphoreType.DMA((5 * count,)),
             pltpu.SemaphoreType.DMA((count,)),
         ],
         name="spatial",
@@ -256,7 +255,7 @@
         cost_estimate=pl.CostEstimate(
             flops=8 * rows * rows * HD * count, bytes_accessed=12 * rows * HD * count, transcendentals=2 * rows * rows * count
         ),
-    )(heads, mask.reshape(-1, blocks), query, key_own, key_other, value_own, value_other)
+    )(heads, mask, query, key_own, key_other, value_own, value_other)
 
 
 def spatial_heads(ids, heads_here):
@@ -321,9 +320,11 @@
 def merge_kernel(heads_here, ids_ref, given, *rest):
     pieces, out, sems = rest[:-2], rest[-2], rest[-1]
     frame = lax.axis_index("frames")
+    ids = lax.rem(ids_ref[...], heads_here).astype(jnp.float32)
+    slot = lax.broadcasted_iota(jnp.int32, ids.shape, 1)
     copies = []
     for mask, piece in enumerate(pieces):
-        head = head_of(ids_ref, frame ^ mask, heads_here)
+        head = jnp.sum(jnp.where(slot == frame ^ mask, ids, 0.0)).astype(jnp.int32)
         copies.append(pltpu.make_async_copy(piece, out.at[:, columns(head)], sems.at[mask]))
         copies[-1].start()
     for copy in copies:
@@ -335,14 +336,18 @@
     return pl.pallas_call(
         lambda *refs: merge_kernel(width // HD, *refs),
         out_shape=jax.ShapeDtypeStruct(out.shape, out.dtype),
-        in_specs=[SMEM, ANY] + [VMEM] * len(pieces),
+        in_specs=[VMEM, ANY] + [VMEM] * len(pieces),
         out_specs=ANY,
         scratch_shapes=[pltpu.SemaphoreType.DMA((len(pieces),))],
         input_output_aliases={1: 0},
         name="merge",
         compiler_params=pltpu.CompilerParams(vmem_limit_bytes=4 << 20),
         cost_estimate=pl.CostEstimate(flops=0, bytes_accessed=4 * len(pieces) * rows * HD, transcendentals=0),
-    )(ids, out, *pieces)
+    )(ids.reshape(1, -1), out, *pieces)
+
+
+PLAN = ("s3", "k2", "s1", "wk", "wv", "x", "q2", "a31", "b3", "b1", "a2", "b2", "a0")
+NAMES = {"s": "qkv", "k": "kv", "q": "q"}
 
 
 def local_by_head(query, key_proj, value, block_mask, tile_sizes, temporal_ids):
@@ -352,40 +357,39 @@
     def exchange(array, mask):
         return lax.ppermute(array, "frames", [(i, i ^ mask) for i in range(frames)])
 
-    def swap(array):
-        return lax.ppermute(array, "rep", [(0, 1), (1, 0)])
-
-    first, last = frames - 1, frames // 2
-    near = [m for m in range(1, first) if m != last]
-    parts = [(first, "qkv"), (last, "kv")] + [(m, "qkv") for m in near] + [(last, "q"), (0, "qkv")]
-    packed = pack(temporal_ids, query, key_proj, value, parts, heads_here)
-    *travelling, own = packed
-    arrived = [exchange(piece, mask) for piece, (mask, _) in zip(travelling, parts)]
-    keys_sent, values_sent, *_ = lax.optimization_barrier((key_proj, value, *packed))
-    key_other, value_other = swap(keys_sent), swap(values_sent)
+    sends = [step for step in PLAN if step[0] in NAMES]
+    parts = [(int(step[1:]), NAMES[step[0]]) for step in sends] + [(0, "qkv")]
+    packed = dict(zip(sends + ["own"], pack(temporal_ids, query, key_proj, value, parts, heads_here)))
+    keys_sent, values_sent, *_ = lax.optimization_barrier((key_proj, value, *packed.values()))
+    swapped = {"wk": keys_sent, "wv": values_sent}
     bias = tile_bias(tile_sizes, query.shape[0])
     heads = spatial_heads(temporal_ids, heads_here)
-    bias, *inputs = lax.optimization_barrier((bias, key_other, value_other))
-    out = spatial(heads, block_mask, query, key_proj, inputs[0], value, inputs[1])
-    *arrived, late_query = arrived
-    out, *arrived = lax.optimization_barrier((out, *arrived))
-    groups = [own] + arrived
-    keys_at = [HD] + [HD if names == "qkv" else 0 for _, names in parts[: len(arrived)]]
-    turns = [(mask, piece) for piece, (mask, names) in zip(arrived, parts) if names == "qkv"]
-    turns = turns[:1] + [(last, late_query)] + turns[1:] + [(0, own)]
-    order = turns[:1] + turns[2:-1] + turns[1:2] + turns[-1:]
-    attended = {}
-    for mask, rows in order:
-        (attended[mask],) = temporal(bias, [rows], groups, keys_at)
-    returned = {0: attended[0]}
-    for mask, _ in turns[:-1]:
-        returned[mask] = exchange(attended[mask], mask)
+    queries, groups, keys_at, attended, returned = {0: packed["own"]}, [packed["own"]], [HD], {}, {}
+    for step in PLAN:
+        kind, masks = step[0], [int(digit) for digit in step[1:] if digit.isdigit()]
+        if kind in NAMES:
+            arrived = exchange(packed[step], masks[0])
+            if kind in "sq":
+                queries[masks[0]] = arrived
+            if kind in "sk":
+                groups.append(arrived)
+                keys_at.append(HD if kind == "s" else 0)
+        elif kind == "w":
+            swapped[step] = lax.ppermute(swapped[step], "rep", [(0, 1), (1, 0)])
+        elif kind == "x":
+            bias, *others = lax.optimization_barrier((bias, swapped["wk"], swapped["wv"]))
+            out = spatial(heads, block_mask, query, key_proj, others[0], value, others[1])
+        elif kind == "a":
+            attended.update(zip(masks, temporal(bias, [queries[mask] for mask in masks], groups, keys_at)))
+        elif kind == "b":
+            returned[masks[0]] = exchange(attended[masks[0]], masks[0])
+    returned[0] = attended[0]
     return merge(temporal_ids, out, [returned[mask] for mask in range(frames)])
 
 
 def local(query, key_proj, value, block_mask, tile_sizes, temporal_ids):
     frames, reps = lax.axis_size("frames"), lax.axis_size("rep")
-    by_head = temporal_ids.shape[0] == frames and frames & (frames - 1) == 0 and reps == 2
+    by_head = temporal_ids.shape[0] == frames == 4 and reps == 2
     form = local_by_head if by_head else local_by_tile
     return form(query, key_proj, value, block_mask, tile_sizes, temporal_ids)
 

time: 36.2 us -> 38.9 us (1.075)
  waiting for transfers between devices: 6.22 us -> 12.5 us
  starting transfers between devices: 16.4 us -> 13.2 us
    ppermute x7, waiting for transfers between devices: 6.22 us -> 12.5 us  [exchange(): return lax.ppermute(array, 'frames', [(i, i ^ mask) for i in range(frames)])]
    ppermute x7, starting transfers between devices: 15.7 us -> 12.5 us  [exchange(): return lax.ppermute(array, 'frames', [(i, i ^ mask) for i in range(frames)])]
    pallas_call x1, Pallas kernels: 1.29 us -> 0.87 us  [merge(): pl.pallas_call(lambda *refs: merge_kernel(width // HD, *refs), out_shape=...]
    pallas_call x4 -> x3, Pallas kernels: 2.6 us -> 2.44 us  [temporal(): pl.pallas_call(lambda *refs: temporal_kernel(keys_at, len(queries), *refs...]
    unnamed x7 -> x11, local copies, waits for them, and re-layouts: 0.79 us -> 0.7 us
  transfers between devices with their start and end apart: 9 -> 9, of which waited for: 3 -> 1; matrix products, arithmetic and copies ran while one was open for 1% -> 1% of each run, Pallas kernels for 24% -> 21%
where the time goes in v5:
time: 38.9 us; the launch traced here: 38.6 us
  starting transfers between devices  13.2 us (34%)
  waiting for transfers between devices  12.5 us (32%)
  Pallas kernels  11.8 us (30%)
  local copies, waits for them, and re-layouts  0.7 us (2%)
    ppermute x7, waiting for transfers between devices, exchange(): return lax.ppermute(array, 'frames', [(i, i ^ mask) for i in range(frames)])  12.5 us
    ppermute x7, starting transfers between devices, exchange(): return lax.ppermute(array, 'frames', [(i, i ^ mask) for i in range(frames)])  12.5 us
    pallas_call x1, Pallas kernels, spatial(): pl.pallas_call(spatial_kernel, out_shape=jax.ShapeDtypeStruct((rows, widt...  5.74 us
    pallas_call x3, Pallas kernels, temporal(): pl.pallas_call(lambda *refs: temporal_kernel(keys_at, len(queries), *refs...  2.44 us
    pallas_call x1, Pallas kernels, pack(): pl.pallas_call(lambda *refs: pack_kernel(heads_here, parts, *refs), out_s...  2.1 us
    pallas_call x1, Pallas kernels, merge(): pl.pallas_call(lambda *refs: merge_kernel(width // HD, *refs), out_shape=...  0.87 us
  transfers between devices with their start and end apart: 9, of which 1 were waited for; matrix products, arithmetic and copies ran while one was open for 1% of the time, Pallas kernels for 21%

profile of v5, /device:TPU:0, one launch (start us, length us, event | category | flops | bytes accessed | tf_op | source)
XLA Modules:
  0.0 38.6 jit_solution(7002988996976211570)
XLA Ops:
  0.0 2.1 %pack.1 = (bf16[256,384]{1,0:T(8,128)(2,1)S(1)}, bf16[256,256]{1,0:T(8,128)(2,1)S(1)}, bf16[256,384]{1,0:T(8,128)(2,1)S(1)}, bf16[256,128]{1,0:T(8,128)(2,1)S(1)}, bf16[256,384]{1,0:T(8,128)(2,1)S(1)}) custom-call(s32[4]{0:T(128)} %refs_0_.1, bf16[256,1536]{1,0:T(8,128)(2,1)} %query.1, bf16[256,1536]{1,0:T(8,128)(2,1)} %key_own.1, bf16[256,1536]{1,0:T(8,128)(2,1)} %value_own.1), custom_call_target="tpu_custom_call" | custom-call | bytes 1572864 | tf_op jit(solution)/shard_map/pack/pallas_call | solution.py:185
  2.1 0.0 copy-start
  2.1 0.6 %collective-permute-start = (bf16[256,1536]{1,0:T(8,128)(2,1)S(1)}, bf16[256,1536]{1,0:T(8,128)(2,1)S(1)}, u32[]{:S(2)}, u32[]{:S(2)}) collective-permute-start(bf16[256,1536]{1,0:T(8,128)(2,1)S(1)} %copy-done.2), channel_id=1, source_target_pairs={{0,1},{1,0},{2,3},{3,2},{4,5},{5,4},{6,7},{7,6},{8,9},{9,8},{10,11... | collective-permute-start | bytes 2359304 | tf_op jit(solution)/shard_map/ppermute | solution.py:378
  2.7 0.1 collective-permute-start.1
  2.8 5.0 %collective-permute-start.2 = (bf16[256,384]{1,0:T(8,128)(2,1)S(1)}, bf16[256,384]{1,0:T(8,128)(2,1)S(1)}, u32[]{:S(2)}, u32[]{:S(2)}) collective-permute-start(bf16[256,384]{1,0:T(8,128)(2,1)S(1)} %get-tuple-element.17), channel_id=1, source_target_pairs={{0,12},{4,8},{8,4},{12,0},{1,13},{5,9},{9,5},{13,1},{2,14},{6,10},... | collective-permute-start | bytes 589832 | tf_op jit(solution)/shard_map/ppermute | solution.py:358
  7.8 0.0 collective-permute-start.4
  7.8 0.6 %collective-permute-start.3 = (bf16[256,256]{1,0:T(8,128)(2,1)S(1)}, bf16[256,256]{1,0:T(8,128)(2,1)S(1)}, u32[]{:S(2)}, u32[]{:S(2)}) collective-permute-start(bf16[256,256]{1,0:T(8,128)(2,1)S(1)} %get-tuple-element.18), channel_id=1, source_target_pairs={{0,8},{4,12},{8,0},{12,4},{1,9},{5,13},{9,1},{13,5},{2,10},{6,14},... | collective-permute-start | bytes 393224 | tf_op jit(solution)/shard_map/ppermute | solution.py:358
  8.4 0.0 copy-start.1
  8.4 0.1 fusion.2
  8.5 0.6 %copy-done.1 = s32[1,4]{1,0:T(1,128)S(1)} copy-done((s32[1,4]{1,0:T(1,128)S(1)}, s32[1,4]{1,0:T(1,128)}, u32[]{:S(2)}) %copy-start.1) | copy-done | bytes 40
  9.0 0.6 %tile_bias.1.refs_0_ = f32[256,256]{1,0:T(8,128)S(1)} custom-call(s32[1,4]{1,0:T(1,128)S(1)} %copy-done.1), custom_call_target="tpu_custom_call" | custom-call | flops 65536 | bytes 262144 | tf_op jit(solution)/shard_map/tile_bias/pallas_call | solution.py:282
  9.6 0.0 collective-permute-done.key_other
  9.7 2.4 %collective-permute-start.6 = (bf16[256,128]{1,0:T(8,128)(2,1)S(1)}, bf16[256,128]{1,0:T(8,128)(2,1)S(1)}, u32[]{:S(2)}, u32[]{:S(2)}) collective-permute-start(bf16[256,128]{1,0:T(8,128)(2,1)S(1)} %get-tuple-element.20), channel_id=1, source_target_pairs={{0,8},{4,12},{8,0},{12,4},{1,9},{5,13},{9,1},{13,5},{2,10},{6,14},... | collective-permute-start | bytes 196616 | tf_op jit(solution)/shard_map/ppermute | solution.py:358
  12.1 0.1 convert_reduce_fusion
  12.2 0.0 collective-permute-done.1.value_other
  12.2 12.5 %collective-permute-done.6.refs_1_ = bf16[256,128]{1,0:T(8,128)(2,1)S(1)} collective-permute-done((bf16[256,128]{1,0:T(8,128)(2,1)S(1)}, bf16[256,128]{1,0:T(8,128)(2,1)S(1)}, u32[]{:S(2)}, u32[]{:S(2)}) %collective-permute-start.6) | collective-permute-done | bytes 65568 | tf_op jit(solution)/shard_map/ppermute | solution.py:358
  24.7 0.0 collective-permute-done.3.refs_4_.refs_5_
  24.7 0.0 collective-permute-done.2.refs_3_.refs_1_.refs_4_
  24.7 0.0 collective-permute-done.4.refs_5_.refs_2_.refs_6_
  24.7 0.6 %temporal.5 = bf16[256,128]{1,0:T(8,128)(2,1)S(1)} custom-call(f32[256,256]{1,0:T(8,128)S(1)} %tile_bias.1.refs_0_, bf16[256,128]{1,0:T(8,128)(2,1)S(1)} %collective-permute-done.6.refs_1_, bf16[256,384]{1,0:T(8,128)(2,1)S(1)} %get-tuple-element.21.refs_1_.refs_2_.refs_3_, bf16[256,384]{1,0:T(8,128)(2,1)S(1)} %collective-permute-done.2.refs_3_.refs_1_.refs_4_, ...), custom_call_target="tpu_custom_call" | custom-call | flops 134217728 | bytes 655360 | tf_op jit(solution)/shard_map/temporal/pallas_call | solution.py:307
  25.4 0.0 copy-start.4
  25.4 0.1 collective-permute-start.7
  25.5 1.1 %temporal.4 = (bf16[256,128]{1,0:T(8,128)(2,1)S(1)}, bf16[256,128]{1,0:T(8,128)(2,1)S(1)}) custom-call(f32[256,256]{1,0:T(8,128)S(1)} %tile_bias.1.refs_0_, bf16[256,384]{1,0:T(8,128)(2,1)S(1)} %collective-permute-done.2.refs_3_.refs_1_.refs_4_, bf16[256,384]{1,0:T(8,128)(2,1)S(1)} %collective-permute-done.4.refs_5_.refs_2_.refs_6_, ...), custom_call_target="tpu_custom_call" | custom-call | flops 268435456 | bytes 786432 | tf_op jit(solution)/shard_map/temporal/pallas_call | solution.py:307
  26.6 3.1 %collective-permute-start.5 = (bf16[256,128]{1,0:T(8,128)(2,1)S(1)}, bf16[256,128]{1,0:T(8,128)(2,1)S(1)}, u32[]{:S(2)}, u32[]{:S(2)}) collective-permute-start(bf16[256,128]{1,0:T(8,128)(2,1)S(1)} %get-tuple-element.27), channel_id=1, source_target_pairs={{0,4},{4,0},{8,12},{12,8},{1,5},{5,1},{9,13},{13,9},{2,6},{6,2},{1... | collective-permute-start | bytes 196616 | tf_op jit(solution)/shard_map/ppermute | solution.py:358
  29.7 1.3 %collective-permute-start.8 = (bf16[256,128]{1,0:T(8,128)(2,1)S(1)}, bf16[256,128]{1,0:T(8,128)(2,1)S(1)}, u32[]{:S(2)}, u32[]{:S(2)}) collective-permute-start(bf16[256,128]{1,0:T(8,128)(2,1)S(1)} %get-tuple-element.28), channel_id=1, source_target_pairs={{0,12},{4,8},{8,4},{12,0},{1,13},{5,9},{9,5},{13,1},{2,14},{6,10},... | collective-permute-start | bytes 196616 | tf_op jit(solution)/shard_map/ppermute | solution.py:358
  31.1 0.1 select_reduce_fusion.heads_ref
  31.2 0.1 copy.9.mask_ref
  31.3 0.7 %temporal.3.refs_2_ = bf16[256,128]{1,0:T(8,128)(2,1)S(1)} custom-call(f32[256,256]{1,0:T(8,128)S(1)} %tile_bias.1.refs_0_, bf16[256,384]{1,0:T(8,128)(2,1)S(1)} %get-tuple-element.21.refs_1_.refs_2_.refs_3_, bf16[256,384]{1,0:T(8,128)(2,1)S(1)} %get-tuple-element.21.refs_1_.refs_2_.refs_3_, ...), custom_call_target="tpu_custom_call" | custom-call | flops 134217728 | bytes 655360 | tf_op jit(solution)/shard_map/temporal/pallas_call | solution.py:307
  32.0 5.7 %spatial.1.refs_1_ = bf16[256,1536]{1,0:T(8,128)(2,1)} custom-call(s32[8]{0:T(128)S(1)} %select_reduce_fusion.heads_ref, s32[12,8,8]{2,1,0:T(8,128)S(1)} %copy.9.mask_ref, bf16[256,1536]{1,0:T(8,128)(2,1)} %query.1, bf16[256,1536]{1,0:T(8,128)(2,1)} %key_own.1, bf16[256,1536]{1,0:T(8,128)(2,1)S(1)} %collective-permute-done.key_other, ...), custom_call_target="tpu_custom_call" | custom-call | flops 536870912 | bytes 3145728 | tf_op jit(solution)/shard_map/spatial/pallas_call | solution.py:240
  37.7 0.0 collective-permute-done.5.refs_3_
  37.7 0.0 collective-permute-done.8.refs_5_
  37.7 0.9 %merge.1 = bf16[256,1536]{1,0:T(8,128)(2,1)} custom-call(s32[1,4]{1,0:T(1,128)S(1)} %bitcast.1, bf16[256,1536]{1,0:T(8,128)(2,1)} %spatial.1.refs_1_, bf16[256,128]{1,0:T(8,128)(2,1)S(1)} %temporal.3.refs_2_, bf16[256,128]{1,0:T(8,128)(2,1)S(1)} %collective-permute-done.5.refs_3_, ...), custom_call_target="tpu_custom_call", output_to_operand_aliasing={{}: (1, {})} | custom-call | bytes 524288 | tf_op jit(solution)/shard_map/merge/pallas_call | solution.py:336
  (8 shorter events, 0.0 us)
Async XLA Ops:
  0.0 2.1 %copy-start.2 = (bf16[256,1536]{1,0:T(8,128)(2,1)S(1)}, bf16[256,1536]{1,0:T(8,128)(2,1)}, u32[]{:S(2)}) copy-start(bf16[256,1536]{1,0:T(8,128)(2,1)} %key_own.1) | copy-start | bytes 2359300
  0.0 2.7 %copy-start.3 = (bf16[256,1536]{1,0:T(8,128)(2,1)S(1)}, bf16[256,1536]{1,0:T(8,128)(2,1)}, u32[]{:S(2)}) copy-start(bf16[256,1536]{1,0:T(8,128)(2,1)} %value_own.1) | copy-start | bytes 2359300
  2.1 6.2 %copy-start = (s32[4]{0:T(128)S(1)}, s32[4]{0:T(128)}, u32[]{:S(2)}) copy-start(s32[4]{0:T(128)} %refs_0_.1) | copy-start | bytes 52
  2.1 7.5 %collective-permute-start = (bf16[256,1536]{1,0:T(8,128)(2,1)S(1)}, bf16[256,1536]{1,0:T(8,128)(2,1)S(1)}, u32[]{:S(2)}, u32[]{:S(2)}) collective-permute-start(bf16[256,1536]{1,0:T(8,128)(2,1)S(1)} %copy-done.2), channel_id=1, source_target_pairs={{0,1},{1,0},{2,3},{3,2},{4,5},{5,4},{6,7},{7,6},{8,9},{9,8},{10,11... | collective-permute-start | bytes 2359304 | tf_op jit(solution)/shard_map/ppermute | solution.py:378
  2.7 9.5 %collective-permute-start.1 = (bf16[256,1536]{1,0:T(8,128)(2,1)S(1)}, bf16[256,1536]{1,0:T(8,128)(2,1)S(1)}, u32[]{:S(2)}, u32[]{:S(2)}) collective-permute-start(bf16[256,1536]{1,0:T(8,128)(2,1)S(1)} %copy-done.3), channel_id=1, source_target_pairs={{0,1},{1,0},{2,3},{3,2},{4,5},{5,4},{6,7},{7,6},{8,9},{9,8},{10,11... | collective-permute-start | bytes 2359304 | tf_op jit(solution)/shard_map/ppermute | solution.py:378
  2.8 22.0 %collective-permute-start.2 = (bf16[256,384]{1,0:T(8,128)(2,1)S(1)}, bf16[256,384]{1,0:T(8,128)(2,1)S(1)}, u32[]{:S(2)}, u32[]{:S(2)}) collective-permute-start(bf16[256,384]{1,0:T(8,128)(2,1)S(1)} %get-tuple-element.17), channel_id=1, source_target_pairs={{0,12},{4,8},{8,4},{12,0},{1,13},{5,9},{9,5},{13,1},{2,14},{6,10},... | collective-permute-start | bytes 589832 | tf_op jit(solution)/shard_map/ppermute | solution.py:358
  7.8 17.0 %collective-permute-start.4 = (bf16[256,384]{1,0:T(8,128)(2,1)S(1)}, bf16[256,384]{1,0:T(8,128)(2,1)S(1)}, u32[]{:S(2)}, u32[]{:S(2)}) collective-permute-start(bf16[256,384]{1,0:T(8,128)(2,1)S(1)} %get-tuple-element.19), channel_id=1, source_target_pairs={{0,4},{4,0},{8,12},{12,8},{1,5},{5,1},{9,13},{13,9},{2,6},{6,2},{1... | collective-permute-start | bytes 589832 | tf_op jit(solution)/shard_map/ppermute | solution.py:358
  7.8 16.9 %collective-permute-start.3 = (bf16[256,256]{1,0:T(8,128)(2,1)S(1)}, bf16[256,256]{1,0:T(8,128)(2,1)S(1)}, u32[]{:S(2)}, u32[]{:S(2)}) collective-permute-start(bf16[256,256]{1,0:T(8,128)(2,1)S(1)} %get-tuple-element.18), channel_id=1, source_target_pairs={{0,8},{4,12},{8,0},{12,4},{1,9},{5,13},{9,1},{13,5},{2,10},{6,14},... | collective-permute-start | bytes 393224 | tf_op jit(solution)/shard_map/ppermute | solution.py:358
  8.4 0.7 %copy-start.1 = (s32[1,4]{1,0:T(1,128)S(1)}, s32[1,4]{1,0:T(1,128)}, u32[]{:S(2)}) copy-start(s32[1,4]{1,0:T(1,128)} %sizes_ref.1) | copy-start | bytes 52
  9.7 15.1 %collective-permute-start.6 = (bf16[256,128]{1,0:T(8,128)(2,1)S(1)}, bf16[256,128]{1,0:T(8,128)(2,1)S(1)}, u32[]{:S(2)}, u32[]{:S(2)}) collective-permute-start(bf16[256,128]{1,0:T(8,128)(2,1)S(1)} %get-tuple-element.20), channel_id=1, source_target_pairs={{0,8},{4,12},{8,0},{12,4},{1,9},{5,13},{9,1},{13,5},{2,10},{6,14},... | collective-permute-start | bytes 196616 | tf_op jit(solution)/shard_map/ppermute | solution.py:358
  25.4 5.8 %copy-start.4 = (s32[12,8,8]{0,2,1:T(8,128)S(1)}, s32[12,8,8]{0,2,1:T(8,128)}, u32[]{:S(2)}) copy-start(s32[12,8,8]{0,2,1:T(8,128)} %param.9) | copy-start | bytes 9220
  25.4 12.3 %collective-permute-start.7 = (bf16[256,128]{1,0:T(8,128)(2,1)S(1)}, bf16[256,128]{1,0:T(8,128)(2,1)S(1)}, u32[]{:S(2)}, u32[]{:S(2)}) collective-permute-start(bf16[256,128]{1,0:T(8,128)(2,1)S(1)} %temporal.5), channel_id=1, source_target_pairs={{0,8},{4,12},{8,0},{12,4},{1,9},{5,13},{9,1},{13,5},{2,10},{6,14},... | collective-permute-start | bytes 196616 | tf_op jit(solution)/shard_map/ppermute | solution.py:358
  26.6 11.1 %collective-permute-start.5 = (bf16[256,128]{1,0:T(8,128)(2,1)S(1)}, bf16[256,128]{1,0:T(8,128)(2,1)S(1)}, u32[]{:S(2)}, u32[]{:S(2)}) collective-permute-start(bf16[256,128]{1,0:T(8,128)(2,1)S(1)} %get-tuple-element.27), channel_id=1, source_target_pairs={{0,4},{4,0},{8,12},{12,8},{1,5},{5,1},{9,13},{13,9},{2,6},{6,2},{1... | collective-permute-start | bytes 196616 | tf_op jit(solution)/shard_map/ppermute | solution.py:358
  29.7 8.0 %collective-permute-start.8 = (bf16[256,128]{1,0:T(8,128)(2,1)S(1)}, bf16[256,128]{1,0:T(8,128)(2,1)S(1)}, u32[]{:S(2)}, u32[]{:S(2)}) collective-permute-start(bf16[256,128]{1,0:T(8,128)(2,1)S(1)} %get-tuple-element.28), channel_id=1, source_target_pairs={{0,12},{4,8},{8,4},{12,0},{1,13},{5,9},{9,5},{13,1},{2,14},{6,10},... | collective-permute-start | bytes 196616 | tf_op jit(solution)/shard_map/ppermute | solution.py:358

commit v6 on v5

--- a/solution.py
+++ b/solution.py
@@ -133,19 +133,21 @@
     return lax.dot_general(rows, keys, (((1,), (1,)), ((), ())), preferred_element_type=jnp.float32)
 
 
-def attend(scores, values):
+def attend(scores, values, ones=False):
     highest = scores[0]
     for more in scores[1:]:
         highest = jnp.maximum(highest, more)
     highest = highest.max(axis=-1, keepdims=True)
-    raised = [jnp.exp2((group - highest) * EXP2_SCALE) for group in scores]
-    total = raised[0]
-    for more in raised[1:]:
-        total = total + more
-    out = jnp.dot(raised[0].astype(jnp.bfloat16), values[0], preferred_element_type=jnp.float32)
-    for weights, group_values in zip(raised[1:], values[1:]):
-        out = out + jnp.dot(weights.astype(jnp.bfloat16), group_values, preferred_element_type=jnp.float32)
-    return (out / total.sum(axis=-1, keepdims=True)).astype(jnp.bfloat16)
+    out, total = 0.0, 0.0
+    for group, group_values in zip(scores, values):
+        raised = jnp.exp2((group - highest) * EXP2_SCALE)
+        if ones:
+            group_values = jnp.concatenate([group_values, jnp.ones_like(group_values)], axis=1)
+        else:
+            total = total + raised
+        out = out + jnp.dot(raised.astype(jnp.bfloat16), group_values, preferred_element_type=jnp.float32)
+    total = out[:, HD:] if ones else total.sum(axis=-1, keepdims=True)
+    return (out[:, :HD] / total).astype(jnp.bfloat16)
 
 
 def columns(index):
@@ -224,7 +226,7 @@
     for item in range(count):
         bias = jnp.broadcast_to(bias_ref[item][:, None, :], (own_blocks, BLK, 2 * rows)).reshape(rows, 2 * rows)
         scores = [scores_of(asked[item], held[item, 0, half]) + bias[:, half * rows : (half + 1) * rows] for half in range(2)]
-        stage[item] = attend(scores, [held[item, 1, half] for half in range(2)])
+        stage[item] = attend(scores, [held[item, 1, half] for half in range(2)], ones=True)
         if (item + 1) % 4 == 0 or item + 1 == count:
             for sent in range(len(going), item + 1):
                 going.append(pltpu.make_async_copy(stage.at[sent], out.at[:, columns(heads_ref[sent])], leave.at[sent]))
@@ -346,7 +348,7 @@
     )(ids.reshape(1, -1), out, *pieces)
 
 
-PLAN = ("s3", "k2", "s1", "wk", "wv", "x", "q2", "a31", "b3", "b1", "a2", "b2", "a0")
+PLAN = ("s3", "s1", "k2", "d", "wk", "wv", "x", "q2", "a31", "b3", "b1", "a2", "b2", "a0")
 NAMES = {"s": "qkv", "k": "kv", "q": "q"}
 
 
@@ -362,7 +364,6 @@
     packed = dict(zip(sends + ["own"], pack(temporal_ids, query, key_proj, value, parts, heads_here)))
     keys_sent, values_sent, *_ = lax.optimization_barrier((key_proj, value, *packed.values()))
     swapped = {"wk": keys_sent, "wv": values_sent}
-    bias = tile_bias(tile_sizes, query.shape[0])
     heads = spatial_heads(temporal_ids, heads_here)
     queries, groups, keys_at, attended, returned = {0: packed["own"]}, [packed["own"]], [HD], {}, {}
     for step in PLAN:
@@ -377,8 +378,9 @@
         elif kind == "w":
             swapped[step] = lax.ppermute(swapped[step], "rep", [(0, 1), (1, 0)])
         elif kind == "x":
-            bias, *others = lax.optimization_barrier((bias, swapped["wk"], swapped["wv"]))
-            out = spatial(heads, block_mask, query, key_proj, others[0], value, others[1])
+            out = spatial(heads, block_mask, query, key_proj, swapped["wk"], value, swapped["wv"])
+        elif kind == "d":
+            bias = tile_bias(tile_sizes, query.shape[0])
         elif kind == "a":
             attended.update(zip(masks, temporal(bias, [queries[mask] for mask in masks], groups, keys_at)))
         elif kind == "b":

time: 38.9 us -> 36 us (0.925)
  waiting for transfers between devices: 12.5 us -> 11.1 us
  Pallas kernels: 11.8 us -> 10.6 us
  local copies, waits for them, and re-layouts: 0.7 us -> 0.13 us
    ppermute x7, waiting for transfers between devices: 12.5 us -> 11.1 us  [exchange(): return lax.ppermute(array, 'frames', [(i, i ^ mask) for i in range(frames)])]
    pallas_call x1, Pallas kernels: 5.74 us -> 4.69 us  [spatial(): pl.pallas_call(spatial_kernel, out_shape=jax.ShapeDtypeStruct((rows, widt...]
    unnamed x11 -> x7, local copies, waits for them, and re-layouts: 0.7 us -> 0.13 us
  transfers between devices with their start and end apart: 9 -> 9, of which waited for: 1 -> 2; matrix products, arithmetic and copies ran while one was open for 1% -> 1% of each run, Pallas kernels for 21% -> 22%
where the time goes in v6:
time: 36 us; the launch traced here: 35.7 us
  starting transfers between devices  13.4 us (37%)
  waiting for transfers between devices  11.1 us (31%)
  Pallas kernels  10.6 us (29%)
    ppermute x7, starting transfers between devices, exchange(): return lax.ppermute(array, 'frames', [(i, i ^ mask) for i in range(frames)])  12.8 us
    ppermute x7, waiting for transfers between devices, exchange(): return lax.ppermute(array, 'frames', [(i, i ^ mask) for i in range(frames)])  11.1 us
    pallas_call x1, Pallas kernels, spatial(): pl.pallas_call(spatial_kernel, out_shape=jax.ShapeDtypeStruct((rows, widt...  4.69 us
    pallas_call x3, Pallas kernels, temporal(): pl.pallas_call(lambda *refs: temporal_kernel(keys_at, len(queries), *refs...  2.43 us
    pallas_call x1, Pallas kernels, pack(): pl.pallas_call(lambda *refs: pack_kernel(heads_here, parts, *refs), out_s...  1.97 us
    pallas_call x1, Pallas kernels, merge(): pl.pallas_call(lambda *refs: merge_kernel(width // HD, *refs), out_shape=...  0.87 us
  transfers between devices with their start and end apart: 9, of which 2 were waited for; matrix products, arithmetic and copies ran while one was open for 1% of the time, Pallas kernels for 22%

profile of v6, /device:TPU:0, one launch (start us, length us, event | category | flops | bytes accessed | tf_op | source)
XLA Modules:
  0.0 35.7 jit_solution(7750642607575780296)
XLA Ops:
  0.0 2.0 %pack.1 = (bf16[256,384]{1,0:T(8,128)(2,1)S(1)}, bf16[256,384]{1,0:T(8,128)(2,1)S(1)}, bf16[256,256]{1,0:T(8,128)(2,1)S(1)}, bf16[256,128]{1,0:T(8,128)(2,1)S(1)}, bf16[256,384]{1,0:T(8,128)(2,1)S(1)}) custom-call(s32[4]{0:T(128)} %refs_0_.1, bf16[256,1536]{1,0:T(8,128)(2,1)} %query.1, bf16[256,1536]{1,0:T(8,128)(2,1)} %key_own.1, bf16[256,1536]{1,0:T(8,128)(2,1)} %value_own.1), custom_call_target="tpu_custom_call" | custom-call | bytes 1572864 | tf_op jit(solution)/shard_map/pack/pallas_call | solution.py:187
  2.0 0.0 copy-start
  2.0 0.6 %collective-permute-start = (bf16[256,1536]{1,0:T(8,128)(2,1)}, bf16[256,1536]{1,0:T(8,128)(2,1)S(1)}, u32[]{:S(2)}, u32[]{:S(2)}) collective-permute-start(bf16[256,1536]{1,0:T(8,128)(2,1)} %key_own.1), channel_id=1, source_target_pairs={{0,1},{1,0},{2,3},{3,2},{4,5},{5,4},{6,7},{7,6},{8,9},{9,8},{10,11... | collective-permute-start | bytes 2359304 | tf_op jit(solution)/shard_map/ppermute | solution.py:379
  2.5 0.1 collective-permute-start.1
  2.6 4.0 %collective-permute-start.4 = (bf16[256,256]{1,0:T(8,128)(2,1)S(1)}, bf16[256,256]{1,0:T(8,128)(2,1)S(1)}, u32[]{:S(2)}, u32[]{:S(2)}) collective-permute-start(bf16[256,256]{1,0:T(8,128)(2,1)S(1)} %get-tuple-element.16), channel_id=1, source_target_pairs={{0,8},{4,12},{8,0},{12,4},{1,9},{5,13},{9,1},{13,5},{2,10},{6,14},... | collective-permute-start | bytes 393224 | tf_op jit(solution)/shard_map/ppermute | solution.py:360
  6.6 1.3 %collective-permute-start.2 = (bf16[256,384]{1,0:T(8,128)(2,1)S(1)}, bf16[256,384]{1,0:T(8,128)(2,1)S(1)}, u32[]{:S(2)}, u32[]{:S(2)}) collective-permute-start(bf16[256,384]{1,0:T(8,128)(2,1)S(1)} %get-tuple-element.14), channel_id=1, source_target_pairs={{0,12},{4,8},{8,4},{12,0},{1,13},{5,9},{9,5},{13,1},{2,14},{6,10},... | collective-permute-start | bytes 589832 | tf_op jit(solution)/shard_map/ppermute | solution.py:360
  8.0 0.2 collective-permute-start.3
  8.2 0.0 copy-done
  8.2 0.1 fusion.2
  8.3 9.7 %collective-permute-done.4.refs_5_.refs_6_ = bf16[256,256]{1,0:T(8,128)(2,1)S(1)} collective-permute-done((bf16[256,256]{1,0:T(8,128)(2,1)S(1)}, bf16[256,256]{1,0:T(8,128)(2,1)S(1)}, u32[]{:S(2)}, u32[]{:S(2)}) %collective-permute-start.4) | collective-permute-done | bytes 131104 | tf_op jit(solution)/shard_map/ppermute | solution.py:360
  18.0 0.0 collective-permute-start.6
  18.0 0.1 convert_reduce_fusion
  18.2 0.0 copy-done.1
  18.2 0.6 %tile_bias.1.refs_0_ = f32[256,256]{1,0:T(8,128)S(1)} custom-call(s32[1,4]{1,0:T(1,128)S(1)} %copy-done.1), custom_call_target="tpu_custom_call" | custom-call | flops 65536 | bytes 262144 | tf_op jit(solution)/shard_map/tile_bias/pallas_call | solution.py:284
  18.8 0.0 collective-permute-done.2.refs_3_.refs_1_.refs_4_
  18.8 1.4 %collective-permute-done.3.refs_4_.refs_2_.refs_5_ = bf16[256,384]{1,0:T(8,128)(2,1)S(1)} collective-permute-done((bf16[256,384]{1,0:T(8,128)(2,1)S(1)}, bf16[256,384]{1,0:T(8,128)(2,1)S(1)}, u32[]{:S(2)}, u32[]{:S(2)}) %collective-permute-start.3) | collective-permute-done | bytes 196640 | tf_op jit(solution)/shard_map/ppermute | solution.py:360
  20.2 1.1 %temporal.4 = (bf16[256,128]{1,0:T(8,128)(2,1)S(1)}, bf16[256,128]{1,0:T(8,128)(2,1)S(1)}) custom-call(f32[256,256]{1,0:T(8,128)S(1)} %tile_bias.1.refs_0_, bf16[256,384]{1,0:T(8,128)(2,1)S(1)} %collective-permute-done.2.refs_3_.refs_1_.refs_4_, bf16[256,384]{1,0:T(8,128)(2,1)S(1)} %collective-permute-done.3.refs_4_.refs_2_.refs_5_, ...), custom_call_target="tpu_custom_call" | custom-call | flops 268435456 | bytes 786432 | tf_op jit(solution)/shard_map/temporal/pallas_call | solution.py:309
  21.3 4.1 %collective-permute-start.5 = (bf16[256,128]{1,0:T(8,128)(2,1)S(1)}, bf16[256,128]{1,0:T(8,128)(2,1)S(1)}, u32[]{:S(2)}, u32[]{:S(2)}) collective-permute-start(bf16[256,128]{1,0:T(8,128)(2,1)S(1)} %get-tuple-element.21), channel_id=1, source_target_pairs={{0,4},{4,0},{8,12},{12,8},{1,5},{5,1},{9,13},{13,9},{2,6},{6,2},{1... | collective-permute-start | bytes 196616 | tf_op jit(solution)/shard_map/ppermute | solution.py:360
  25.4 3.0 %collective-permute-start.8 = (bf16[256,128]{1,0:T(8,128)(2,1)S(1)}, bf16[256,128]{1,0:T(8,128)(2,1)S(1)}, u32[]{:S(2)}, u32[]{:S(2)}) collective-permute-start(bf16[256,128]{1,0:T(8,128)(2,1)S(1)} %get-tuple-element.22), channel_id=1, source_target_pairs={{0,12},{4,8},{8,4},{12,0},{1,13},{5,9},{9,5},{13,1},{2,14},{6,10},... | collective-permute-start | bytes 196616 | tf_op jit(solution)/shard_map/ppermute | solution.py:360
  28.4 0.0 collective-permute-done.6.refs_1_
  28.4 0.6 %temporal.5 = bf16[256,128]{1,0:T(8,128)(2,1)S(1)} custom-call(f32[256,256]{1,0:T(8,128)S(1)} %tile_bias.1.refs_0_, bf16[256,128]{1,0:T(8,128)(2,1)S(1)} %collective-permute-done.6.refs_1_, bf16[256,384]{1,0:T(8,128)(2,1)S(1)} %get-tuple-element.18.refs_1_.refs_2_.refs_3_, bf16[256,384]{1,0:T(8,128)(2,1)S(1)} %collective-permute-done.2.refs_3_.refs_1_.refs_4_, ...), custom_call_target="tpu_custom_call" | custom-call | flops 134217728 | bytes 655360 | tf_op jit(solution)/shard_map/temporal/pallas_call | solution.py:309
  29.1 0.1 collective-permute-start.7
  29.2 0.1 select_reduce_fusion.heads_ref
  29.3 0.1 copy.9.mask_ref
  29.4 0.7 %temporal.3.refs_2_ = bf16[256,128]{1,0:T(8,128)(2,1)S(1)} custom-call(f32[256,256]{1,0:T(8,128)S(1)} %tile_bias.1.refs_0_, bf16[256,384]{1,0:T(8,128)(2,1)S(1)} %get-tuple-element.18.refs_1_.refs_2_.refs_3_, bf16[256,384]{1,0:T(8,128)(2,1)S(1)} %get-tuple-element.18.refs_1_.refs_2_.refs_3_, ...), custom_call_target="tpu_custom_call" | custom-call | flops 134217728 | bytes 655360 | tf_op jit(solution)/shard_map/temporal/pallas_call | solution.py:309
  30.1 0.0 collective-permute-done.key_other
  30.1 0.0 collective-permute-done.1.value_other
  30.1 4.7 %spatial.1.refs_1_ = bf16[256,1536]{1,0:T(8,128)(2,1)} custom-call(s32[8]{0:T(128)S(1)} %select_reduce_fusion.heads_ref, s32[12,8,8]{2,1,0:T(8,128)S(1)} %copy.9.mask_ref, bf16[256,1536]{1,0:T(8,128)(2,1)} %query.1, bf16[256,1536]{1,0:T(8,128)(2,1)} %key_own.1, bf16[256,1536]{1,0:T(8,128)(2,1)S(1)} %collective-permute-done.key_other, ...), custom_call_target="tpu_custom_call" | custom-call | flops 536870912 | bytes 3145728 | tf_op jit(solution)/shard_map/spatial/pallas_call | solution.py:242
  34.8 0.0 collective-permute-done.5.refs_3_
  34.8 0.0 collective-permute-done.8.refs_5_
  34.8 0.0 collective-permute-done.7.refs_4_
  34.8 0.9 %merge.1 = bf16[256,1536]{1,0:T(8,128)(2,1)} custom-call(s32[1,4]{1,0:T(1,128)S(1)} %bitcast.1, bf16[256,1536]{1,0:T(8,128)(2,1)} %spatial.1.refs_1_, bf16[256,128]{1,0:T(8,128)(2,1)S(1)} %temporal.3.refs_2_, bf16[256,128]{1,0:T(8,128)(2,1)S(1)} %collective-permute-done.5.refs_3_, ...), custom_call_target="tpu_custom_call", output_to_operand_aliasing={{}: (1, {})} | custom-call | bytes 524288 | tf_op jit(solution)/shard_map/merge/pallas_call | solution.py:338
  (4 shorter events, 0.0 us)
Async XLA Ops:
  2.0 6.2 %copy-start = (s32[4]{0:T(128)S(1)}, s32[4]{0:T(128)}, u32[]{:S(2)}) copy-start(s32[4]{0:T(128)} %refs_0_.1) | copy-start | bytes 52
  2.0 28.1 %collective-permute-start = (bf16[256,1536]{1,0:T(8,128)(2,1)}, bf16[256,1536]{1,0:T(8,128)(2,1)S(1)}, u32[]{:S(2)}, u32[]{:S(2)}) collective-permute-start(bf16[256,1536]{1,0:T(8,128)(2,1)} %key_own.1), channel_id=1, source_target_pairs={{0,1},{1,0},{2,3},{3,2},{4,5},{5,4},{6,7},{7,6},{8,9},{9,8},{10,11... | collective-permute-start | bytes 2359304 | tf_op jit(solution)/shard_map/ppermute | solution.py:379
  2.5 27.5 %collective-permute-start.1 = (bf16[256,1536]{1,0:T(8,128)(2,1)}, bf16[256,1536]{1,0:T(8,128)(2,1)S(1)}, u32[]{:S(2)}, u32[]{:S(2)}) collective-permute-start(bf16[256,1536]{1,0:T(8,128)(2,1)} %value_own.1), channel_id=1, source_target_pairs={{0,1},{1,0},{2,3},{3,2},{4,5},{5,4},{6,7},{7,6},{8,9},{9,8},{10,11... | collective-permute-start | bytes 2359304 | tf_op jit(solution)/shard_map/ppermute | solution.py:379
  2.6 15.4 %collective-permute-start.4 = (bf16[256,256]{1,0:T(8,128)(2,1)S(1)}, bf16[256,256]{1,0:T(8,128)(2,1)S(1)}, u32[]{:S(2)}, u32[]{:S(2)}) collective-permute-start(bf16[256,256]{1,0:T(8,128)(2,1)S(1)} %get-tuple-element.16), channel_id=1, source_target_pairs={{0,8},{4,12},{8,0},{12,4},{1,9},{5,13},{9,1},{13,5},{2,10},{6,14},... | collective-permute-start | bytes 393224 | tf_op jit(solution)/shard_map/ppermute | solution.py:360
  6.6 12.2 %collective-permute-start.2 = (bf16[256,384]{1,0:T(8,128)(2,1)S(1)}, bf16[256,384]{1,0:T(8,128)(2,1)S(1)}, u32[]{:S(2)}, u32[]{:S(2)}) collective-permute-start(bf16[256,384]{1,0:T(8,128)(2,1)S(1)} %get-tuple-element.14), channel_id=1, source_target_pairs={{0,12},{4,8},{8,4},{12,0},{1,13},{5,9},{9,5},{13,1},{2,14},{6,10},... | collective-permute-start | bytes 589832 | tf_op jit(solution)/shard_map/ppermute | solution.py:360
  8.0 12.2 %collective-permute-start.3 = (bf16[256,384]{1,0:T(8,128)(2,1)S(1)}, bf16[256,384]{1,0:T(8,128)(2,1)S(1)}, u32[]{:S(2)}, u32[]{:S(2)}) collective-permute-start(bf16[256,384]{1,0:T(8,128)(2,1)S(1)} %get-tuple-element.15), channel_id=1, source_target_pairs={{0,4},{4,0},{8,12},{12,8},{1,5},{5,1},{9,13},{13,9},{2,6},{6,2},{1... | collective-permute-start | bytes 589832 | tf_op jit(solution)/shard_map/ppermute | solution.py:360
  8.3 9.9 %copy-start.1 = (s32[1,4]{1,0:T(1,128)S(1)}, s32[1,4]{1,0:T(1,128)}, u32[]{:S(2)}) copy-start(s32[1,4]{1,0:T(1,128)} %sizes_ref.1) | copy-start | bytes 52
  18.0 10.4 %collective-permute-start.6 = (bf16[256,128]{1,0:T(8,128)(2,1)S(1)}, bf16[256,128]{1,0:T(8,128)(2,1)S(1)}, u32[]{:S(2)}, u32[]{:S(2)}) collective-permute-start(bf16[256,128]{1,0:T(8,128)(2,1)S(1)} %get-tuple-element.17), channel_id=1, source_target_pairs={{0,8},{4,12},{8,0},{12,4},{1,9},{5,13},{9,1},{13,5},{2,10},{6,14},... | collective-permute-start | bytes 196616 | tf_op jit(solution)/shard_map/ppermute | solution.py:360
  21.3 13.5 %collective-permute-start.5 = (bf16[256,128]{1,0:T(8,128)(2,1)S(1)}, bf16[256,128]{1,0:T(8,128)(2,1)S(1)}, u32[]{:S(2)}, u32[]{:S(2)}) collective-permute-start(bf16[256,128]{1,0:T(8,128)(2,1)S(1)} %get-tuple-element.21), channel_id=1, source_target_pairs={{0,4},{4,0},{8,12},{12,8},{1,5},{5,1},{9,13},{13,9},{2,6},{6,2},{1... | collective-permute-start | bytes 196616 | tf_op jit(solution)/shard_map/ppermute | solution.py:360
  25.4 3.9 %copy-start.2 = (s32[12,8,8]{0,2,1:T(8,128)S(1)}, s32[12,8,8]{0,2,1:T(8,128)}, u32[]{:S(2)}) copy-start(s32[12,8,8]{0,2,1:T(8,128)} %param.9) | copy-start | bytes 9220
  25.4 9.4 %collective-permute-start.8 = (bf16[256,128]{1,0:T(8,128)(2,1)S(1)}, bf16[256,128]{1,0:T(8,128)(2,1)S(1)}, u32[]{:S(2)}, u32[]{:S(2)}) collective-permute-start(bf16[256,128]{1,0:T(8,128)(2,1)S(1)} %get-tuple-element.22), channel_id=1, source_target_pairs={{0,12},{4,8},{8,4},{12,0},{1,13},{5,9},{9,5},{13,1},{2,14},{6,10},... | collective-permute-start | bytes 196616 | tf_op jit(solution)/shard_map/ppermute | solution.py:360
  29.1 5.7 %collective-permute-start.7 = (bf16[256,128]{1,0:T(8,128)(2,1)S(1)}, bf16[256,128]{1,0:T(8,128)(2,1)S(1)}, u32[]{:S(2)}, u32[]{:S(2)}) collective-permute-start(bf16[256,128]{1,0:T(8,128)(2,1)S(1)} %temporal.5), channel_id=1, source_target_pairs={{0,8},{4,12},{8,0},{12,4},{1,9},{5,13},{9,1},{13,5},{2,10},{6,14},... | collective-permute-start | bytes 196616 | tf_op jit(solution)/shard_map/ppermute | solution.py:360

commit v7 on v6

--- a/solution.py
+++ b/solution.py
@@ -319,24 +319,24 @@
     )(bias, *queries, *groups)
 
 
-def merge_kernel(heads_here, ids_ref, given, *rest):
+def merge_kernel(heads_here, masks, ids_ref, given, *rest):
     pieces, out, sems = rest[:-2], rest[-2], rest[-1]
     frame = lax.axis_index("frames")
     ids = lax.rem(ids_ref[...], heads_here).astype(jnp.float32)
     slot = lax.broadcasted_iota(jnp.int32, ids.shape, 1)
     copies = []
-    for mask, piece in enumerate(pieces):
+    for place, (mask, piece) in enumerate(zip(masks, pieces)):
         head = jnp.sum(jnp.where(slot == frame ^ mask, ids, 0.0)).astype(jnp.int32)
-        copies.append(pltpu.make_async_copy(piece, out.at[:, columns(head)], sems.at[mask]))
+        copies.append(pltpu.make_async_copy(piece, out.at[:, columns(head)], sems.at[place]))
         copies[-1].start()
     for copy in copies:
         copy.wait()
 
 
-def merge(ids, out, pieces):
+def merge(ids, out, masks, pieces):
     rows, width = out.shape
     return pl.pallas_call(
-        lambda *refs: merge_kernel(width // HD, *refs),
+        lambda *refs: merge_kernel(width // HD, masks, *refs),
         out_shape=jax.ShapeDtypeStruct(out.shape, out.dtype),
         in_specs=[VMEM, ANY] + [VMEM] * len(pieces),
         out_specs=ANY,
@@ -364,7 +364,10 @@
     packed = dict(zip(sends + ["own"], pack(temporal_ids, query, key_proj, value, parts, heads_here)))
     keys_sent, values_sent, *_ = lax.optimization_barrier((key_proj, value, *packed.values()))
     swapped = {"wk": keys_sent, "wv": values_sent}
-    heads = spatial_heads(temporal_ids, heads_here)
+    late = int([step for step in PLAN if step[0] == "b"][-1][1:])
+    slot = jnp.arange(frames, dtype=jnp.int32) == lax.axis_index("frames") ^ late
+    head = jnp.sum(jnp.where(slot, lax.rem(temporal_ids, heads_here), 0))
+    heads, head = lax.optimization_barrier((spatial_heads(temporal_ids, heads_here), head))
     queries, groups, keys_at, attended, returned = {0: packed["own"]}, [packed["own"]], [HD], {}, {}
     for step in PLAN:
         kind, masks = step[0], [int(digit) for digit in step[1:] if digit.isdigit()]
@@ -386,7 +389,9 @@
         elif kind == "b":
             returned[masks[0]] = exchange(attended[masks[0]], masks[0])
     returned[0] = attended[0]
-    return merge(temporal_ids, out, [returned[mask] for mask in range(frames)])
+    masks = [mask for mask in range(frames) if mask != late]
+    out = merge(temporal_ids, out, masks, [returned[mask] for mask in masks])
+    return lax.dynamic_update_slice(out, returned[late], (0, head * HD))
 
 
 def local(query, key_proj, value, block_mask, tile_sizes, temporal_ids):

time: 36 us -> 37.2 us (1.033)
  local copies, waits for them, and re-layouts: 0.13 us -> 1.42 us
  waiting for transfers between devices: 11.1 us -> 9.82 us
  between operations: 0.11 us -> 0.78 us
  other arithmetic: 0.33 us -> 0.96 us
    ppermute x7, waiting for transfers between devices: 11.1 us -> 9.82 us  [exchange(): return lax.ppermute(array, 'frames', [(i, i ^ mask) for i in range(frames)])]
    unnamed x7, local copies, waits for them, and re-layouts: 0.13 us -> 0.78 us
    dynamic_update_slice x0 -> x1, local copies, waits for them, and re-layouts: none -> 0.64 us  [local_by_head(): return lax.dynamic_update_slice(out, returned[late], (0, head * HD))]
    reduce_sum x0 -> x1, other arithmetic: none -> 0.64 us  [local_by_head(): head = jnp.sum(jnp.where(slot, lax.rem(temporal_ids, heads_here), 0))]
  transfers between devices with their start and end apart: 9 -> 9, of which waited for: 2 -> 2; matrix products, arithmetic and copies ran while one was open for 1% -> 3% of each run, Pallas kernels for 22% -> 23%
where the time goes in v7:
time: 37.2 us; the launch traced here: 37 us
  starting transfers between devices  13.4 us (36%)
  Pallas kernels  10.5 us (28%)
  waiting for transfers between devices  9.82 us (26%)
  local copies, waits for them, and re-layouts  1.42 us (4%)
  other arithmetic  0.96 us (3%)
  between operations  0.78 us (2%)
    ppermute x7, starting transfers between devices, exchange(): return lax.ppermute(array, 'frames', [(i, i ^ mask) for i in range(frames)])  12.8 us
    ppermute x7, waiting for transfers between devices, exchange(): return lax.ppermute(array, 'frames', [(i, i ^ mask) for i in range(frames)])  9.82 us
    pallas_call x1, Pallas kernels, spatial(): pl.pallas_call(spatial_kernel, out_shape=jax.ShapeDtypeStruct((rows, widt...  4.69 us
    pallas_call x3, Pallas kernels, temporal(): pl.pallas_call(lambda *refs: temporal_kernel(keys_at, len(queries), *refs...  2.43 us
    pallas_call x1, Pallas kernels, pack(): pl.pallas_call(lambda *refs: pack_kernel(heads_here, parts, *refs), out_s...  1.97 us
    pallas_call x1, Pallas kernels, merge(): pl.pallas_call(lambda *refs: merge_kernel(width // HD, masks, *refs), out...  0.84 us
    unnamed x7, local copies, waits for them, and re-layouts  0.78 us
  transfers between devices with their start and end apart: 9, of which 2 were waited for; matrix products, arithmetic and copies ran while one was open for 3% of the time, Pallas kernels for 23%

profile of v7, /device:TPU:0, one launch (start us, length us, event | category | flops | bytes accessed | tf_op | source)
XLA Modules:
  0.0 37.0 jit_solution(14470948226566857127)
XLA Ops:
  0.0 2.0 %pack.1 = (bf16[256,384]{1,0:T(8,128)(2,1)S(1)}, bf16[256,384]{1,0:T(8,128)(2,1)S(1)}, bf16[256,256]{1,0:T(8,128)(2,1)S(1)}, bf16[256,128]{1,0:T(8,128)(2,1)S(1)}, bf16[256,384]{1,0:T(8,128)(2,1)S(1)}) custom-call(s32[4]{0:T(128)} %refs_0_.1, bf16[256,1536]{1,0:T(8,128)(2,1)} %query.1, bf16[256,1536]{1,0:T(8,128)(2,1)} %key_own.1, bf16[256,1536]{1,0:T(8,128)(2,1)} %value_own.1), custom_call_target="tpu_custom_call" | custom-call | bytes 1572864 | tf_op jit(solution)/shard_map/pack/pallas_call | solution.py:187
  2.0 0.6 %collective-permute-start = (bf16[256,1536]{1,0:T(8,128)(2,1)}, bf16[256,1536]{1,0:T(8,128)(2,1)S(1)}, u32[]{:S(2)}, u32[]{:S(2)}) collective-permute-start(bf16[256,1536]{1,0:T(8,128)(2,1)} %key_own.1), channel_id=1, source_target_pairs={{0,1},{1,0},{2,3},{3,2},{4,5},{5,4},{6,7},{7,6},{8,9},{9,8},{10,11... | collective-permute-start | bytes 2359304 | tf_op jit(solution)/shard_map/ppermute | solution.py:382
  2.5 0.1 collective-permute-start.1
  2.6 4.0 %collective-permute-start.4 = (bf16[256,256]{1,0:T(8,128)(2,1)S(1)}, bf16[256,256]{1,0:T(8,128)(2,1)S(1)}, u32[]{:S(2)}, u32[]{:S(2)}) collective-permute-start(bf16[256,256]{1,0:T(8,128)(2,1)S(1)} %get-tuple-element.19), channel_id=1, source_target_pairs={{0,8},{4,12},{8,0},{12,4},{1,9},{5,13},{9,1},{13,5},{2,10},{6,14},... | collective-permute-start | bytes 393224 | tf_op jit(solution)/shard_map/ppermute | solution.py:360
  6.6 1.3 %collective-permute-start.2 = (bf16[256,384]{1,0:T(8,128)(2,1)S(1)}, bf16[256,384]{1,0:T(8,128)(2,1)S(1)}, u32[]{:S(2)}, u32[]{:S(2)}) collective-permute-start(bf16[256,384]{1,0:T(8,128)(2,1)S(1)} %get-tuple-element.17), channel_id=1, source_target_pairs={{0,12},{4,8},{8,4},{12,0},{1,13},{5,9},{9,5},{13,1},{2,14},{6,10},... | collective-permute-start | bytes 589832 | tf_op jit(solution)/shard_map/ppermute | solution.py:360
  8.0 0.2 collective-permute-start.3
  8.2 0.7 %copy-done = s32[4]{0:T(128)S(1)} copy-done((s32[4]{0:T(128)S(1)}, s32[4]{0:T(128)}, u32[]{:S(2)}) %copy-start) | copy-done | bytes 40
  8.9 0.6 %fusion.3 = (s32[]{:T(128)}, s32[4]{0:T(128)S(1)}) fusion(s32[]{:T(128)S(6)} %xor.3, s32[4]{0:T(128)S(1)} %copy-done), kind=kLoop, calls=%fused_computation.9 | loop fusion | flops 15 | bytes 40 | tf_op jit(solution)/shard_map/reduce_sum | solution.py:369
  9.5 0.1 fusion.2
  9.6 8.5 %collective-permute-done.4.refs_5_.refs_6_ = bf16[256,256]{1,0:T(8,128)(2,1)S(1)} collective-permute-done((bf16[256,256]{1,0:T(8,128)(2,1)S(1)}, bf16[256,256]{1,0:T(8,128)(2,1)S(1)}, u32[]{:S(2)}, u32[]{:S(2)}) %collective-permute-start.4) | collective-permute-done | bytes 131104 | tf_op jit(solution)/shard_map/ppermute | solution.py:360
  18.0 0.0 collective-permute-start.7
  18.0 0.1 convert_reduce_fusion
  18.2 0.6 %tile_bias.1.refs_0_ = f32[256,256]{1,0:T(8,128)S(1)} custom-call(s32[1,4]{1,0:T(1,128)S(1)} %copy-done.1), custom_call_target="tpu_custom_call" | custom-call | flops 65536 | bytes 262144 | tf_op jit(solution)/shard_map/tile_bias/pallas_call | solution.py:284
  18.8 0.0 collective-permute-done.2.refs_3_.refs_1_.refs_4_
  18.8 1.4 %collective-permute-done.3.refs_4_.refs_2_.refs_5_ = bf16[256,384]{1,0:T(8,128)(2,1)S(1)} collective-permute-done((bf16[256,384]{1,0:T(8,128)(2,1)S(1)}, bf16[256,384]{1,0:T(8,128)(2,1)S(1)}, u32[]{:S(2)}, u32[]{:S(2)}) %collective-permute-start.3) | collective-permute-done | bytes 196640 | tf_op jit(solution)/shard_map/ppermute | solution.py:360
  20.1 1.1 %temporal.4 = (bf16[256,128]{1,0:T(8,128)(2,1)S(1)}, bf16[256,128]{1,0:T(8,128)(2,1)S(1)}) custom-call(f32[256,256]{1,0:T(8,128)S(1)} %tile_bias.1.refs_0_, bf16[256,384]{1,0:T(8,128)(2,1)S(1)} %collective-permute-done.2.refs_3_.refs_1_.refs_4_, bf16[256,384]{1,0:T(8,128)(2,1)S(1)} %collective-permute-done.3.refs_4_.refs_2_.refs_5_, ...), custom_call_target="tpu_custom_call" | custom-call | flops 268435456 | bytes 786432 | tf_op jit(solution)/shard_map/temporal/pallas_call | solution.py:309
  21.3 4.1 %collective-permute-start.5 = (bf16[256,128]{1,0:T(8,128)(2,1)S(1)}, bf16[256,128]{1,0:T(8,128)(2,1)S(1)}, u32[]{:S(2)}, u32[]{:S(2)}) collective-permute-start(bf16[256,128]{1,0:T(8,128)(2,1)S(1)} %get-tuple-element.24), channel_id=1, source_target_pairs={{0,4},{4,0},{8,12},{12,8},{1,5},{5,1},{9,13},{13,9},{2,6},{6,2},{1... | collective-permute-start | bytes 196616 | tf_op jit(solution)/shard_map/ppermute | solution.py:360
  25.4 3.0 %collective-permute-start.6 = (bf16[256,128]{1,0:T(8,128)(2,1)S(1)}, bf16[256,128]{1,0:T(8,128)(2,1)S(1)}, u32[]{:S(2)}, u32[]{:S(2)}) collective-permute-start(bf16[256,128]{1,0:T(8,128)(2,1)S(1)} %get-tuple-element.25), channel_id=1, source_target_pairs={{0,12},{4,8},{8,4},{12,0},{1,13},{5,9},{9,5},{13,1},{2,14},{6,10},... | collective-permute-start | bytes 196616 | tf_op jit(solution)/shard_map/ppermute | solution.py:360
  28.4 0.0 collective-permute-done.7.refs_1_
  28.4 0.7 %temporal.5 = bf16[256,128]{1,0:T(8,128)(2,1)S(1)} custom-call(f32[256,256]{1,0:T(8,128)S(1)} %tile_bias.1.refs_0_, bf16[256,128]{1,0:T(8,128)(2,1)S(1)} %collective-permute-done.7.refs_1_, bf16[256,384]{1,0:T(8,128)(2,1)S(1)} %get-tuple-element.21.refs_1_.refs_2_.refs_3_, bf16[256,384]{1,0:T(8,128)(2,1)S(1)} %collective-permute-done.2.refs_3_.refs_1_.refs_4_, ...), custom_call_target="tpu_custom_call" | custom-call | flops 134217728 | bytes 655360 | tf_op jit(solution)/shard_map/temporal/pallas_call | solution.py:309
  29.1 0.1 collective-permute-start.8
  29.2 0.1 select_reduce_fusion.heads_ref
  29.9 0.1 copy.9.mask_ref
  30.1 0.7 %temporal.3.refs_2_ = bf16[256,128]{1,0:T(8,128)(2,1)S(1)} custom-call(f32[256,256]{1,0:T(8,128)S(1)} %tile_bias.1.refs_0_, bf16[256,384]{1,0:T(8,128)(2,1)S(1)} %get-tuple-element.21.refs_1_.refs_2_.refs_3_, bf16[256,384]{1,0:T(8,128)(2,1)S(1)} %get-tuple-element.21.refs_1_.refs_2_.refs_3_, ...), custom_call_target="tpu_custom_call" | custom-call | flops 134217728 | bytes 655360 | tf_op jit(solution)/shard_map/temporal/pallas_call | solution.py:309
  30.7 0.0 collective-permute-done.key_other
  30.7 0.0 collective-permute-done.1.value_other
  30.7 4.7 %spatial.1.refs_1_ = bf16[256,1536]{1,0:T(8,128)(2,1)} custom-call(s32[8]{0:T(128)S(1)} %select_reduce_fusion.heads_ref, s32[12,8,8]{2,1,0:T(8,128)S(1)} %copy.9.mask_ref, bf16[256,1536]{1,0:T(8,128)(2,1)} %query.1, bf16[256,1536]{1,0:T(8,128)(2,1)} %key_own.1, bf16[256,1536]{1,0:T(8,128)(2,1)S(1)} %collective-permute-done.key_other, ...), custom_call_target="tpu_custom_call" | custom-call | flops 536870912 | bytes 3145728 | tf_op jit(solution)/shard_map/spatial/pallas_call | solution.py:242
  35.4 0.0 collective-permute-done.5.refs_3_
  35.5 0.0 collective-permute-done.6.refs_4_
  35.5 0.8 %merge.1 = bf16[256,1536]{1,0:T(8,128)(2,1)} custom-call(s32[1,4]{1,0:T(1,128)S(1)} %bitcast.1, bf16[256,1536]{1,0:T(8,128)(2,1)} %spatial.1.refs_1_, bf16[256,128]{1,0:T(8,128)(2,1)S(1)} %temporal.3.refs_2_, bf16[256,128]{1,0:T(8,128)(2,1)S(1)} %collective-permute-done.5.refs_3_, ...), custom_call_target="tpu_custom_call", output_to_operand_aliasing={{}: (1, {})} | custom-call | bytes 393216 | tf_op jit(solution)/shard_map/merge/pallas_call | solution.py:338
  36.3 0.0 collective-permute-done.8
  36.3 0.6 %constant_dynamic-update-slice_fusion = bf16[256,1536]{1,0:T(8,128)(2,1)} fusion(bf16[256,1536]{1,0:T(8,128)(2,1)} %merge.1, bf16[256,128]{1,0:T(8,128)(2,1)S(1)} %collective-permute-done.8, s32[]{:T(128)S(6)} %select_n.13), kind=kLoop, calls=%fused_computation.10 | loop fusion | bytes 131076 | tf_op jit(solution)/shard_map/dynamic_update_slice | solution.py:394
  (5 shorter events, 0.0 us)
Async XLA Ops:
  2.0 28.8 %collective-permute-start = (bf16[256,1536]{1,0:T(8,128)(2,1)}, bf16[256,1536]{1,0:T(8,128)(2,1)S(1)}, u32[]{:S(2)}, u32[]{:S(2)}) collective-permute-start(bf16[256,1536]{1,0:T(8,128)(2,1)} %key_own.1), channel_id=1, source_target_pairs={{0,1},{1,0},{2,3},{3,2},{4,5},{5,4},{6,7},{7,6},{8,9},{9,8},{10,11... | collective-permute-start | bytes 2359304 | tf_op jit(solution)/shard_map/ppermute | solution.py:382
  2.5 28.2 %collective-permute-start.1 = (bf16[256,1536]{1,0:T(8,128)(2,1)}, bf16[256,1536]{1,0:T(8,128)(2,1)S(1)}, u32[]{:S(2)}, u32[]{:S(2)}) collective-permute-start(bf16[256,1536]{1,0:T(8,128)(2,1)} %value_own.1), channel_id=1, source_target_pairs={{0,1},{1,0},{2,3},{3,2},{4,5},{5,4},{6,7},{7,6},{8,9},{9,8},{10,11... | collective-permute-start | bytes 2359304 | tf_op jit(solution)/shard_map/ppermute | solution.py:382
  2.6 15.4 %collective-permute-start.4 = (bf16[256,256]{1,0:T(8,128)(2,1)S(1)}, bf16[256,256]{1,0:T(8,128)(2,1)S(1)}, u32[]{:S(2)}, u32[]{:S(2)}) collective-permute-start(bf16[256,256]{1,0:T(8,128)(2,1)S(1)} %get-tuple-element.19), channel_id=1, source_target_pairs={{0,8},{4,12},{8,0},{12,4},{1,9},{5,13},{9,1},{13,5},{2,10},{6,14},... | collective-permute-start | bytes 393224 | tf_op jit(solution)/shard_map/ppermute | solution.py:360
  6.6 12.2 %collective-permute-start.2 = (bf16[256,384]{1,0:T(8,128)(2,1)S(1)}, bf16[256,384]{1,0:T(8,128)(2,1)S(1)}, u32[]{:S(2)}, u32[]{:S(2)}) collective-permute-start(bf16[256,384]{1,0:T(8,128)(2,1)S(1)} %get-tuple-element.17), channel_id=1, source_target_pairs={{0,12},{4,8},{8,4},{12,0},{1,13},{5,9},{9,5},{13,1},{2,14},{6,10},... | collective-permute-start | bytes 589832 | tf_op jit(solution)/shard_map/ppermute | solution.py:360
  8.0 12.2 %collective-permute-start.3 = (bf16[256,384]{1,0:T(8,128)(2,1)S(1)}, bf16[256,384]{1,0:T(8,128)(2,1)S(1)}, u32[]{:S(2)}, u32[]{:S(2)}) collective-permute-start(bf16[256,384]{1,0:T(8,128)(2,1)S(1)} %get-tuple-element.18), channel_id=1, source_target_pairs={{0,4},{4,0},{8,12},{12,8},{1,5},{5,1},{9,13},{13,9},{2,6},{6,2},{1... | collective-permute-start | bytes 589832 | tf_op jit(solution)/shard_map/ppermute | solution.py:360
  8.2 0.7 %copy-start = (s32[4]{0:T(128)S(1)}, s32[4]{0:T(128)}, u32[]{:S(2)}) copy-start(s32[4]{0:T(128)} %refs_0_.1) | copy-start | bytes 52
  9.6 8.6 %copy-start.1 = (s32[1,4]{1,0:T(1,128)S(1)}, s32[1,4]{1,0:T(1,128)}, u32[]{:S(2)}) copy-start(s32[1,4]{1,0:T(1,128)} %sizes_ref.1) | copy-start | bytes 52
  18.0 10.4 %collective-permute-start.7 = (bf16[256,128]{1,0:T(8,128)(2,1)S(1)}, bf16[256,128]{1,0:T(8,128)(2,1)S(1)}, u32[]{:S(2)}, u32[]{:S(2)}) collective-permute-start(bf16[256,128]{1,0:T(8,128)(2,1)S(1)} %get-tuple-element.20), channel_id=1, source_target_pairs={{0,8},{4,12},{8,0},{12,4},{1,9},{5,13},{9,1},{13,5},{2,10},{6,14},... | collective-permute-start | bytes 196616 | tf_op jit(solution)/shard_map/ppermute | solution.py:360
  21.3 14.2 %collective-permute-start.5 = (bf16[256,128]{1,0:T(8,128)(2,1)S(1)}, bf16[256,128]{1,0:T(8,128)(2,1)S(1)}, u32[]{:S(2)}, u32[]{:S(2)}) collective-permute-start(bf16[256,128]{1,0:T(8,128)(2,1)S(1)} %get-tuple-element.24), channel_id=1, source_target_pairs={{0,4},{4,0},{8,12},{12,8},{1,5},{5,1},{9,13},{13,9},{2,6},{6,2},{1... | collective-permute-start | bytes 196616 | tf_op jit(solution)/shard_map/ppermute | solution.py:360
  25.4 4.5 %copy-start.2 = (s32[12,8,8]{0,2,1:T(8,128)S(1)}, s32[12,8,8]{0,2,1:T(8,128)}, u32[]{:S(2)}) copy-start(s32[12,8,8]{0,2,1:T(8,128)} %param.9) | copy-start | bytes 9220
  25.4 10.1 %collective-permute-start.6 = (bf16[256,128]{1,0:T(8,128)(2,1)S(1)}, bf16[256,128]{1,0:T(8,128)(2,1)S(1)}, u32[]{:S(2)}, u32[]{:S(2)}) collective-permute-start(bf16[256,128]{1,0:T(8,128)(2,1)S(1)} %get-tuple-element.25), channel_id=1, source_target_pairs={{0,12},{4,8},{8,4},{12,0},{1,13},{5,9},{9,5},{13,1},{2,14},{6,10},... | collective-permute-start | bytes 196616 | tf_op jit(solution)/shard_map/ppermute | solution.py:360
  29.1 7.2 %collective-permute-start.8 = (bf16[256,128]{1,0:T(8,128)(2,1)S(1)}, bf16[256,128]{1,0:T(8,128)(2,1)S(1)}, u32[]{:S(2)}, u32[]{:S(2)}) collective-permute-start(bf16[256,128]{1,0:T(8,128)(2,1)S(1)} %temporal.5), channel_id=1, source_target_pairs={{0,8},{4,12},{8,0},{12,4},{1,9},{5,13},{9,1},{13,5},{2,10},{6,14},... | collective-permute-start | bytes 196616 | tf_op jit(solution)/shard_map/ppermute | solution.py:360

commit v8 on v7

--- a/solution.py
+++ b/solution.py
@@ -348,7 +348,7 @@
     )(ids.reshape(1, -1), out, *pieces)
 
 
-PLAN = ("s3", "s1", "k2", "d", "wk", "wv", "x", "q2", "a31", "b3", "b1", "a2", "b2", "a0")
+PLAN = ("s3", "s1", "k2", "d", "wk", "wv", "p", "x", "q2", "a31", "b3", "b1", "a2", "b2", "a0")
 NAMES = {"s": "qkv", "k": "kv", "q": "q"}
 
 
@@ -360,15 +360,21 @@
         return lax.ppermute(array, "frames", [(i, i ^ mask) for i in range(frames)])
 
     sends = [step for step in PLAN if step[0] in NAMES]
-    parts = [(int(step[1:]), NAMES[step[0]]) for step in sends] + [(0, "qkv")]
-    packed = dict(zip(sends + ["own"], pack(temporal_ids, query, key_proj, value, parts, heads_here)))
+    early = [step for step in sends if step[0] != "q"]
+    rest = [step for step in sends if step[0] == "q"] + ["own"]
+
+    def packed_for(steps, *operands):
+        parts = [(0, "qkv") if step == "own" else (int(step[1:]), NAMES[step[0]]) for step in steps]
+        return dict(zip(steps, pack(temporal_ids, *operands, parts, heads_here)))
+
+    packed = packed_for(early, query, key_proj, value)
     keys_sent, values_sent, *_ = lax.optimization_barrier((key_proj, value, *packed.values()))
     swapped = {"wk": keys_sent, "wv": values_sent}
     late = int([step for step in PLAN if step[0] == "b"][-1][1:])
     slot = jnp.arange(frames, dtype=jnp.int32) == lax.axis_index("frames") ^ late
     head = jnp.sum(jnp.where(slot, lax.rem(temporal_ids, heads_here), 0))
     heads, head = lax.optimization_barrier((spatial_heads(temporal_ids, heads_here), head))
-    queries, groups, keys_at, attended, returned = {0: packed["own"]}, [packed["own"]], [HD], {}, {}
+    queries, groups, keys_at, attended, returned = {}, [], [], {}, {}
     for step in PLAN:
         kind, masks = step[0], [int(digit) for digit in step[1:] if digit.isdigit()]
         if kind in NAMES:
@@ -382,6 +388,12 @@
             swapped[step] = lax.ppermute(swapped[step], "rep", [(0, 1), (1, 0)])
         elif kind == "x":
             out = spatial(heads, block_mask, query, key_proj, swapped["wk"], value, swapped["wv"])
+        elif kind == "p":
+            late_query, *_ = lax.optimization_barrier((query, *packed.values()))
+            packed.update(packed_for(rest, late_query, key_proj, value))
+            queries[0] = packed["own"]
+            groups.append(packed["own"])
+            keys_at.append(HD)
         elif kind == "d":
             bias = tile_bias(tile_sizes, query.shape[0])
         elif kind == "a":

time: 37.2 us -> 37.8 us (1.016)
  waiting for transfers between devices: 9.82 us -> 7.63 us
  Pallas kernels: 10.5 us -> 12 us
  local copies, waits for them, and re-layouts: 1.42 us -> 2.58 us
    ppermute x7, waiting for transfers between devices: 9.82 us -> 7.63 us  [exchange(): return lax.ppermute(array, 'frames', [(i, i ^ mask) for i in range(frames)])]
    pallas_call x1 -> x2, Pallas kernels: 1.97 us -> 3.48 us  [pack(): pl.pallas_call(lambda *refs: pack_kernel(heads_here, parts, *refs), out_s...]
    unnamed x7 -> x9, local copies, waits for them, and re-layouts: 0.78 us -> 1.94 us
  transfers between devices with their start and end apart: 9 -> 9, of which waited for: 2 -> 2; matrix products, arithmetic and copies ran while one was open for 3% -> 3% of each run, Pallas kernels for 23% -> 27%
where the time goes in v8:
time: 37.8 us; the launch traced here: 37.5 us
  starting transfers between devices  13.4 us (35%)
  Pallas kernels  12 us (32%)
  waiting for transfers between devices  7.63 us (20%)
  local copies, waits for them, and re-layouts  2.58 us (7%)
  other arithmetic  0.96 us (3%)
  between operations  0.8 us (2%)
    ppermute x7, starting transfers between devices, exchange(): return lax.ppermute(array, 'frames', [(i, i ^ mask) for i in range(frames)])  12.8 us
    ppermute x7, waiting for transfers between devices, exchange(): return lax.ppermute(array, 'frames', [(i, i ^ mask) for i in range(frames)])  7.63 us
    pallas_call x1, Pallas kernels, spatial(): pl.pallas_call(spatial_kernel, out_shape=jax.ShapeDtypeStruct((rows, widt...  4.69 us
    pallas_call x2, Pallas kernels, pack(): pl.pallas_call(lambda *refs: pack_kernel(heads_here, parts, *refs), out_s...  3.48 us
    pallas_call x3, Pallas kernels, temporal(): pl.pallas_call(lambda *refs: temporal_kernel(keys_at, len(queries), *refs...  2.42 us
    unnamed x9, local copies, waits for them, and re-layouts  1.94 us
    pallas_call x1, Pallas kernels, merge(): pl.pallas_call(lambda *refs: merge_kernel(width // HD, masks, *refs), out...  0.83 us
  transfers between devices with their start and end apart: 9, of which 2 were waited for; matrix products, arithmetic and copies ran while one was open for 3% of the time, Pallas kernels for 27%

profile of v8, /device:TPU:0, one launch (start us, length us, event | category | flops | bytes accessed | tf_op | source)
XLA Modules:
  0.0 37.5 jit_solution(11121976909315677025)
XLA Ops:
  0.0 1.8 %pack.2 = (bf16[256,384]{1,0:T(8,128)(2,1)S(1)}, bf16[256,384]{1,0:T(8,128)(2,1)S(1)}, bf16[256,256]{1,0:T(8,128)(2,1)S(1)}) custom-call(s32[4]{0:T(128)} %refs_0_.3, bf16[256,1536]{1,0:T(8,128)(2,1)} %refs_1_.2, bf16[256,1536]{1,0:T(8,128)(2,1)} %refs_2_.3, bf16[256,1536]{1,0:T(8,128)(2,1)} %refs_3_.3), custom_call_target="tpu_custom_call" | custom-call | bytes 1048576 | tf_op jit(solution)/shard_map/pack/pallas_call | solution.py:187
  1.8 0.6 %collective-permute-start = (bf16[256,1536]{1,0:T(8,128)(2,1)}, bf16[256,1536]{1,0:T(8,128)(2,1)S(1)}, u32[]{:S(2)}, u32[]{:S(2)}) collective-permute-start(bf16[256,1536]{1,0:T(8,128)(2,1)} %refs_2_.3), channel_id=1, source_target_pairs={{0,1},{1,0},{2,3},{3,2},{4,5},{5,4},{6,7},{7,6},{8,9},{9,8},{10,11... | collective-permute-start | bytes 2359304 | tf_op jit(solution)/shard_map/ppermute | solution.py:388
  2.4 0.1 collective-permute-start.1
  2.5 4.0 %collective-permute-start.4 = (bf16[256,256]{1,0:T(8,128)(2,1)S(1)}, bf16[256,256]{1,0:T(8,128)(2,1)S(1)}, u32[]{:S(2)}, u32[]{:S(2)}) collective-permute-start(bf16[256,256]{1,0:T(8,128)(2,1)S(1)} %get-tuple-element.20), channel_id=1, source_target_pairs={{0,8},{4,12},{8,0},{12,4},{1,9},{5,13},{9,1},{13,5},{2,10},{6,14},... | collective-permute-start | bytes 393224 | tf_op jit(solution)/shard_map/ppermute | solution.py:360
  6.5 1.3 %collective-permute-start.2 = (bf16[256,384]{1,0:T(8,128)(2,1)S(1)}, bf16[256,384]{1,0:T(8,128)(2,1)S(1)}, u32[]{:S(2)}, u32[]{:S(2)}) collective-permute-start(bf16[256,384]{1,0:T(8,128)(2,1)S(1)} %get-tuple-element.18), channel_id=1, source_target_pairs={{0,12},{4,8},{8,4},{12,0},{1,13},{5,9},{9,5},{13,1},{2,14},{6,10},... | collective-permute-start | bytes 589832 | tf_op jit(solution)/shard_map/ppermute | solution.py:360
  7.8 0.2 collective-permute-start.3
  8.1 0.7 %copy-done = s32[4]{0:T(128)S(1)} copy-done((s32[4]{0:T(128)S(1)}, s32[4]{0:T(128)}, u32[]{:S(2)}) %copy-start) | copy-done | bytes 40
  8.7 0.6 %fusion.3 = (s32[]{:T(128)}, s32[4]{0:T(128)S(1)}) fusion(s32[]{:T(128)S(6)} %xor.3, s32[4]{0:T(128)S(1)} %copy-done), kind=kLoop, calls=%fused_computation.9 | loop fusion | flops 15 | bytes 40 | tf_op jit(solution)/shard_map/reduce_sum | solution.py:375
  9.3 1.7 %pack.3 = (bf16[256,128]{1,0:T(8,128)(2,1)S(1)}, bf16[256,384]{1,0:T(8,128)(2,1)S(1)}) custom-call(s32[4]{0:T(128)} %refs_0_.3, bf16[256,1536]{1,0:T(8,128)(2,1)} %refs_1_.2, bf16[256,1536]{1,0:T(8,128)(2,1)} %refs_2_.3, bf16[256,1536]{1,0:T(8,128)(2,1)} %refs_3_.3), custom_call_target="tpu_custom_call" | custom-call | bytes 524288 | tf_op jit(solution)/shard_map/pack/pallas_call | solution.py:187
  11.0 0.1 fusion.2
  11.1 6.8 %collective-permute-done.4.refs_4_.refs_5_ = bf16[256,256]{1,0:T(8,128)(2,1)S(1)} collective-permute-done((bf16[256,256]{1,0:T(8,128)(2,1)S(1)}, bf16[256,256]{1,0:T(8,128)(2,1)S(1)}, u32[]{:S(2)}, u32[]{:S(2)}) %collective-permute-start.4) | collective-permute-done | bytes 131104 | tf_op jit(solution)/shard_map/ppermute | solution.py:360
  17.9 0.0 collective-permute-start.7
  17.9 0.1 convert_reduce_fusion
  18.0 0.5 %copy-done.2 = s32[1,4]{1,0:T(1,128)S(1)} copy-done((s32[1,4]{1,0:T(1,128)S(1)}, s32[1,4]{1,0:T(1,128)}, u32[]{:S(2)}) %copy-start.2) | copy-done | bytes 40
  18.6 0.6 %tile_bias.1.refs_0_ = f32[256,256]{1,0:T(8,128)S(1)} custom-call(s32[1,4]{1,0:T(1,128)S(1)} %copy-done.2), custom_call_target="tpu_custom_call" | custom-call | flops 65536 | bytes 262144 | tf_op jit(solution)/shard_map/tile_bias/pallas_call | solution.py:284
  19.2 0.0 collective-permute-done.2.refs_2_.refs_1_.refs_3_
  19.2 0.8 %collective-permute-done.3.refs_3_.refs_2_.refs_4_ = bf16[256,384]{1,0:T(8,128)(2,1)S(1)} collective-permute-done((bf16[256,384]{1,0:T(8,128)(2,1)S(1)}, bf16[256,384]{1,0:T(8,128)(2,1)S(1)}, u32[]{:S(2)}, u32[]{:S(2)}) %collective-permute-start.3) | collective-permute-done | bytes 196640 | tf_op jit(solution)/shard_map/ppermute | solution.py:360
  20.0 1.1 %temporal.4 = (bf16[256,128]{1,0:T(8,128)(2,1)S(1)}, bf16[256,128]{1,0:T(8,128)(2,1)S(1)}) custom-call(f32[256,256]{1,0:T(8,128)S(1)} %tile_bias.1.refs_0_, bf16[256,384]{1,0:T(8,128)(2,1)S(1)} %collective-permute-done.2.refs_2_.refs_1_.refs_3_, bf16[256,384]{1,0:T(8,128)(2,1)S(1)} %collective-permute-done.3.refs_3_.refs_2_.refs_4_, ...), custom_call_target="tpu_custom_call" | custom-call | flops 268435456 | bytes 786432 | tf_op jit(solution)/shard_map/temporal/pallas_call | solution.py:309
  21.1 4.1 %collective-permute-start.5 = (bf16[256,128]{1,0:T(8,128)(2,1)S(1)}, bf16[256,128]{1,0:T(8,128)(2,1)S(1)}, u32[]{:S(2)}, u32[]{:S(2)}) collective-permute-start(bf16[256,128]{1,0:T(8,128)(2,1)S(1)} %get-tuple-element.25), channel_id=1, source_target_pairs={{0,4},{4,0},{8,12},{12,8},{1,5},{5,1},{9,13},{13,9},{2,6},{6,2},{1... | collective-permute-start | bytes 196616 | tf_op jit(solution)/shard_map/ppermute | solution.py:360
  25.3 3.0 %collective-permute-start.6 = (bf16[256,128]{1,0:T(8,128)(2,1)S(1)}, bf16[256,128]{1,0:T(8,128)(2,1)S(1)}, u32[]{:S(2)}, u32[]{:S(2)}) collective-permute-start(bf16[256,128]{1,0:T(8,128)(2,1)S(1)} %get-tuple-element.26), channel_id=1, source_target_pairs={{0,12},{4,8},{8,4},{12,0},{1,13},{5,9},{9,5},{13,1},{2,14},{6,10},... | collective-permute-start | bytes 196616 | tf_op jit(solution)/shard_map/ppermute | solution.py:360
  28.3 0.0 collective-permute-done.7.refs_1_
  28.3 0.6 %temporal.5 = bf16[256,128]{1,0:T(8,128)(2,1)S(1)} custom-call(f32[256,256]{1,0:T(8,128)S(1)} %tile_bias.1.refs_0_, bf16[256,128]{1,0:T(8,128)(2,1)S(1)} %collective-permute-done.7.refs_1_, bf16[256,384]{1,0:T(8,128)(2,1)S(1)} %collective-permute-done.2.refs_2_.refs_1_.refs_3_, bf16[256,384]{1,0:T(8,128)(2,1)S(1)} %collective-permute-done.3.refs_3_.refs_2_.refs_4_, ...), custom_call_target="tpu_custom_call" | custom-call | flops 134217728 | bytes 655360 | tf_op jit(solution)/shard_map/temporal/pallas_call | solution.py:309
  28.9 0.1 collective-permute-start.8
  29.0 0.1 select_reduce_fusion.heads_ref
  29.8 0.1 copy.9.mask_ref
  29.9 0.7 %temporal.3.refs_2_ = bf16[256,128]{1,0:T(8,128)(2,1)S(1)} custom-call(f32[256,256]{1,0:T(8,128)S(1)} %tile_bias.1.refs_0_, bf16[256,384]{1,0:T(8,128)(2,1)S(1)} %get-tuple-element.24.refs_1_.refs_5_.refs_6_, bf16[256,384]{1,0:T(8,128)(2,1)S(1)} %collective-permute-done.2.refs_2_.refs_1_.refs_3_, ...), custom_call_target="tpu_custom_call" | custom-call | flops 134217728 | bytes 655360 | tf_op jit(solution)/shard_map/temporal/pallas_call | solution.py:309
  30.6 0.0 collective-permute-done.key_other
  30.6 4.7 %spatial.1.refs_1_ = bf16[256,1536]{1,0:T(8,128)(2,1)} custom-call(s32[8]{0:T(128)S(1)} %select_reduce_fusion.heads_ref, s32[12,8,8]{2,1,0:T(8,128)S(1)} %copy.9.mask_ref, bf16[256,1536]{1,0:T(8,128)(2,1)} %refs_1_.2, bf16[256,1536]{1,0:T(8,128)(2,1)} %refs_2_.3, bf16[256,1536]{1,0:T(8,128)(2,1)S(1)} %collective-permute-done.key_other, ...), custom_call_target="tpu_custom_call" | custom-call | flops 536870912 | bytes 3145728 | tf_op jit(solution)/shard_map/spatial/pallas_call | solution.py:242
  35.3 0.0 copy-start.1
  35.3 0.6 %copy-done.1 = s32[4]{0:T(128)S(1)} copy-done((s32[4]{0:T(128)S(1)}, s32[4]{0:T(128)}, u32[]{:S(2)}) %copy-start.1) | copy-done | bytes 40
  36.0 0.8 %merge.1 = bf16[256,1536]{1,0:T(8,128)(2,1)} custom-call(s32[1,4]{1,0:T(1,128)S(1)} %bitcast.1, bf16[256,1536]{1,0:T(8,128)(2,1)} %spatial.1.refs_1_, bf16[256,128]{1,0:T(8,128)(2,1)S(1)} %temporal.3.refs_2_, bf16[256,128]{1,0:T(8,128)(2,1)S(1)} %collective-permute-done.5.refs_3_, ...), custom_call_target="tpu_custom_call", output_to_operand_aliasing={{}: (1, {})} | custom-call | bytes 393216 | tf_op jit(solution)/shard_map/merge/pallas_call | solution.py:338
  36.8 0.6 %constant_dynamic-update-slice_fusion = bf16[256,1536]{1,0:T(8,128)(2,1)} fusion(bf16[256,1536]{1,0:T(8,128)(2,1)} %merge.1, bf16[256,128]{1,0:T(8,128)(2,1)S(1)} %collective-permute-done.8, s32[]{:T(128)S(6)} %select_n.13), kind=kLoop, calls=%fused_computation.10 | loop fusion | bytes 131076 | tf_op jit(solution)/shard_map/dynamic_update_slice | solution.py:406
  (8 shorter events, 0.0 us)
Async XLA Ops:
  1.8 28.8 %collective-permute-start = (bf16[256,1536]{1,0:T(8,128)(2,1)}, bf16[256,1536]{1,0:T(8,128)(2,1)S(1)}, u32[]{:S(2)}, u32[]{:S(2)}) collective-permute-start(bf16[256,1536]{1,0:T(8,128)(2,1)} %refs_2_.3), channel_id=1, source_target_pairs={{0,1},{1,0},{2,3},{3,2},{4,5},{5,4},{6,7},{7,6},{8,9},{9,8},{10,11... | collective-permute-start | bytes 2359304 | tf_op jit(solution)/shard_map/ppermute | solution.py:388
  2.4 28.2 %collective-permute-start.1 = (bf16[256,1536]{1,0:T(8,128)(2,1)}, bf16[256,1536]{1,0:T(8,128)(2,1)S(1)}, u32[]{:S(2)}, u32[]{:S(2)}) collective-permute-start(bf16[256,1536]{1,0:T(8,128)(2,1)} %refs_3_.3), channel_id=1, source_target_pairs={{0,1},{1,0},{2,3},{3,2},{4,5},{5,4},{6,7},{7,6},{8,9},{9,8},{10,11... | collective-permute-start | bytes 2359304 | tf_op jit(solution)/shard_map/ppermute | solution.py:388
  2.5 15.4 %collective-permute-start.4 = (bf16[256,256]{1,0:T(8,128)(2,1)S(1)}, bf16[256,256]{1,0:T(8,128)(2,1)S(1)}, u32[]{:S(2)}, u32[]{:S(2)}) collective-permute-start(bf16[256,256]{1,0:T(8,128)(2,1)S(1)} %get-tuple-element.20), channel_id=1, source_target_pairs={{0,8},{4,12},{8,0},{12,4},{1,9},{5,13},{9,1},{13,5},{2,10},{6,14},... | collective-permute-start | bytes 393224 | tf_op jit(solution)/shard_map/ppermute | solution.py:360
  6.5 12.7 %collective-permute-start.2 = (bf16[256,384]{1,0:T(8,128)(2,1)S(1)}, bf16[256,384]{1,0:T(8,128)(2,1)S(1)}, u32[]{:S(2)}, u32[]{:S(2)}) collective-permute-start(bf16[256,384]{1,0:T(8,128)(2,1)S(1)} %get-tuple-element.18), channel_id=1, source_target_pairs={{0,12},{4,8},{8,4},{12,0},{1,13},{5,9},{9,5},{13,1},{2,14},{6,10},... | collective-permute-start | bytes 589832 | tf_op jit(solution)/shard_map/ppermute | solution.py:360
  7.8 12.2 %collective-permute-start.3 = (bf16[256,384]{1,0:T(8,128)(2,1)S(1)}, bf16[256,384]{1,0:T(8,128)(2,1)S(1)}, u32[]{:S(2)}, u32[]{:S(2)}) collective-permute-start(bf16[256,384]{1,0:T(8,128)(2,1)S(1)} %get-tuple-element.19), channel_id=1, source_target_pairs={{0,4},{4,0},{8,12},{12,8},{1,5},{5,1},{9,13},{13,9},{2,6},{6,2},{1... | collective-permute-start | bytes 589832 | tf_op jit(solution)/shard_map/ppermute | solution.py:360
  8.1 0.7 %copy-start = (s32[4]{0:T(128)S(1)}, s32[4]{0:T(128)}, u32[]{:S(2)}) copy-start(s32[4]{0:T(128)} %refs_0_.3) | copy-start | bytes 52
  17.9 0.7 %copy-start.2 = (s32[1,4]{1,0:T(1,128)S(1)}, s32[1,4]{1,0:T(1,128)}, u32[]{:S(2)}) copy-start(s32[1,4]{1,0:T(1,128)} %sizes_ref.1) | copy-start | bytes 52
  17.9 10.4 %collective-permute-start.7 = (bf16[256,128]{1,0:T(8,128)(2,1)S(1)}, bf16[256,128]{1,0:T(8,128)(2,1)S(1)}, u32[]{:S(2)}, u32[]{:S(2)}) collective-permute-start(bf16[256,128]{1,0:T(8,128)(2,1)S(1)} %get-tuple-element.27), channel_id=1, source_target_pairs={{0,8},{4,12},{8,0},{12,4},{1,9},{5,13},{9,1},{13,5},{2,10},{6,14},... | collective-permute-start | bytes 196616 | tf_op jit(solution)/shard_map/ppermute | solution.py:360
  21.1 14.2 %collective-permute-start.5 = (bf16[256,128]{1,0:T(8,128)(2,1)S(1)}, bf16[256,128]{1,0:T(8,128)(2,1)S(1)}, u32[]{:S(2)}, u32[]{:S(2)}) collective-permute-start(bf16[256,128]{1,0:T(8,128)(2,1)S(1)} %get-tuple-element.25), channel_id=1, source_target_pairs={{0,4},{4,0},{8,12},{12,8},{1,5},{5,1},{9,13},{13,9},{2,6},{6,2},{1... | collective-permute-start | bytes 196616 | tf_op jit(solution)/shard_map/ppermute | solution.py:360
  25.3 4.5 %copy-start.3 = (s32[12,8,8]{0,2,1:T(8,128)S(1)}, s32[12,8,8]{0,2,1:T(8,128)}, u32[]{:S(2)}) copy-start(s32[12,8,8]{0,2,1:T(8,128)} %param.9) | copy-start | bytes 9220
  25.3 10.1 %collective-permute-start.6 = (bf16[256,128]{1,0:T(8,128)(2,1)S(1)}, bf16[256,128]{1,0:T(8,128)(2,1)S(1)}, u32[]{:S(2)}, u32[]{:S(2)}) collective-permute-start(bf16[256,128]{1,0:T(8,128)(2,1)S(1)} %get-tuple-element.26), channel_id=1, source_target_pairs={{0,12},{4,8},{8,4},{12,0},{1,13},{5,9},{9,5},{13,1},{2,14},{6,10},... | collective-permute-start | bytes 196616 | tf_op jit(solution)/shard_map/ppermute | solution.py:360
  28.9 7.9 %collective-permute-start.8 = (bf16[256,128]{1,0:T(8,128)(2,1)S(1)}, bf16[256,128]{1,0:T(8,128)(2,1)S(1)}, u32[]{:S(2)}, u32[]{:S(2)}) collective-permute-start(bf16[256,128]{1,0:T(8,128)(2,1)S(1)} %temporal.5), channel_id=1, source_target_pairs={{0,8},{4,12},{8,0},{12,4},{1,9},{5,13},{9,1},{13,5},{2,10},{6,14},... | collective-permute-start | bytes 196616 | tf_op jit(solution)/shard_map/ppermute | solution.py:360
  35.3 0.7 %copy-start.1 = (s32[4]{0:T(128)S(1)}, s32[4]{0:T(128)}, u32[]{:S(2)}) copy-start(s32[4]{0:T(128)} %refs_0_.3) | copy-start | bytes 52
